TPU v7x, 32 devices: a whole 2x2x4 slice. The times are simulated.
32 devices in a mesh: grp: 2 (over x), seq: 16 (over z, y, core).
Axes of the slice: x: 2, y: 2, z: 4, core: 2. Of those that a mesh axis runs over, the one named last changes fastest.
Arguments:
- hidden_in: bfloat16 [8192, 768], P(('grp', 'seq')), parts along dimension 0, may hold values from -6 to 6
- w_in: bfloat16 [768, 1024], replicated, may hold values from -0.21875 to 0.21875
- w_dt: bfloat16 [768, 12], replicated, may hold values from -0.21875 to 0.21875
- dt_bias: float32 [12], replicated, may hold values from -7 to -2
- a_log: float32 [12], replicated, may hold values from -4 to 3
- conv_w: float32 [4, 1024], replicated, may hold values from -3 to 3
- d_skip: float32 [12], replicated, may hold values from 0.5 to 1.5
- norm_gain: float32 [768], replicated, may hold values from 0.5 to 1.5
- w_out: bfloat16 [768, 768], replicated, may hold values from -0.21875 to 0.21875
- w_cls: bfloat16 [768, 16], replicated, may hold values from -0.21875 to 0.21875
- teacher_rows: bfloat16 [4096, 4096], P(('grp', 'seq')), parts along dimension 0, may hold values from -1800 to 1800
- w_teacher: bfloat16 [4096, 16], replicated, may hold values from -0.09375 to 0.09375
- row_dest: int32 [4096, 1], P(('grp', 'seq')), parts along dimension 0, may hold values from 0 to 15; in each aligned block of 128 rows (0 to 127, 128 to 255, ...) at most 16 rows name the same one
- row_start: int32 [4096], P(('grp', 'seq')), parts along dimension 0, may hold values from 0 to 224
- row_len: int32 [4096], P(('grp', 'seq')), parts along dimension 0, may hold values from 1 to 32
Outputs:
- grad_hidden: bfloat16 [8192, 768], P(('grp', 'seq')), parts along dimension 0
- grad_w_in: float32 [1536, 1024], P(('grp', 'seq')), parts along dimension 0
- grad_w_out: float32 [1536, 768], P(('grp', 'seq')), parts along dimension 0
- grad_conv: float32 [8, 1024], P('grp'), parts along dimension 0
- grad_w_dt: float32 [1536, 12], P('grp'), parts along dimension 0
- grad_heads: float32 [6, 12], P('grp'), parts along dimension 0
- grad_norm_gain: float32 [1536], P('grp'), parts along dimension 0
- grad_w_cls: float32 [1536, 16], P('grp'), parts along dimension 0
- loss: float32 [2], P('grp'), parts along dimension 0
There are 2 independent parts, one for each index of `grp`. A program takes and returns all parts, laid end to end along the dimension named above; an argument that names none is the same for every part. Nothing has to cross between parts.
Inputs may be any that keep to these rules, and one draw needn't show every extreme that they name: `row_dest`: within the rows of one device (aligned blocks of 128 rows), no destination is named by more than 16 rows, a bound that some block reaches.
All inputs are finite; a program needn't handle non-finite values.
Results may differ from a plain program's by a relative error of at most 0.014.
Values may be sent and summed in bfloat16 or wider, within the bound.
No kernel may reach another device: no remote copies, remote signals or barrier semaphores. Data moves between devices by JAX's collectives and lax.ppermute only.
A program may use at most 128 MiB of HBM per device.

v0:
```python
import jax
import jax.numpy as jnp
from jax import lax
from jax.sharding import PartitionSpec as P

HEADS = 12
HDIM = 64
STATE = 128
LABELS = 16
BLOCK = 64


PRECISE = lax.Precision.HIGHEST
EPSILON = 1e-05
CONTRACT_ROWS = (((0,), (0,)), ((), ()))


def partner(x, axis, apart):
    return lax.ppermute(x, axis, [(i, i ^ 1 << apart) for i in range(lax.axis_size(axis))])


def passed_along(x, axis, by):
    length = lax.axis_size(axis)
    pairs = [(i, i + by) for i in range(length) if 0 <= i + by < length]
    return lax.ppermute(x, axis, pairs)


def prefix(part, axis, combine, identity, reverse):
    count = lax.axis_size(axis)
    place = lax.axis_index(axis)
    ahead = count - 1 - place if reverse else place
    gathered = jax.tree.map(lambda a: lax.all_gather(a, axis), part)
    state = jax.tree.map(lambda a, e: jnp.zeros_like(a) + jnp.asarray(e, a.dtype), part, identity)

    def one(turn, state):
        source = count - 1 - turn if reverse else turn
        return combine(
            state, jax.tree.map(lambda a: lax.dynamic_index_in_dim(a, source, 0, False), gathered)
        )

    return lax.fori_loop(0, ahead, one, state)


def carried_in(x, axis, combine, identity, reverse):
    length, place = (lax.axis_size(axis), lax.axis_index(axis))
    everything = jax.tree.map(
        lambda part, kind: lax.all_gather(part.astype(kind), axis),
        x,
        jax.tree.map(lambda a: jnp.bfloat16 if a.dtype == jnp.float32 else a.dtype, x),
    )
    start = jax.tree.map(
        lambda part, zero: jnp.broadcast_to(jnp.asarray(zero, part.dtype), part.shape), x, identity
    )

    def turn(k, before):
        at = length - 1 - k if reverse else k
        reached = at > place if reverse else at < place
        new = combine(
            before, jax.tree.map(lambda part, own: part[at].astype(own.dtype), everything, x)
        )
        return jax.tree.map(lambda a, b: jnp.where(reached, a, b), new, before)

    return lax.fori_loop(0, length, turn, start)


def block_step(carry_state, pieces):
    values, in_map, out_map, step_size, log_decay = pieces
    running = jnp.cumsum(log_decay, axis=0)
    block_width = log_decay.shape[0]
    causal = jnp.arange(block_width)[:, None] >= jnp.arange(block_width)[None, :]
    spread = running.T[:, :, None] - running.T[:, None, :]
    decay_mix = jnp.exp(jnp.where(causal[None, :, :], spread, -jnp.inf))
    scores = jnp.dot(out_map, in_map.T, precision=PRECISE)
    weighted = values * step_size[:, :, None]
    within = jnp.einsum("hts,shp->thp", decay_mix * scores[None, :, :], weighted, precision=PRECISE)
    carried = (
        jnp.einsum("tn,hnp->thp", out_map, carry_state, precision=PRECISE)
        * jnp.exp(running)[:, :, None]
    )
    tail_decay = jnp.exp(running[-1][None, :] - running)
    fresh_state = jnp.einsum(
        "sn,shp->hnp", in_map, weighted * tail_decay[:, :, None], precision=PRECISE
    )
    carry_state = carry_state * jnp.exp(running[-1])[:, None, None] + fresh_state
    return (carry_state, within + carried)


def unpack(mixed_f, raw_step, dt_bias, a_log):
    inner_width = HEADS * HDIM
    values = mixed_f[:, :inner_width].reshape(mixed_f.shape[0], HEADS, HDIM)
    in_map = mixed_f[:, inner_width : inner_width + STATE]
    out_map = mixed_f[:, inner_width + STATE :]
    step_size = jax.nn.softplus(raw_step + dt_bias)
    log_decay = -step_size * jnp.exp(a_log)
    return (values, in_map, out_map, step_size, log_decay)


def full_branch(mixed_f, raw_step, dt_bias, a_log, d_skip, norm_gain, start_state):
    values, in_map, out_map, step_size, log_decay = unpack(mixed_f, raw_step, dt_bias, a_log)
    block_count = values.shape[0] // BLOCK
    pieces = tuple(
        (
            piece.reshape((block_count, BLOCK) + piece.shape[1:])
            for piece in (values, in_map, out_map, step_size, log_decay)
        )
    )
    _, outputs = lax.scan(block_step, start_state, pieces)
    scanned = outputs.reshape(values.shape) + d_skip[None, :, None] * values
    flat = scanned.reshape(values.shape[0], HEADS * HDIM)
    mean_square = jnp.mean(flat * flat, axis=1, keepdims=True)
    return flat * lax.rsqrt(mean_square + EPSILON) * norm_gain


def end_state(mixed_f, raw_step, dt_bias, a_log):
    values, in_map, out_map, step_size, log_decay = unpack(mixed_f, raw_step, dt_bias, a_log)
    running = jnp.cumsum(log_decay, axis=0)
    total_log = running[-1]
    weighted = values * (step_size * jnp.exp(total_log[None, :] - running))[:, :, None]
    return (jnp.einsum("sn,shp->hnp", in_map, weighted, precision=PRECISE), total_log)


def compose(earlier, later):
    return (earlier[0] * later[0], later[0][:, None, None] * earlier[1] + later[1])


def per_device(
    hidden_in,
    w_in,
    w_dt,
    dt_bias,
    a_log,
    conv_w,
    d_skip,
    norm_gain,
    w_out,
    w_cls,
    teacher_rows,
    w_teacher,
    row_dest,
    row_start,
    row_len,
):
    devices = lax.axis_size("seq")
    bit_count = devices.bit_length() - 1
    ahead = 1
    taps = conv_w.shape[0]
    local_rows = hidden_in
    for which_bit in range(bit_count):
        local_rows = partner(local_rows, "seq", which_bit)
    flipped = local_rows[::-1]
    length = flipped.shape[0]
    row_count = teacher_rows.shape[0]
    slot_cap = max(2, 2 * row_count // devices)
    target_dev = row_dest[:, 0]
    target_dev = devices - 1 - target_dev
    one_hot = (target_dev[:, None] == jnp.arange(devices, dtype=jnp.int32)[None, :]).astype(
        jnp.int32
    )
    before = jnp.cumsum(one_hot, axis=0) - one_hot
    slot_index = jnp.sum(before * one_hot, axis=1)
    position = target_dev * slot_cap + slot_index
    selector = position[None, :] == jnp.arange(devices * slot_cap, dtype=jnp.int32)[:, None]
    span_meta = jnp.stack([row_start // 16, row_start % 16, row_len], axis=1).astype(jnp.float32)
    selector_f = selector.astype(jnp.float32)
    own_logp = jax.nn.log_softmax(
        jnp.dot(teacher_rows, w_teacher, preferred_element_type=jnp.float32), axis=-1
    )
    packed = jnp.dot(selector_f, own_logp, precision=PRECISE).reshape(devices, slot_cap, LABELS)
    span_tags = jnp.dot(selector_f, span_meta, precision=PRECISE).reshape(devices, slot_cap, 3)
    teacher_logp, span_tags = (
        lax.all_to_all(packed, "seq", split_axis=0, concat_axis=0, tiled=True),
        lax.all_to_all(span_tags, "seq", split_axis=0, concat_axis=0, tiled=True),
    )
    teacher_logp = teacher_logp.reshape(devices * slot_cap, LABELS)
    span_tags = span_tags.reshape(devices * slot_cap, 3)
    span_start = span_tags[:, 0] * 16.0 + span_tags[:, 1]
    span_length = span_tags[:, 2]
    span_low = length - span_start - span_length
    span_high = length - span_start
    positions = jnp.arange(length, dtype=jnp.float32)
    covered = (
        (positions[None, :] >= span_low[:, None]) & (positions[None, :] < span_high[:, None])
    ).astype(jnp.float32)
    teacher_prob = jnp.exp(teacher_logp)
    target = lax.dot_general(covered, teacher_prob, CONTRACT_ROWS, precision=PRECISE)
    cover_count = jnp.sum(covered, axis=0)
    own_term = jnp.sum(span_length * jnp.sum(teacher_prob * teacher_logp, axis=1))
    raw = jnp.dot(flipped, w_in, preferred_element_type=jnp.float32).astype(jnp.bfloat16)
    raw_step = jnp.dot(flipped, w_dt, preferred_element_type=jnp.float32)
    rim_rows = passed_along(raw[length - (taps - 1) :], "seq", ahead)
    padded = jnp.concatenate([rim_rows, raw], axis=0)
    conv_sum = jnp.zeros(raw.shape, jnp.float32)
    for tap_index in range(taps):
        conv_sum = (
            conv_sum
            + conv_w[tap_index] * padded[taps - 1 - tap_index : taps - 1 - tap_index + length]
        )
    mixed_f = jax.nn.silu(conv_sum).astype(jnp.bfloat16).astype(jnp.float32)
    (own_state, own_log), pull_end = jax.vjp(end_state, mixed_f, raw_step, dt_bias, a_log)
    decay_all = jnp.exp(own_log)
    identity = (jnp.ones_like(decay_all), jnp.zeros_like(own_state))
    _, state_in = prefix((decay_all, own_state), "seq", compose, identity, ahead < 0)
    normed_f, pull_full = jax.vjp(
        full_branch, mixed_f, raw_step, dt_bias, a_log, d_skip, norm_gain, state_in
    )
    normed = normed_f.astype(jnp.bfloat16)
    branch = jnp.dot(normed, w_out, preferred_element_type=jnp.float32).astype(jnp.bfloat16)
    student_logp = jax.nn.log_softmax(
        jnp.dot(branch, w_cls, preferred_element_type=jnp.float32), axis=-1
    )
    part_loss = own_term - jnp.sum(target * student_logp)
    back_logits = cover_count[:, None] * jnp.exp(student_logp) - target
    grad_cls_local = lax.dot_general(
        branch.astype(jnp.float32), back_logits, CONTRACT_ROWS, precision=PRECISE
    )
    back_branch = jnp.dot(back_logits, w_cls.astype(jnp.float32).T, precision=PRECISE).astype(
        jnp.bfloat16
    )
    back_normed = jnp.dot(back_branch, w_out.T, preferred_element_type=jnp.float32)
    back_mixed, back_step, back_bias, back_alog, back_skip, back_gain, back_state = pull_full(
        back_normed
    )
    _, state_grad = carried_in((decay_all, back_state), "seq", compose, identity, ahead > 0)
    back_total_log = decay_all * jnp.sum(state_grad * state_in, axis=(1, 2))
    end_mixed, end_step, end_bias, end_alog = pull_end((state_grad, back_total_log))
    back_mixed = back_mixed + end_mixed
    sigmoid_part = jax.nn.sigmoid(conv_sum)
    back_conv = back_mixed * sigmoid_part * (1.0 + conv_sum * (1.0 - sigmoid_part))
    rim_back = passed_along(back_conv[: taps - 1], "seq", -ahead)
    extended = jnp.concatenate([back_conv, rim_back], axis=0)
    back_raw_f = jnp.zeros(back_conv.shape, jnp.float32)
    conv_rows = []
    for tap_index in range(taps):
        back_raw_f = back_raw_f + conv_w[tap_index] * extended[tap_index : tap_index + length]
        conv_rows.append(
            jnp.sum(
                back_conv * padded[taps - 1 - tap_index : taps - 1 - tap_index + length], axis=0
            )
        )
    back_raw = back_raw_f.astype(jnp.bfloat16)
    back_step_b = (back_step + end_step).astype(jnp.bfloat16)
    grad_conv_local = jnp.stack(conv_rows)
    grad_dt_local = lax.dot_general(
        flipped, back_step_b, CONTRACT_ROWS, preferred_element_type=jnp.float32
    )
    grad_flip = jnp.dot(back_raw, w_in.T, preferred_element_type=jnp.float32) + jnp.dot(
        back_step_b, w_dt.T, preferred_element_type=jnp.float32
    )
    grad_local = grad_flip.astype(jnp.bfloat16)[::-1]
    for which_bit in range(bit_count):
        grad_local = partner(grad_local, "seq", which_bit)
    conv_width = w_in.shape[1]
    first_part = lax.dot_general(
        flipped, back_raw, CONTRACT_ROWS, preferred_element_type=jnp.float32
    )
    second_part = lax.dot_general(
        normed, back_branch, CONTRACT_ROWS, preferred_element_type=jnp.float32
    )
    both_grads = lax.psum_scatter(
        jnp.concatenate([first_part, second_part], axis=1), "seq", scatter_dimension=0, tiled=True
    )
    head_grads = jnp.stack([back_bias + end_bias, back_alog + end_alog, back_skip])
    totals = lax.psum(
        (
            grad_conv_local,
            grad_dt_local,
            head_grads,
            back_gain,
            grad_cls_local,
            part_loss.reshape(1),
        ),
        "seq",
    )
    loss = totals[5] / (row_count * devices)
    return (
        grad_local,
        both_grads[:, :conv_width],
        both_grads[:, conv_width:],
        totals[0],
        totals[1],
        totals[2],
        totals[3],
        totals[4],
        loss,
    )


def solution(mesh):
    placed = (
        P(("grp", "seq"), None),
        P(),
        P(),
        P(),
        P(),
        P(),
        P(),
        P(),
        P(),
        P(),
        P(("grp", "seq"), None),
        P(),
        P(("grp", "seq"), None),
        P(("grp", "seq")),
        P(("grp", "seq")),
    )
    return jax.shard_map(
        per_device,
        mesh=mesh,
        in_specs=placed,
        out_specs=(
            P(("grp", "seq"), None),
            P(("grp", "seq"), None),
            P(("grp", "seq"), None),
            P("grp", None),
            P("grp", None),
            P("grp", None),
            P("grp"),
            P("grp", None),
            P("grp"),
        ),
        check_vma=False,
    )
```

profile of v0, /device:TPU:0, one launch (start us, length us, event | category | flops | bytes accessed | tf_op | source)
XLA Modules:
  0.0 674.2 jit_solution(8998488432519138971)
XLA Ops:
  9.3 2.9 collective-permute-start.1
  12.2 9.4 %collective-permute-done.1 = bf16[256,768]{1,0:T(8,128)(2,1)S(1)} collective-permute-done((bf16[256,768]{1,0:T(8,128)(2,1)S(1)}, bf16[256,768]{1,0:T(8,128)(2,1)S(1)}, u32[]{:S(2)}, u32[]{:S(2)}) %collective-permute-start.1) | collective-permute-done | bytes 393248 | tf_op jit(solution)/shard_map/ppermute | solution.py:19
  23.4 8.8 %collective-permute-done.2 = bf16[256,768]{1,0:T(8,128)(2,1)S(1)} collective-permute-done((bf16[256,768]{1,0:T(8,128)(2,1)S(1)}, bf16[256,768]{1,0:T(8,128)(2,1)S(1)}, u32[]{:S(2)}, u32[]{:S(2)}) %collective-permute-start.2) | collective-permute-done | bytes 393248 | tf_op jit(solution)/shard_map/ppermute | solution.py:19
  36.4 15.0 %collective-permute-done.3 = bf16[256,768]{1,0:T(8,128)(2,1)S(1)} collective-permute-done((bf16[256,768]{1,0:T(8,128)(2,1)S(1)}, bf16[256,768]{1,0:T(8,128)(2,1)S(1)}, u32[]{:S(2)}, u32[]{:S(2)}) %collective-permute-start.3) | collective-permute-done | bytes 393248 | tf_op jit(solution)/shard_map/ppermute | solution.py:19
  64.8 8.3 %all-to-all-start = ((f32[16,16,3]{1,2,0:T(4,128)}), f32[16,16,3]{1,2,0:T(4,128)}, u32[]{:S(2)}, u32[]{:S(2)}) async-start(f32[16,16,3]{1,2,0:T(4,128)} %copy.266), calls=%async_computation | async-start | bytes 65536 | tf_op jit(solution)/shard_map/all_to_all | solution.py:172
  76.2 3.4 all-to-all-done
  79.7 3.5 all-to-all-start.1
  84.8 5.1 all-to-all-done.1
  95.4 18.6 %all-gather.2 = f32[16,1,12]{2,1,0:T(1,128)} all-gather(f32[1,1,12]{2,1,0:T(1,128)} %bitcast.554), channel_id=1, replica_groups=mesh['grp'=2,'seq'=16] {'seq'}, dimensions={0}, use_global_device_ids=true | all-gather | bytes 816 | tf_op jit(solution)/shard_map/all_gather | solution.py:32
  119.3 9.8 %all-gather.7.cloned.1.call-done = f32[192,128,64]{1,2,0:T(8,128)} async-done(((f32[12,128,64]{1,2,0:T(8,128)}), f32[192,128,64]{1,2,0:T(8,128)}) %all-gather.7.cloned.1.call-update) | async-done | bytes 6291472 | tf_op jit(solution)/shard_map/all_gather | solution.py:32
  133.7 79.5 %while.99 = (s32[]{:T(128)}, f32[12,128,64]{1,2,0:T(8,128)S(1)}, f32[4,64,12,64]{1,3,2,0:T(8,128)}, f32[4,12,64,64]{3,2,1,0:T(8,128)}, f32[4,128,64]{1,2,0:T(8,1...) while((s32[]{:T(128)}, f32[12,128,64]{1,2,0:T(8,128)S(1)}, ...), condition=%wide.region_9.11_spmd.clone.clone, body=%wide.region_7.10_spmd.clone.clone.sunk | while | flops 195921408 | bytes 7038781 | solution.py:107
  213.3 3.0 copy.304
  234.0 149.6 %while.100 = (s32[]{:T(128)}, f32[12,128,64]{1,2,0:T(8,128)S(1)}, f32[4,64,12,64]{1,3,2,0:T(8,128)}, f32[4,64,128]{2,1,0:T(8,128)}, f32[4,64,128]{2,1,0:T(8,128)...) while((s32[]{:T(128)}, f32[12,128,64]{1,2,0:T(8,128)S(1)}, ...), condition=%wide.region_26.28_spmd.clone, body=%wide.region_16.27_spmd.clone.sunk | while | flops 391806720 | bytes 17948952 | solution.py:107
  385.3 74.4 %all-gather.3 = bf16[16,1,12]{2,1,0:T(2,128)(2,1)S(1)} all-gather(bf16[1,1,12]{2,1,0:T(2,128)(2,1)S(1)} %bitcast.556), channel_id=1, replica_groups=mesh['grp'=2,'seq'=16] {'seq'}, dimensions={0}, use_global_device_ids=true | all-gather | bytes 408 | tf_op jit(solution)/shard_map/all_gather | solution.py:47
  459.7 3.0 copy.307
  467.6 19.9 %all-gather.9.cloned.1.call-done = bf16[192,128,64]{1,2,0:T(8,128)(2,1)} async-done(((bf16[12,128,64]{1,2,0:T(8,128)(2,1)}), bf16[192,128,64]{1,2,0:T(8,128)(2,1)}) %all-gather.9.cloned.1.call-update) | async-done | bytes 3145744 | tf_op jit(solution)/shard_map/all_gather | solution.py:47
  487.5 23.4 %while.101 = (s32[]{:T(128)}, f32[12,128,64]{2,1,0:T(8,128)S(1)}, s32[]{:T(128)}, bf16[16,12]{1,0:T(8,128)(2,1)S(1)}, bf16[16,12,128,64]{2,3,1,0:T(8,128)(2,1)},...) while((s32[]{:T(128)}, f32[12,128,64]{2,1,0:T(8,128)S(1)}, s32[]{:T(128)}, ...), condition=%wide.region_28.30_spmd.clone, body=%wide.region_27.29_spmd.clone.sunk | while | flops 491540 | bytes 1769759 | solution.py:63
  510.9 3.6 multiply_reduce_fusion.3
  519.7 3.2 fusion.112
  527.8 2.8 pad_maximum_fusion
  530.6 6.1 copy.311
  558.7 5.8 collective-permute-done.7
  568.3 19.6 %collective-permute-done.8 = bf16[256,768]{1,0:T(8,128)(2,1)S(1)} collective-permute-done((bf16[256,768]{1,0:T(8,128)(2,1)}, bf16[256,768]{1,0:T(8,128)(2,1)S(1)}, u32[]{:S(2)}, u32[]{:S(2)}) %collective-permute-start.8) | collective-permute-done | bytes 393248 | tf_op jit(solution)/shard_map/ppermute | solution.py:19
  590.0 72.0 %all-reduce.10 = (f32[4,1024]{1,0:T(4,128)}, f32[768,12]{0,1:T(8,128)}, f32[3,12]{1,0:T(4,128)}, f32[768]{0:T(1024)}, f32[768,16]{0,1:T(8,128)}, /*index=5*/f32[1]{0:T(128)}) all-reduce(f32[4,1024]{1,0:T(4,128)S(1)} %pad_maximum_fusion.3, f32[768,12]{0,1:T(8,128)S(1)} %convolution_bitcast_fusion.9, ...), channel_id=1, replica_groups=mesh['grp'=2,'seq'=16] {'seq'}, use_global_device_ids=true, to_apply=%region_39.41 | all-reduce | flops 26405 | bytes 211240 | tf_op jit(solution)/shard_map/psum | solution.py:263
  (643 shorter events, 356.6 us)
Async XLA Ops:
  7.2 48.0 %copy-start = (bf16[768,1024]{1,0:T(8,128)(2,1)S(1)}, bf16[768,1024]{1,0:T(8,128)(2,1)}, u32[]{:S(2)}) copy-start(bf16[768,1024]{1,0:T(8,128)(2,1)} %param.25) | copy-start | bytes 4718596
  7.2 122.0 %all-gather.7.cloned.1.call-start = ((), (), s32[]{:S(2)}) async-start(), calls=%async_computation.3 | async-start | bytes 6684672 | tf_op jit(solution)/shard_map/all_gather | solution.py:32
  7.2 2.1 collective-permute-start
  9.3 12.3 %collective-permute-start.1 = (bf16[256,768]{1,0:T(8,128)(2,1)S(1)}, bf16[256,768]{1,0:T(8,128)(2,1)S(1)}, u32[]{:S(2)}, u32[]{:S(2)}) collective-permute-start(bf16[256,768]{1,0:T(8,128)(2,1)S(1)} %collective-permute-done), channel_id=1, source_target_pairs={{0,2},{1,3},{2,0},{3,1},{4,6},{5,7},{6,4},{7,5},{8,10},{9,11},{10,... | collective-permute-start | bytes 1179656 | tf_op jit(solution)/shard_map/ppermute | solution.py:19
  21.6 10.6 %collective-permute-start.2 = (bf16[256,768]{1,0:T(8,128)(2,1)S(1)}, bf16[256,768]{1,0:T(8,128)(2,1)S(1)}, u32[]{:S(2)}, u32[]{:S(2)}) collective-permute-start(bf16[256,768]{1,0:T(8,128)(2,1)S(1)} %collective-permute-done.1), channel_id=1, source_target_pairs={{0,4},{1,5},{2,6},{3,7},{4,0},{5,1},{6,2},{7,3},{8,12},{9,13},{10,... | collective-permute-start | bytes 1179656 | tf_op jit(solution)/shard_map/ppermute | solution.py:19
  32.3 19.1 %collective-permute-start.3 = (bf16[256,768]{1,0:T(8,128)(2,1)S(1)}, bf16[256,768]{1,0:T(8,128)(2,1)S(1)}, u32[]{:S(2)}, u32[]{:S(2)}) collective-permute-start(bf16[256,768]{1,0:T(8,128)(2,1)S(1)} %collective-permute-done.2), channel_id=1, source_target_pairs={{0,8},{1,9},{2,10},{3,11},{4,12},{5,13},{6,14},{7,15},{8,0},{9,1},... | collective-permute-start | bytes 1179656 | tf_op jit(solution)/shard_map/ppermute | solution.py:19
  36.3 21.6 %copy-start.43 = (f32[1,1024]{1,0:T(1,128)}, f32[1,1024]{1,0:T(1,128)S(1)}, u32[]{:S(2)}) copy-start(f32[1,1024]{1,0:T(1,128)S(1)} %get-tuple-element.1700) | copy-start | bytes 12292
  36.3 21.6 %copy-start.45 = (f32[1,1024]{1,0:T(1,128)}, f32[1,1024]{1,0:T(1,128)S(1)}, u32[]{:S(2)}) copy-start(f32[1,1024]{1,0:T(1,128)S(1)} %get-tuple-element.1701) | copy-start | bytes 12292
  55.7 2.1 collective-permute-start.4
  59.6 59.0 %copy-start.17 = (bf16[256,1024]{1,0:T(8,128)(2,1)}, bf16[256,1024]{1,0:T(8,128)(2,1)S(1)}, u32[]{:S(2)}) copy-start(bf16[256,1024]{1,0:T(8,128)(2,1)S(1)} %get-tuple-element.1659) | copy-start | bytes 1572868
  62.1 51.9 %copy-start.6 = (f32[256,768]{0,1:T(8,128)}, f32[256,768]{0,1:T(8,128)S(1)}, u32[]{:S(2)}) copy-start(f32[256,768]{0,1:T(8,128)S(1)} %copy.254) | copy-start | bytes 2359300
  64.8 14.8 %all-to-all-start = ((f32[16,16,3]{1,2,0:T(4,128)}), f32[16,16,3]{1,2,0:T(4,128)}, u32[]{:S(2)}, u32[]{:S(2)}) async-start(f32[16,16,3]{1,2,0:T(4,128)} %copy.266), calls=%async_computation | async-start | bytes 65536 | tf_op jit(solution)/shard_map/all_to_all | solution.py:172
  75.4 143.7 %copy-start.52 = (f32[768]{0:T(1024)}, f32[768]{0:T(1024)S(1)}, u32[]{:S(2)}) copy-start(f32[768]{0:T(1024)S(1)} %mul.684) | copy-start | bytes 9220
  79.7 10.2 %all-to-all-start.1 = ((f32[16,1,256]{2,1,0:T(1,128)}), f32[16,1,256]{2,1,0:T(1,128)S(1)}, u32[]{:S(2)}, u32[]{:S(2)}) async-start(f32[16,1,256]{2,1,0:T(1,128)} %reshape.520), calls=%async_computation.1 | async-start | bytes 32768 | tf_op jit(solution)/shard_map/all_to_all | solution.py:171
  83.2 404.3 %all-gather.9.cloned.1.call-start = ((), (), s32[]{:S(2)}) async-start(), calls=%async_computation.4 | async-start | bytes 3342336 | tf_op jit(solution)/shard_map/all_gather | solution.py:47
  84.8 137.8 %copy-start.61 = (f32[256]{0:T(256)}, f32[256]{0:T(256)S(1)}, u32[]{:S(2)}) copy-start(f32[256]{0:T(256)S(1)} %convert_reduce_fusion) | copy-start | bytes 3076
  384.3 278.3 %reduce-scatter.4.cloned.1.call-start = ((), (), s32[]{:S(2)}) async-start(), calls=%async_computation.5 | async-start | bytes 5849088
  487.5 23.4 %copy-start.32 = (f32[256,12]{0,1:T(8,128)S(1)}, f32[256,12]{0,1:T(8,128)}, u32[]{:S(2)}) copy-start(f32[256,12]{0,1:T(8,128)} %copy-done.31) | copy-start | bytes 36868
  522.8 3.1 collective-permute-start.5
  548.9 41.0 %copy-start.60 = (f32[768]{0:T(1024)S(1)}, f32[768]{0:T(1024)}, u32[]{:S(2)}) copy-start(f32[768]{0:T(1024)} %get-tuple-element.1510) | copy-start | bytes 9220
  549.5 3.6 collective-permute-start.6
  553.1 11.5 %collective-permute-start.7 = (bf16[256,768]{1,0:T(8,128)(2,1)S(1)}, bf16[256,768]{1,0:T(8,128)(2,1)}, u32[]{:S(2)}, u32[]{:S(2)}) collective-permute-start(bf16[256,768]{1,0:T(8,128)(2,1)S(1)} %collective-permute-done.6), channel_id=1, source_target_pairs={{0,2},{1,3},{2,0},{3,1},{4,6},{5,7},{6,4},{7,5},{8,10},{9,11},{10,... | collective-permute-start | bytes 1179656 | tf_op jit(solution)/shard_map/ppermute | solution.py:19
  564.6 23.3 %collective-permute-start.8 = (bf16[256,768]{1,0:T(8,128)(2,1)}, bf16[256,768]{1,0:T(8,128)(2,1)S(1)}, u32[]{:S(2)}, u32[]{:S(2)}) collective-permute-start(bf16[256,768]{1,0:T(8,128)(2,1)} %collective-permute-done.7), channel_id=1, source_target_pairs={{0,4},{1,5},{2,6},{3,7},{4,0},{5,1},{6,2},{7,3},{8,12},{9,13},{10,... | collective-permute-start | bytes 1179656 | tf_op jit(solution)/shard_map/ppermute | solution.py:19
  587.8 74.8 %collective-permute-start.9 = (bf16[256,768]{1,0:T(8,128)(2,1)S(1)}, bf16[256,768]{1,0:T(8,128)(2,1)S(1)}, u32[]{:S(2)}, u32[]{:S(2)}) collective-permute-start(bf16[256,768]{1,0:T(8,128)(2,1)S(1)} %collective-permute-done.8), channel_id=1, source_target_pairs={{0,8},{1,9},{2,10},{3,11},{4,12},{5,13},{6,14},{7,15},{8,0},{9,1},... | collective-permute-start | bytes 1179656 | tf_op jit(solution)/shard_map/ppermute | solution.py:19
  (79 other events, 460.1 us)
Sparse Core Ops, SparseCore 0:
  63.5 65.5 all-gather.6
  384.5 102.9 all-gather.8
  536.9 95.7 reduce-scatter.3
where the time goes:
time: 683 us; the launch traced here: 674 us
  local copies, waits for them, and re-layouts  173 us (25%)
  blocking collectives  165 us (24%)
  matrix products  111 us (16%)
  waiting for transfers between devices  102 us (15%)
  other arithmetic  75.2 us (11%)
  starting transfers between devices  28.7 us (4%)
  between operations  17.9 us (3%)
    all_gather x1, blocking collectives, carried_in(): lax.all_gather(part.astype(kind), axis)  74.4 us
    psum x1, blocking collectives, per_device(): lax.psum((grad_conv_local, grad_dt_local, head_grads, back_gain, grad_cls...  72 us
    ppermute x8, waiting for transfers between devices, partner(): lax.ppermute(x, axis, [(i, i ^ 1 << apart) for i in range(lax.axis_size(a...  61.6 us
    dynamic_update_slice x56, local copies, waits for them, and re-layouts, full_branch(): _, outputs = lax.scan(block_step, start_state, pieces)  35.7 us
    dot_general x12, matrix products, block_step(): jnp.einsum('hts,shp->thp', decay_mix * scores[None, :, :], weighted, prec...  30.2 us
    dynamic_slice x28, local copies, waits for them, and re-layouts, full_branch(): _, outputs = lax.scan(block_step, start_state, pieces)  26.2 us
    dot_general x12, matrix products, block_step(): jnp.einsum('sn,shp->hnp', in_map, weighted * tail_decay[:, :, None], prec...  23.9 us
    dot_general x12, matrix products, block_step(): jnp.einsum('tn,hnp->thp', out_map, carry_state, precision=PRECISE)  21.2 us
  transfers between devices with their start and end apart: 15, of which 13 were waited for; matrix products, arithmetic and copies ran while one was open for 7% of the time, Pallas kernels for 0%

commit v1 on v0

v1 whole, which is shorter than its diff:
```python
import functools

import jax
import jax.numpy as jnp
from jax import lax
from jax.experimental import pallas as pl
from jax.experimental.pallas import tpu as pltpu
from jax.sharding import PartitionSpec as P

HEADS = 12
HDIM = 64
STATE = 128
LABELS = 16
LANES = 128
HALO = 8
META = 8
EPSILON = 1e-05
FAR = -1e30

F32 = jnp.float32
BF16 = jnp.bfloat16


def partner(x, axis, apart):
    return lax.ppermute(x, axis, [(i, i ^ 1 << apart) for i in range(lax.axis_size(axis))])


def passed_along(x, axis, by):
    length = lax.axis_size(axis)
    pairs = [(i, i + by) for i in range(length) if 0 <= i + by < length]
    return lax.ppermute(x, axis, pairs)


def dot(a, b, left=1, right=0):
    return lax.dot_general(a, b, (((left,), (right,)), ((), ())), preferred_element_type=F32)


def pieces(x, count):
    parts = []
    for _ in range(count):
        part = x.astype(BF16)
        parts.append(part)
        x = x - part.astype(F32)
    return parts


def finer(a, x, count, left=1, right=0):
    return sum(dot(a, part, left, right) for part in pieces(x, count))


def iota(shape, axis):
    return lax.broadcasted_iota(jnp.int32, shape, axis)


def spread_heads(x):
    rows = x.shape[0]
    first = iota((rows, LANES), 1) < HDIM
    return jnp.concatenate(
        [
            jnp.where(
                first,
                jnp.broadcast_to(x[:, 2 * pair : 2 * pair + 1], (rows, LANES)),
                jnp.broadcast_to(x[:, 2 * pair + 1 : 2 * pair + 2], (rows, LANES)),
            )
            for pair in range(HEADS // 2)
        ],
        axis=1,
    )


def head_sums(x):
    width = x.shape[1]
    member = (iota((width, LANES), 0) // HDIM == iota((width, LANES), 1)).astype(BF16)
    return sum(dot(part, member) for part in pieces(x, 2))


def call(body, outs, *args, scratch=(), scalars=0):
    in_specs = [
        pl.BlockSpec(memory_space=pltpu.SMEM if i < scalars else pltpu.VMEM)
        for i in range(len(args))
    ]
    return pl.pallas_call(
        body,
        out_shape=[jax.ShapeDtypeStruct(shape, dtype) for shape, dtype in outs],
        in_specs=in_specs,
        out_specs=[pl.BlockSpec(memory_space=pltpu.VMEM)] * len(outs),
        scratch_shapes=list(scratch),
        compiler_params=pltpu.CompilerParams(vmem_limit_bytes=40 * 1024 * 1024),
    )(*args)


def teacher_kernel(rows, weights, meta, packed, own):
    logits = dot(rows[...], weights[...])
    top = jnp.max(logits, axis=1, keepdims=True)
    shifted = logits - top
    logp = shifted - jnp.log(jnp.sum(jnp.exp(shifted), axis=1, keepdims=True))
    count = logits.shape[0]
    same = (iota((count, count), 0) == iota((count, count), 1)).astype(BF16)
    logp_t = sum(dot(part, same, 0, 0) for part in pieces(logp, 3))
    prob_t = jnp.exp(logp_t)
    packed[0:LABELS, :] = prob_t
    packed[LABELS:, :] = meta[...]
    own[...] = jnp.sum(prob_t * logp_t, axis=0, keepdims=True) * meta[2:3, :]


def target_kernel(place, packed, target):
    length = target.shape[0]
    height = LABELS + META
    count = packed.shape[1]
    me = place[0].astype(F32)
    position = iota((length, count), 0).astype(F32)
    total = jnp.zeros((length, LANES), F32)
    fill = jnp.zeros((LANES - 2 * LABELS, count), F32)
    ones = jnp.ones((LABELS, count), F32)
    for source in range(packed.shape[0] // height):
        base = source * height
        prob = packed[base : base + LABELS, :]
        meta = packed[base + LABELS : base + height, :]
        start = jnp.where(meta[0:1, :] == me, meta[1:2, :], FAR)
        stop = start + meta[2:3, :]
        covered = ((position >= start) & (position < stop)).astype(F32).astype(BF16)
        total = total + finer(covered, jnp.concatenate([prob, ones, fill], axis=0), 2, 1, 1)
    target[...] = total


def front_kernel(
    hidden, edge, w_in, w_dt, heads, conv_w, message, mixed_o, conv_o, raw_o, step_o, run_o, run_t
):
    length = hidden.shape[0]
    taps = conv_w.shape[0]
    weights = w_in[...]
    raw_o[0:length, :] = dot(hidden[...], weights).astype(BF16).astype(F32)
    raw_o[length:, :] = dot(edge[...], weights).astype(BF16).astype(F32)
    before = dot(hidden[...], w_dt[...]) + heads[0:1, :]
    step = jnp.maximum(before, 0.0) + jnp.log1p(jnp.exp(-jnp.abs(before)))
    step = jnp.where(iota((length, LANES), 1) < HEADS, step, 0.0)
    log_decay = -step * jnp.exp(heads[1:2, :])
    later = (iota((length, length), 1) >= iota((length, length), 0)).astype(BF16)
    run = finer(later, log_decay, 3)
    step_o[:, 0:LANES] = step
    step_o[:, LANES:] = before
    run_o[...] = run
    run_t[...] = run.T
    conv = conv_w[0:1, :] * raw_o[0:length, :]
    for tap in range(1, taps):
        conv = conv + conv_w[tap : tap + 1, :] * raw_o[pl.ds(tap, length), :]
    conv_o[...] = conv
    mixed = (conv / (1.0 + jnp.exp(-conv))).astype(BF16)
    mixed_o[...] = mixed
    width = HEADS * HDIM
    total = run[0:1, :]
    weighted = mixed[:, :width].astype(F32) * spread_heads(step * jnp.exp(total - run))
    state = dot(mixed[:, width : width + STATE], weighted.astype(BF16), 0, 0)
    message[:, :width] = state.astype(BF16)
    high, middle, low = (part.astype(F32) for part in pieces(total, 3))
    tags = high + pltpu.roll(middle, 16, 1) + pltpu.roll(low, 32, 1)
    message[:, width:] = jnp.broadcast_to(tags, (STATE, LANES)).astype(BF16)


def decay_blocks(run, run_t, head, half):
    top = run[0:half, head : head + 1] - run_t[head : head + 1, :]
    low = run[half:, head : head + 1] - run_t[head : head + 1, half:]
    top_seen = iota(top.shape, 1) >= iota(top.shape, 0)
    low_seen = iota(low.shape, 1) >= iota(low.shape, 0)
    return jnp.exp(jnp.where(top_seen, top, FAR)), jnp.exp(jnp.where(low_seen, low, FAR))


def local_kernel(mixed, step, run, run_t, local):
    length = mixed.shape[0]
    half = length // 2
    width = HEADS * HDIM
    in_map = mixed[:, width : width + STATE]
    out_map = mixed[:, width + STATE :]
    top_scores = dot(out_map[0:half], in_map, 1, 1)
    low_scores = dot(out_map[half:], in_map[half:], 1, 1)
    weighted = (mixed[:, :width].astype(F32) * spread_heads(step[:, 0:LANES])).astype(BF16)
    first = iota((half, LANES), 1) < HDIM
    for pair in range(HEADS // 2):
        lanes = slice(pair * LANES, (pair + 1) * LANES)
        own = weighted[:, lanes]
        tops, lows = [], []
        for head in (2 * pair, 2 * pair + 1):
            top, low = decay_blocks(run, run_t, head, half)
            tops.append(dot((top * top_scores).astype(BF16), own))
            lows.append(dot((low * low_scores).astype(BF16), own[half:]))
        local[0:half, lanes] = jnp.where(first, tops[0], tops[1])
        local[half:, lanes] = jnp.where(first, lows[0], lows[1])


def states_kernel(arrived, onward, decay):
    count = arrived.shape[0]
    width = HEADS * HDIM
    rows = arrived.shape[1]
    keep = iota((rows, LANES), 1) < HEADS
    state = jnp.zeros((rows, width), F32)
    for source in range(count - 1, -1, -1):
        onward[source] = state.astype(BF16)
        tags = arrived[source, :, width:].astype(F32)
        total = tags + pltpu.roll(tags, LANES - 16, 1) + pltpu.roll(tags, LANES - 32, 1)
        factor = spread_heads(jnp.exp(jnp.where(keep, total, 0.0)))
        decay[source] = factor
        state = arrived[source, :, :width].astype(F32) + factor * state


def state_grads_kernel(arrived, decay, onward):
    count = arrived.shape[0]
    state = jnp.zeros(arrived.shape[1:], F32)
    for source in range(count):
        onward[source] = state.astype(BF16)
        state = arrived[source].astype(F32) + decay[source] * state


def middle_kernel(
    local, mixed, run, state, wide, w_out, w_cls, target,
    back_state, grad_scanned, scaled_o, normed_o, branch_o, back_branch_o, logits_o, run_grad, small,
):
    length = mixed.shape[0]
    width = HEADS * HDIM
    values = mixed[:, :width].astype(F32)
    out_map = mixed[:, width + STATE :]
    reach = spread_heads(jnp.exp(run[...]))
    carried = dot(out_map, state[...]) * reach
    gain = wide[0:1, :]
    skip = wide[1:2, :]
    scanned = local[...] + carried + skip * values
    scale = lax.rsqrt(jnp.mean(scanned * scanned, axis=1, keepdims=True) + EPSILON)
    plain = scanned * scale
    normed = (plain * gain).astype(BF16)
    normed_o[...] = normed
    branch = dot(normed, w_out[...]).astype(BF16)
    branch_o[...] = branch
    label = iota((length, LANES), 1) < LABELS
    logits = jnp.where(label, dot(branch, w_cls[...]), FAR)
    shifted = logits - jnp.max(logits, axis=1, keepdims=True)
    raised = jnp.exp(shifted)
    whole = jnp.sum(raised, axis=1, keepdims=True)
    logp = shifted - jnp.log(whole)
    wanted = target[...]
    cover = wanted[:, LABELS : LABELS + 1]
    back_logits = jnp.where(label, cover * (raised / whole) - wanted, 0.0)
    logits_o[...] = back_logits
    lost = jnp.sum(jnp.where(label, wanted * logp, 0.0), axis=0, keepdims=True)
    back_branch = sum(dot(part, w_cls[...], 1, 1) for part in pieces(back_logits, 2)).astype(BF16)
    back_branch_o[...] = back_branch
    back_normed = dot(back_branch, w_out[...], 1, 1)
    back_plain = back_normed * gain
    along = jnp.mean(back_plain * plain, axis=1, keepdims=True)
    back = scale * (back_plain - plain * along)
    grad_scanned[...] = back
    scaled = (back * reach).astype(BF16)
    scaled_o[...] = scaled
    back_state[...] = dot(out_map, scaled, 0, 0).astype(BF16)
    run_grad[...] = head_sums(back * carried)
    small[0:1, :] = jnp.sum(back_normed * plain, axis=0, keepdims=True)
    small[1:2, :] = jnp.sum(back * values, axis=0, keepdims=True)
    small[2:3, :] = jnp.zeros((1, width), F32)
    small[2:3, 0:LANES] = lost
    small[3:, :] = jnp.zeros((5, width), F32)


def halves(full, keep, send, odd, blocks):
    size = full.shape[0] // blocks
    for side in (0, 1):

        @pl.when(odd == side)
        def _():
            for block in range(blocks // 2):
                at = slice(block * size, (block + 1) * size)
                mine = (2 * block + side) * size
                other = (2 * block + 1 - side) * size
                keep[at, :] = full[mine : mine + size, :]
                send[at, :] = full[other : other + size, :].astype(BF16)


def outward_kernel(blocks, place, normed, back_branch, branch, back_logits, keep, send, cls, full):
    full[...] = dot(normed[...], back_branch[...], 0, 0)
    halves(full, keep, send, place[0] % 2, blocks)
    parts = pieces(back_logits[...], 2)
    cls[...] = sum(dot(part, branch[...], 0, 0) for part in parts)[0:LABELS]


def local_back_kernel(
    mixed, step, run, run_t, grad_scanned, scaled, state, carried_grad, weighted_grad, maps, run_grad
):
    length = mixed.shape[0]
    half = length // 2
    width = HEADS * HDIM
    in_map = mixed[:, width : width + STATE]
    out_map = mixed[:, width + STATE :]
    top_scores = dot(out_map[0:half], in_map, 1, 1)
    low_scores = dot(out_map[half:], in_map[half:], 1, 1)
    weighted = (mixed[:, :width].astype(F32) * spread_heads(step[:, 0:LANES])).astype(BF16)
    lane = iota((length, LANES), 1)
    back_top = jnp.zeros((half, length), F32)
    back_low = jnp.zeros((half, half), F32)
    rows_top = jnp.zeros((half, LANES), F32)
    rows_low = jnp.zeros((half, LANES), F32)
    columns = jnp.zeros((length, LANES), F32)
    columns_low = jnp.zeros((half, LANES), F32)
    for pair in range(HEADS // 2):
        lanes = slice(pair * LANES, (pair + 1) * LANES)
        own = weighted[:, lanes]
        back_f = grad_scanned[:, lanes]
        back = back_f.astype(BF16)
        tops, lows = [], []
        for side in (0, 1):
            head = 2 * pair + side
            top, low = decay_blocks(run, run_t, head, half)
            mine = jnp.where((lane >= HDIM) == (side == 1), back_f, 0.0).astype(BF16)
            mix_top = (top * top_scores).astype(BF16)
            mix_low = (low * low_scores).astype(BF16)
            tops.append(dot(mix_top, back[0:half], 0, 0))
            lows.append(dot(mix_low, back[half:], 0, 0))
            grad_top = top * dot(mine[0:half], own, 1, 1)
            grad_low = low * dot(mine[half:], own[half:], 1, 1)
            back_top = back_top + grad_top
            back_low = back_low + grad_low
            part_top = (grad_top * top_scores).astype(BF16)
            part_low = (grad_low * low_scores).astype(BF16)
            marker = (lane == head).astype(F32).astype(BF16)
            rows_top = rows_top + dot(part_top, marker)
            rows_low = rows_low + dot(part_low, marker[half:])
            columns = columns + dot(part_top, marker[0:half], 0, 0)
            columns_low = columns_low + dot(part_low, marker[half:], 0, 0)
        weighted_grad[0:half, lanes] = jnp.where(lane[0:half] < HDIM, tops[0][0:half], tops[1][0:half])
        weighted_grad[half:, lanes] = jnp.where(
            lane[half:] < HDIM, tops[0][half:] + lows[0], tops[1][half:] + lows[1]
        )
    back_top = back_top.astype(BF16)
    back_low = back_low.astype(BF16)
    from_state = dot(scaled[...], state[...], 1, 1)
    maps[0:half, STATE:] = dot(back_top, in_map) + from_state[0:half]
    maps[half:, STATE:] = dot(back_low, in_map[half:]) + from_state[half:]
    in_grad = dot(back_top, out_map[0:half], 0, 0)
    maps[0:half, 0:STATE] = in_grad[0:half]
    maps[half:, 0:STATE] = in_grad[half:] + dot(back_low, out_map[half:], 0, 0)
    run_grad[0:half, :] = carried_grad[0:half, :] + rows_top - columns[0:half]
    run_grad[half:, :] = carried_grad[half:, :] + rows_low - columns[half:] - columns_low


def last_kernel(
    blocks, place, hidden, edge, mixed, conv, raw, step, run, state, state_grad, weighted_grad, maps,
    run_grad, grad_scanned, heads, wide, conv_w, small, cls, own,
    keep, send, rim, back_raw_o, step_grad_o, conv_sums, sums, full, padded,
):
    length = mixed.shape[0]
    taps = conv_w.shape[0]
    width = HEADS * HDIM
    values = mixed[:, :width].astype(F32)
    in_map = mixed[:, width : width + STATE]
    total = run[0:1, :]
    tail = spread_heads(jnp.exp(total - run[...]))
    steps = spread_heads(step[:, 0:LANES])
    incoming = state_grad[...]
    reached = dot(in_map, incoming) * tail
    weighted = values * steps
    ended = head_sums(reached * weighted)
    in_grad = maps[:, 0:STATE] + dot((weighted * tail).astype(BF16), incoming, 1, 1)
    weighted_all = weighted_grad[...] + reached
    product = jnp.sum(incoming.astype(F32) * state[...].astype(F32), axis=0, keepdims=True)
    total_grad = jnp.exp(total) * head_sums(jnp.broadcast_to(product, (8, width)))[0:1]
    row, column = iota((length, length), 0), iota((length, length), 1)
    decay_grad = (
        finer((column <= row).astype(BF16), run_grad[...], 3)
        + finer((column > row).astype(BF16), ended, 3)
        + total_grad
    )
    rate = jnp.exp(heads[1:2, :])
    step_grad = head_sums(weighted_all * values) - rate * decay_grad
    before = step[:, LANES:]
    step_grad = jnp.where(
        iota((length, LANES), 1) < HEADS, step_grad / (1.0 + jnp.exp(-before)), 0.0
    )
    step_grad_b = step_grad.astype(BF16)
    step_grad_o[...] = step_grad_b
    values_grad = weighted_all * steps + wide[1:2, :] * grad_scanned[...]
    padded[0:HALO, :] = jnp.zeros((HALO, padded.shape[1]), F32)
    padded[HALO + length :, :] = jnp.zeros((HALO, padded.shape[1]), F32)

    def through(mixed_grad, lanes):
        inner = conv[:, lanes]
        gate = 1.0 / (1.0 + jnp.exp(-inner))
        padded[HALO : HALO + length, lanes] = mixed_grad * gate * (1.0 + inner * (1.0 - gate))

    through(values_grad, slice(0, width))
    through(in_grad, slice(width, width + STATE))
    through(maps[:, STATE:], slice(width + STATE, width + 2 * STATE))
    back_conv = padded[HALO : HALO + length, :]
    rim[...] = padded[length : length + HALO, :]
    back_raw = jnp.zeros((length + HALO, padded.shape[1]), F32)
    for tap in range(taps):
        conv_sums[tap : tap + 1, :] = jnp.sum(
            back_conv * raw[pl.ds(tap, length), :], axis=0, keepdims=True
        )
        back_raw = back_raw + conv_w[tap : tap + 1, :] * padded[pl.ds(HALO - tap, length + HALO), :]
    back_raw_o[...] = back_raw[0:length]
    full[...] = dot(hidden[...], back_raw[0:length].astype(BF16), 0, 0) + dot(
        edge[...], back_raw[length:].astype(BF16), 0, 0
    )
    halves(full, keep, send, place[0] % 2, blocks)
    dt_grad = dot(step_grad_b, hidden[...], 0, 0)
    sums[0:LABELS, :] = dt_grad[0:LABELS]
    sums[LABELS : 2 * LABELS, :] = cls[...]
    base = 2 * LABELS
    sums[base:, :] = jnp.zeros((8, width), F32)
    sums[base : base + 1, :] = small[0:1, :]
    sums[base + 1 : base + 2, 0:LANES] = jnp.sum(step_grad, axis=0, keepdims=True)
    log_decay = -step[:, 0:LANES] * rate
    sums[base + 2 : base + 3, 0:LANES] = jnp.sum(decay_grad * log_decay, axis=0, keepdims=True)
    sums[base + 3 : base + 4, 0:LANES] = head_sums(jnp.broadcast_to(small[1:2, :], (8, width)))[0:1]
    sums[base + 4 : base + 5, 0:LANES] = own[...] - small[2:3, 0:LANES]


def hidden_kernel(back_raw, rim, step_grad, w_in, w_dt, conv_w, out, joined, edge):
    taps = conv_w.shape[0]
    joined[...] = back_raw[...]
    edge[0:HALO, :] = rim[...]
    edge[HALO:, :] = jnp.zeros((HALO, edge.shape[1]), F32)
    head = joined[0:HALO, :]
    for tap in range(taps):
        head = head + conv_w[tap : tap + 1, :] * edge[pl.ds(HALO - tap, HALO), :]
    joined[0:HALO, :] = head
    out[...] = (
        dot(joined[...].astype(BF16), w_in[...], 1, 1) + dot(step_grad[...], w_dt[...], 1, 1)
    ).astype(BF16)


def swapped(x, axis="seq"):
    return lax.all_to_all(x, axis, split_axis=0, concat_axis=0, tiled=True)


def scattered(keep, send, devices):
    both = keep + partner(send, "seq", 0).astype(F32)
    groups = [[i for i in range(devices) if i % 2 == side] for side in (0, 1)]
    parts = lax.all_to_all(
        both.astype(BF16), "seq", split_axis=0, concat_axis=0, axis_index_groups=groups, tiled=True
    )
    size = keep.shape[0] // (devices // 2)
    return jnp.sum(parts.reshape(devices // 2, size, keep.shape[1]).astype(F32), axis=0)


def per_device(
    hidden_in, w_in, w_dt, dt_bias, a_log, conv_w, d_skip, norm_gain, w_out, w_cls,
    teacher_rows, w_teacher, row_dest, row_start, row_len,
):
    devices = lax.axis_size("seq")
    length = hidden_in.shape[0]
    width = HEADS * HDIM
    channels = w_in.shape[1]
    slice_rows = STATE // devices
    row_count = teacher_rows.shape[0]
    place = lax.axis_index("seq").astype(jnp.int32).reshape(1)

    edge = passed_along(hidden_in[:HALO], "seq", -1)
    meta = jnp.concatenate(
        [
            row_dest.reshape(1, row_count),
            row_start.reshape(1, row_count),
            row_len.reshape(1, row_count),
            jnp.zeros((META - 3, row_count), jnp.int32),
        ],
        axis=0,
    ).astype(F32)
    packed, own = call(
        teacher_kernel,
        [((LABELS + META, row_count), F32), ((1, row_count), F32)],
        teacher_rows, w_teacher, meta,
    )
    everyone = lax.all_gather(packed, "seq", axis=0, tiled=True)

    w_dt_wide = jnp.pad(w_dt, ((0, 0), (0, LANES - HEADS)))
    w_cls_wide = jnp.pad(w_cls, ((0, 0), (0, LANES - LABELS)))
    heads = jnp.pad(jnp.stack([dt_bias, a_log]), ((0, 6), (0, LANES - HEADS)))
    wide = jnp.pad(jnp.stack([norm_gain, jnp.repeat(d_skip, HDIM)]), ((0, 6), (0, 0)))

    message, mixed, conv, raw, step, run, run_t = call(
        front_kernel,
        [
            ((STATE, width + LANES), BF16),
            ((length, channels), BF16),
            ((length, channels), F32),
            ((length + HALO, channels), F32),
            ((length, 2 * LANES), F32),
            ((length, LANES), F32),
            ((LANES, length), F32),
        ],
        hidden_in, edge, w_in, w_dt_wide, heads, conv_w,
    )
    arrived = swapped(message).reshape(devices, slice_rows, width + LANES)
    (local,) = call(local_kernel, [((length, width), F32)], mixed, step, run, run_t)
    onward, decay = call(
        states_kernel,
        [((devices, slice_rows, width), BF16), ((devices, slice_rows, width), F32)],
        arrived,
    )
    state = swapped(onward.reshape(STATE, width))
    (target,) = call(target_kernel, [((length, LANES), F32)], place, everyone, scalars=1)

    (
        back_state, grad_scanned, scaled, normed, branch, back_branch, back_logits, carried_grad, small,
    ) = call(
        middle_kernel,
        [
            ((STATE, width), BF16),
            ((length, width), F32),
            ((length, width), BF16),
            ((length, width), BF16),
            ((length, width), BF16),
            ((length, width), BF16),
            ((length, LANES), F32),
            ((length, LANES), F32),
            ((8, width), F32),
        ],
        local, mixed, run, state, wide, w_out, w_cls_wide, target,
    )
    back_arrived = swapped(back_state).reshape(devices, slice_rows, width)
    keep_out, send_out, cls = call(
        functools.partial(outward_kernel, devices),
        [((width // 2, width), F32), ((width // 2, width), BF16), ((LABELS, width), F32)],
        place, normed, back_branch, branch, back_logits,
        scratch=[pltpu.VMEM((width, width), F32)], scalars=1,
    )
    weighted_grad, maps, run_grad = call(
        local_back_kernel,
        [((length, width), F32), ((length, 2 * STATE), F32), ((length, LANES), F32)],
        mixed, step, run, run_t, grad_scanned, scaled, state, carried_grad,
    )
    (back_onward,) = call(
        state_grads_kernel, [((devices, slice_rows, width), BF16)], back_arrived, decay
    )
    state_grad = swapped(back_onward.reshape(STATE, width))
    grad_w_out = scattered(keep_out, send_out, devices)

    keep_in, send_in, rim, back_raw, step_grad, conv_sums, sums = call(
        functools.partial(last_kernel, devices),
        [
            ((width // 2, channels), F32),
            ((width // 2, channels), BF16),
            ((HALO, channels), F32),
            ((length, channels), F32),
            ((length, LANES), BF16),
            (conv_w.shape, F32),
            ((2 * LABELS + 8, width), F32),
        ],
        place, hidden_in, edge, mixed, conv, raw, step, run, state, state_grad, weighted_grad, maps,
        run_grad, grad_scanned, heads, wide, conv_w, small, cls, own,
        scratch=[pltpu.VMEM((width, channels), F32), pltpu.VMEM((length + 2 * HALO, channels), F32)],
        scalars=1,
    )
    grad_w_in = scattered(keep_in, send_in, devices)
    (grad_hidden,) = call(
        hidden_kernel,
        [((length, w_in.shape[0]), BF16)],
        back_raw, passed_along(rim, "seq", 1), step_grad, w_in, w_dt_wide, conv_w,
        scratch=[pltpu.VMEM((length, channels), F32), pltpu.VMEM((2 * HALO, channels), F32)],
    )
    flat = jnp.concatenate([sums.reshape(-1, LANES), conv_sums.reshape(-1, LANES)], axis=0)
    for bit in range(devices.bit_length() - 1):
        flat = flat + partner(flat, "seq", bit)
    split = sums.size // LANES
    sums = flat[:split].reshape(sums.shape)
    base = 2 * LABELS
    loss = jnp.sum(sums[base + 4, 0:LANES]).reshape(1) / (row_count * devices)
    return (
        grad_hidden,
        grad_w_in,
        grad_w_out,
        flat[split:].reshape(conv_w.shape),
        sums[0:HEADS].T,
        sums[base + 1 : base + 4, 0:HEADS],
        sums[base],
        sums[LABELS : 2 * LABELS].T,
        loss,
    )


def solution(mesh):
    rows = P(("grp", "seq"), None)
    placed = (rows,) + (P(),) * 9 + (rows, P(), rows, P(("grp", "seq")), P(("grp", "seq")))
    part = P("grp", None)
    return jax.shard_map(
        per_device,
        mesh=mesh,
        in_specs=placed,
        out_specs=(rows, rows, rows, part, part, part, P("grp"), part, P("grp")),
        check_vma=False,
    )
```

time: 683 us -> 176 us (0.26); the launches traced: 674 us -> 175 us
  blocking collectives: 165 us -> 22.2 us
  local copies, waits for them, and re-layouts: 173 us -> 33.6 us
  matrix products: 111 us -> 0 us
  other arithmetic: 75.2 us -> 9.12 us
  waiting for transfers between devices: 102 us -> 48.9 us
  Pallas kernels: 0 us -> 22.5 us
  between operations: 17.9 us -> 2.86 us
    dot_general x67 -> x0, matrix products: 111 us -> none  [the longest x12 30.2 us: block_step(): jnp.einsum('hts,shp->thp', decay_mix * scores[None, :, :], weighted, prec...]
    psum x1 -> x0, blocking collectives: 72 us -> none  [per_device(): lax.psum((grad_conv_local, grad_dt_local, head_grads, back_gain, grad_cls...]
    all_gather x2 -> x1, blocking collectives: 92.9 us -> 22.2 us  [per_device(): everyone = lax.all_gather(packed, 'seq', axis=0, tiled=True)]
    dynamic_slice x60 -> x0, local copies, waits for them, and re-layouts: 45.1 us -> none  [the longest x28 26.2 us: full_branch(): _, outputs = lax.scan(block_step, start_state, pieces)]
    ppermute x8 -> x6, waiting for transfers between devices: 61.6 us -> 20.8 us  [partner(): lax.ppermute(x, axis, [(i, i ^ 1 << apart) for i in range(lax.axis_size(a...]
    dynamic_update_slice x56 -> x0, local copies, waits for them, and re-layouts: 35.7 us -> none  [full_branch(): _, outputs = lax.scan(block_step, start_state, pieces)]
    all_gather x2 -> x0, waiting for transfers between devices: 29.8 us -> none  [the longest x1 19.9 us: carried_in(): lax.all_gather(part.astype(kind), axis)]
    reshape x22 -> x4, local copies, waits for them, and re-layouts: 25.9 us -> 0.66 us  [the longest x1 0.62 us: per_device(): flat[split:].reshape(conv_w.shape)]
  transfers between devices with their start and end apart: 15 -> 14, of which waited for: 13 -> 10; matrix products, arithmetic and copies ran while one was open for 7% -> 7% of each run, Pallas kernels for 0% -> 8%
where the time goes in v1:
time: 176 us; the launch traced here: 175 us
  waiting for transfers between devices  48.9 us (28%)
  starting transfers between devices  35.5 us (20%)
  local copies, waits for them, and re-layouts  33.6 us (19%)
  Pallas kernels  22.5 us (13%)
  blocking collectives  22.2 us (13%)
  other arithmetic  9.12 us (5%)
  between operations  2.86 us (2%)
    unnamed x106, local copies, waits for them, and re-layouts  29.5 us
    pallas_call x11, Pallas kernels, call(): pl.pallas_call(body, out_shape=[jax.ShapeDtypeStruct(shape, dtype) for sh...  22.5 us
    all_gather x1, blocking collectives, per_device(): everyone = lax.all_gather(packed, 'seq', axis=0, tiled=True)  22.2 us
    ppermute x6, waiting for transfers between devices, partner(): lax.ppermute(x, axis, [(i, i ^ 1 << apart) for i in range(lax.axis_size(a...  20.8 us
    all_to_all x4, starting transfers between devices, swapped(): return lax.all_to_all(x, axis, split_axis=0, concat_axis=0, tiled=True)  19.5 us
    all_to_all x2, waiting for transfers between devices, scattered(): lax.all_to_all(both.astype(BF16), 'seq', split_axis=0, concat_axis=0, axi...  13.7 us
    all_to_all x4, waiting for transfers between devices, swapped(): return lax.all_to_all(x, axis, split_axis=0, concat_axis=0, tiled=True)  13.5 us
    all_to_all x2, starting transfers between devices, scattered(): lax.all_to_all(both.astype(BF16), 'seq', split_axis=0, concat_axis=0, axi...  8.3 us
  transfers between devices with their start and end apart: 14, of which 10 were waited for; matrix products, arithmetic and copies ran while one was open for 7% of the time, Pallas kernels for 8%

profile of v1, /device:TPU:0, one launch (start us, length us, event | category | flops | bytes accessed | tf_op | source)
XLA Modules:
  0.0 174.8 jit_solution(16384539213844291934)
XLA Ops:
  7.5 2.8 %shard_map.214 = (bf16[128,896]{1,0:T(8,128)(2,1)}, bf16[256,1024]{1,0:T(8,128)(2,1)S(1)}, f32[256,1024]{1,0:T(8,128)S(1)}, f32[264,1024]{1,0:T(8,128)S(1)}, f32...) custom-call(bf16[256,768]{1,0:T(8,128)(2,1)S(1)} %copy-done.2, ...), custom_call_target="tpu_custom_call" | custom-call | tf_op jit(solution)/shard_map/pallas_call | solution.py:82
  12.3 8.7 %all-to-all-start = ((bf16[16,8,896]{2,1,0:T(8,128)(2,1)}), bf16[16,8,896]{2,1,0:T(8,128)(2,1)S(1)}, u32[]{:S(2)}, u32[]{:S(2)}) async-start(bf16[16,8,896]{2,1,0:T(8,128)(2,1)} %bitcast.3), calls=%async_computation | async-start | bytes 458752 | tf_op jit(solution)/shard_map/all_to_all | solution.py:429
  22.0 8.5 %all-to-all-done.arrived = bf16[16,8,896]{2,1,0:T(8,128)(2,1)S(1)} async-done(((bf16[16,8,896]{2,1,0:T(8,128)(2,1)}), bf16[16,8,896]{2,1,0:T(8,128)(2,1)S(1)}, u32[]{:S(2)}, u32[]{:S(2)}) %all-to-all-start) | async-done | bytes 229408 | tf_op jit(solution)/shard_map/all_to_all | solution.py:429
  32.1 3.5 %all-to-all-start.1 = ((bf16[16,8,768]{2,1,0:T(8,128)(2,1)}), bf16[16,8,768]{2,1,0:T(8,128)(2,1)S(1)}, u32[]{:S(2)}, u32[]{:S(2)}) async-start(bf16[16,8,768]{2,1,0:T(8,128)(2,1)} %get-tuple-element.48), calls=%async_computation.1 | async-start | bytes 393216 | tf_op jit(solution)/shard_map/all_to_all | solution.py:429
  37.8 22.2 %all_gather.3.packed = f32[384,128]{1,0:T(8,128)S(1)} all-gather(f32[24,128]{1,0:T(8,128)S(1)} %get-tuple-element.50), channel_id=1, replica_groups=mesh['grp'=2,'seq'=16] {'seq'}, dimensions={0}, use_global_device_ids=true | all-gather | bytes 208896 | tf_op jit(solution)/shard_map/all_gather | solution.py:469
  63.2 3.5 %shard_map.219 = (bf16[128,768]{1,0:T(8,128)(2,1)S(1)}, f32[256,768]{1,0:T(8,128)S(1)}, bf16[256,768]{1,0:T(8,128)(2,1)S(1)}, bf16[256,768]{1,0:T(8,128)(2,1)S(1...) custom-call(f32[256,768]{1,0:T(8,128)S(1)} %shard_map.216.local, ...), custom_call_target="tpu_custom_call" | custom-call | tf_op jit(solution)/shard_map/pallas_call | solution.py:82
  71.1 3.7 %all-to-all-start.2 = ((bf16[16,8,768]{2,1,0:T(8,128)(2,1)}), bf16[16,8,768]{2,1,0:T(8,128)(2,1)S(1)}, u32[]{:S(2)}, u32[]{:S(2)}) async-start(bf16[16,8,768]{2,1,0:T(8,128)(2,1)} %bitcast.21), calls=%async_computation.2 | async-start | bytes 393216 | tf_op jit(solution)/shard_map/all_to_all | solution.py:429
  80.6 3.1 %all-to-all-done.2.arrived = bf16[16,8,768]{2,1,0:T(8,128)(2,1)S(1)} async-done(((bf16[16,8,768]{2,1,0:T(8,128)(2,1)}), bf16[16,8,768]{2,1,0:T(8,128)(2,1)S(1)}, u32[]{:S(2)}, u32[]{:S(2)}) %all-to-all-start.2) | async-done | bytes 196640 | tf_op jit(solution)/shard_map/all_to_all | solution.py:429
  84.4 3.7 %all-to-all-start.3 = ((bf16[16,8,768]{2,1,0:T(8,128)(2,1)}), bf16[16,8,768]{2,1,0:T(8,128)(2,1)S(1)}, u32[]{:S(2)}, u32[]{:S(2)}) async-start(bf16[16,8,768]{2,1,0:T(8,128)(2,1)} %shard_map.220), calls=%async_computation.3 | async-start | bytes 393216 | tf_op jit(solution)/shard_map/all_to_all | solution.py:429
  89.1 3.7 %shard_map.221 = (f32[256,768]{1,0:T(8,128)S(1)}, f32[256,256]{1,0:T(8,128)S(1)}, f32[256,128]{1,0:T(8,128)S(1)}) custom-call(bf16[256,1024]{1,0:T(8,128)(2,1)S(1)} %get-tuple-element.42.mixed, f32[256,256]{1,0:T(8,128)S(1)} %get-tuple-element.45.step, f32[256,128]{1,0:T(8,128)S(1)} %get-tuple-element.46.run, f32[128,256]{1,0:T(8,128)S(1)} %get-tuple-element.49.run_t, ...), custom_call_target="tpu_custom_call" | custom-call | tf_op jit(solution)/shard_map/pallas_call | solution.py:82
  95.0 1.9 %all-to-all-done.3 = bf16[16,8,768]{2,1,0:T(8,128)(2,1)S(1)} async-done(((bf16[16,8,768]{2,1,0:T(8,128)(2,1)}), bf16[16,8,768]{2,1,0:T(8,128)(2,1)S(1)}, u32[]{:S(2)}, u32[]{:S(2)}) %all-to-all-start.3) | async-done | bytes 196640 | tf_op jit(solution)/shard_map/all_to_all | solution.py:429
  103.8 4.6 %shard_map.223 = (f32[384,1024]{1,0:T(8,128)S(1)}, bf16[384,1024]{1,0:T(8,128)(2,1)}, f32[8,1024]{1,0:T(8,128)S(1)}, f32[256,1024]{1,0:T(8,128)S(1)}, bf16[256,1...) custom-call(s32[1]{0:T(128)} %bitcast.place, bf16[256,768]{1,0:T(8,128)(2,1)S(1)} %copy-done.3, ...), custom_call_target="tpu_custom_call" | custom-call | tf_op jit(solution)/shard_map/pallas_call | solution.py:82
  109.4 2.4 %add_convert_fusion.1 = bf16[384,768]{1,0:T(8,128)(2,1)} fusion(f32[384,768]{1,0:T(8,128)S(1)} %copy-done.7, bf16[384,768]{1,0:T(8,128)(2,1)} %collective-permute-done.3), kind=kLoop, calls=%fused_computation.3 | loop fusion | flops 884736 | bytes 2359296 | tf_op jit(solution)/shard_map/convert_element_type | solution.py:436
  111.9 4.0 %all-to-all-start.5 = ((bf16[8,48,768]{2,1,0:T(8,128)(2,1)}), bf16[8,48,768]{2,1,0:T(8,128)(2,1)S(1)}, u32[]{:S(2)}, u32[]{:S(2)}) async-start(bf16[8,48,768]{2,1,0:T(8,128)(2,1)} %bitcast.11), calls=%async_computation.5 | async-start | bytes 1179648 | tf_op jit(solution)/shard_map/all_to_all | solution.py:435
  115.9 2.6 %add_convert_fusion = bf16[384,1024]{1,0:T(8,128)(2,1)} fusion(f32[384,1024]{1,0:T(8,128)} %copy-done.4, bf16[384,1024]{1,0:T(8,128)(2,1)S(1)} %collective-permute-done.2), kind=kLoop, calls=%fused_computation.1 | loop fusion | flops 1179648 | bytes 3145728 | tf_op jit(solution)/shard_map/convert_element_type | solution.py:436
  118.4 13.7 %all-to-all-done.5 = bf16[8,48,768]{2,1,0:T(8,128)(2,1)S(1)} async-done(((bf16[8,48,768]{2,1,0:T(8,128)(2,1)}), bf16[8,48,768]{2,1,0:T(8,128)(2,1)S(1)}, u32[]{:S(2)}, u32[]{:S(2)}) %all-to-all-start.5) | async-done | bytes 589856 | tf_op jit(solution)/shard_map/all_to_all | solution.py:435
  132.9 4.3 %all-to-all-start.4 = ((bf16[8,48,1024]{2,1,0:T(8,128)(2,1)}), bf16[8,48,1024]{2,1,0:T(8,128)(2,1)}, u32[]{:S(2)}, u32[]{:S(2)}) async-start(bf16[8,48,1024]{2,1,0:T(8,128)(2,1)} %bitcast.10), calls=%async_computation.4 | async-start | bytes 1572864 | tf_op jit(solution)/shard_map/all_to_all | solution.py:435
  138.8 1.9 %collective-permute-start.5 = (f32[272,128]{1,0:T(8,128)S(1)}, f32[272,128]{1,0:T(8,128)S(1)}, u32[]{:S(2)}, u32[]{:S(2)}) collective-permute-start(f32[272,128]{1,0:T(8,128)S(1)} %add.28), channel_id=1, source_target_pairs={{0,2},{1,3},{2,0},{3,1},{4,6},{5,7},{6,4},{7,5},{8,10},{9,11},{10,... | collective-permute-start | bytes 417800 | tf_op jit(solution)/shard_map/ppermute | solution.py:25
  140.7 8.8 %collective-permute-done.5 = f32[272,128]{1,0:T(8,128)S(1)} collective-permute-done((f32[272,128]{1,0:T(8,128)S(1)}, f32[272,128]{1,0:T(8,128)S(1)}, u32[]{:S(2)}, u32[]{:S(2)}) %collective-permute-start.5) | collective-permute-done | bytes 139296 | tf_op jit(solution)/shard_map/ppermute | solution.py:25
  150.2 7.4 %collective-permute-done.6 = f32[272,128]{1,0:T(8,128)S(1)} collective-permute-done((f32[272,128]{1,0:T(8,128)S(1)}, f32[272,128]{1,0:T(8,128)S(1)}, u32[]{:S(2)}, u32[]{:S(2)}) %collective-permute-start.6) | collective-permute-done | bytes 139296 | tf_op jit(solution)/shard_map/ppermute | solution.py:25
  157.6 1.7 collective-permute-start.7
  159.3 1.6 collective-permute-start.1
  163.2 3.4 %collective-permute-done.7 = f32[272,128]{1,0:T(8,128)S(1)} collective-permute-done((f32[272,128]{1,0:T(8,128)S(1)}, f32[272,128]{1,0:T(8,128)S(1)}, u32[]{:S(2)}, u32[]{:S(2)}) %collective-permute-start.7) | collective-permute-done | bytes 139296 | tf_op jit(solution)/shard_map/ppermute | solution.py:25
  171.7 1.9 %convert_reduce_fusion = f32[48,1024]{1,0:T(8,128)} fusion(bf16[8,48,1024]{2,1,0:T(8,128)(2,1)} %all-to-all-done.4), kind=kLoop, calls=%fused_computation | loop fusion | flops 737280 | bytes 983040 | tf_op jit(solution)/shard_map/reduce_sum | solution.py:439
  (155 shorter events, 48.4 us)
Async XLA Ops:
  1.4 3.1 %collective-permute-start = (bf16[8,768]{1,0:T(8,128)(2,1)S(1)}, bf16[8,768]{1,0:T(8,128)(2,1)S(1)}, u32[]{:S(2)}, u32[]{:S(2)}) collective-permute-start(bf16[8,768]{1,0:T(8,128)(2,1)S(1)} %slice.34), channel_id=1, source_target_pairs={{1,0},{2,1},{3,2},{4,3},{5,4},{6,5},{7,6},{8,7},{9,8},{10,9},{11,1... | collective-permute-start | bytes 36872 | tf_op jit(solution)/shard_map/ppermute | solution.py:31
  7.5 13.6 %copy-start.47 = (f32[12]{0:T(128)S(1)}, f32[12]{0:T(128)}, u32[]{:S(2)}) copy-start(f32[12]{0:T(128)} %param.21) | copy-start | bytes 148
  7.5 13.7 %copy-start.45 = (bf16[768,16]{0,1:T(8,128)(2,1)S(1)}, bf16[768,16]{0,1:T(8,128)(2,1)}, u32[]{:S(2)}) copy-start(bf16[768,16]{0,1:T(8,128)(2,1)} %param.24) | copy-start | bytes 73732
  7.5 14.0 %copy-start.44 = (bf16[4096,16]{0,1:T(8,128)(2,1)S(1)}, bf16[4096,16]{0,1:T(8,128)(2,1)}, u32[]{:S(2)}) copy-start(bf16[4096,16]{0,1:T(8,128)(2,1)} %param.26) | copy-start | bytes 393220
  12.3 18.2 %all-to-all-start = ((bf16[16,8,896]{2,1,0:T(8,128)(2,1)}), bf16[16,8,896]{2,1,0:T(8,128)(2,1)S(1)}, u32[]{:S(2)}, u32[]{:S(2)}) async-start(bf16[16,8,896]{2,1,0:T(8,128)(2,1)} %bitcast.3), calls=%async_computation | async-start | bytes 458752 | tf_op jit(solution)/shard_map/all_to_all | solution.py:429
  21.3 14.4 %copy-start.48 = (s32[128]{0:T(128)S(1)}, s32[128]{0:T(128)}, u32[]{:S(2)}) copy-start(s32[128]{0:T(128)} %param.29) | copy-start | bytes 1540
  21.3 14.4 %copy-start.49 = (s32[128]{0:T(128)S(1)}, s32[128]{0:T(128)}, u32[]{:S(2)}) copy-start(s32[128]{0:T(128)} %param.28) | copy-start | bytes 1540
  21.3 14.4 %copy-start.50 = (s32[128,1]{0,1:T(1,128)S(1)}, s32[128,1]{0,1:T(1,128)}, u32[]{:S(2)}) copy-start(s32[128,1]{0,1:T(1,128)} %param.27) | copy-start | bytes 1540
  32.1 29.8 %all-to-all-start.1 = ((bf16[16,8,768]{2,1,0:T(8,128)(2,1)}), bf16[16,8,768]{2,1,0:T(8,128)(2,1)S(1)}, u32[]{:S(2)}, u32[]{:S(2)}) async-start(bf16[16,8,768]{2,1,0:T(8,128)(2,1)} %get-tuple-element.48), calls=%async_computation.1 | async-start | bytes 393216 | tf_op jit(solution)/shard_map/all_to_all | solution.py:429
  37.8 24.1 %copy-start.40 = (f32[1,128]{1,0:T(1,128)}, f32[1,128]{1,0:T(1,128)S(1)}, u32[]{:S(2)}) copy-start(f32[1,128]{1,0:T(1,128)S(1)} %get-tuple-element.65.own) | copy-start | bytes 1540
  71.1 12.6 %all-to-all-start.2 = ((bf16[16,8,768]{2,1,0:T(8,128)(2,1)}), bf16[16,8,768]{2,1,0:T(8,128)(2,1)S(1)}, u32[]{:S(2)}, u32[]{:S(2)}) async-start(bf16[16,8,768]{2,1,0:T(8,128)(2,1)} %bitcast.21), calls=%async_computation.2 | async-start | bytes 393216 | tf_op jit(solution)/shard_map/all_to_all | solution.py:429
  80.3 29.1 %collective-permute-start.3 = (bf16[384,768]{1,0:T(8,128)(2,1)}, bf16[384,768]{1,0:T(8,128)(2,1)}, u32[]{:S(2)}, u32[]{:S(2)}) collective-permute-start(bf16[384,768]{1,0:T(8,128)(2,1)} %get-tuple-element.72), channel_id=1, source_target_pairs={{0,1},{1,0},{2,3},{3,2},{4,5},{5,4},{6,7},{7,6},{8,9},{9,8},{10,11... | collective-permute-start | bytes 1769480 | tf_op jit(solution)/shard_map/ppermute | solution.py:25
  84.4 12.5 %all-to-all-start.3 = ((bf16[16,8,768]{2,1,0:T(8,128)(2,1)}), bf16[16,8,768]{2,1,0:T(8,128)(2,1)S(1)}, u32[]{:S(2)}, u32[]{:S(2)}) async-start(bf16[16,8,768]{2,1,0:T(8,128)(2,1)} %shard_map.220), calls=%async_computation.3 | async-start | bytes 393216 | tf_op jit(solution)/shard_map/all_to_all | solution.py:429
  109.4 6.4 %collective-permute-start.2 = (bf16[384,1024]{1,0:T(8,128)(2,1)}, bf16[384,1024]{1,0:T(8,128)(2,1)S(1)}, u32[]{:S(2)}, u32[]{:S(2)}) collective-permute-start(bf16[384,1024]{1,0:T(8,128)(2,1)} %get-tuple-element.70), channel_id=1, source_target_pairs={{0,1},{1,0},{2,3},{3,2},{4,5},{5,4},{6,7},{7,6},{8,9},{9,8},{10,11... | collective-permute-start | bytes 2359304 | tf_op jit(solution)/shard_map/ppermute | solution.py:25
  111.9 20.2 %all-to-all-start.5 = ((bf16[8,48,768]{2,1,0:T(8,128)(2,1)}), bf16[8,48,768]{2,1,0:T(8,128)(2,1)S(1)}, u32[]{:S(2)}, u32[]{:S(2)}) async-start(bf16[8,48,768]{2,1,0:T(8,128)(2,1)} %bitcast.11), calls=%async_computation.5 | async-start | bytes 1179648 | tf_op jit(solution)/shard_map/all_to_all | solution.py:435
  118.4 18.9 %copy-start.37 = (f32[40,768]{1,0:T(8,128)S(1)}, f32[40,768]{1,0:T(8,128)}, u32[]{:S(2)}) copy-start(f32[40,768]{1,0:T(8,128)} %copy-done.36) | copy-start | bytes 368644
  132.9 28.9 %copy-start.13 = (f32[256,1024]{1,0:T(8,128)S(1)}, f32[256,1024]{1,0:T(8,128)}, u32[]{:S(2)}) copy-start(f32[256,1024]{1,0:T(8,128)} %copy-done.12) | copy-start | bytes 3145732
  132.9 38.8 %all-to-all-start.4 = ((bf16[8,48,1024]{2,1,0:T(8,128)(2,1)}), bf16[8,48,1024]{2,1,0:T(8,128)(2,1)}, u32[]{:S(2)}, u32[]{:S(2)}) async-start(bf16[8,48,1024]{2,1,0:T(8,128)(2,1)} %bitcast.10), calls=%async_computation.4 | async-start | bytes 1572864 | tf_op jit(solution)/shard_map/all_to_all | solution.py:435
  137.2 24.5 %copy-start.1 = (bf16[768,1024]{1,0:T(8,128)(2,1)S(1)}, bf16[768,1024]{1,0:T(8,128)(2,1)}, u32[]{:S(2)}) copy-start(bf16[768,1024]{1,0:T(8,128)(2,1)} %w_in.3) | copy-start | bytes 4718596
  137.3 1.4 collective-permute-start.4
  138.8 10.7 %collective-permute-start.5 = (f32[272,128]{1,0:T(8,128)S(1)}, f32[272,128]{1,0:T(8,128)S(1)}, u32[]{:S(2)}, u32[]{:S(2)}) collective-permute-start(f32[272,128]{1,0:T(8,128)S(1)} %add.28), channel_id=1, source_target_pairs={{0,2},{1,3},{2,0},{3,1},{4,6},{5,7},{6,4},{7,5},{8,10},{9,11},{10,... | collective-permute-start | bytes 417800 | tf_op jit(solution)/shard_map/ppermute | solution.py:25
  149.5 8.0 %collective-permute-start.6 = (f32[272,128]{1,0:T(8,128)S(1)}, f32[272,128]{1,0:T(8,128)S(1)}, u32[]{:S(2)}, u32[]{:S(2)}) collective-permute-start(f32[272,128]{1,0:T(8,128)S(1)} %add.29), channel_id=1, source_target_pairs={{0,4},{1,5},{2,6},{3,7},{4,0},{5,1},{6,2},{7,3},{8,12},{9,13},{10,... | collective-permute-start | bytes 417800 | tf_op jit(solution)/shard_map/ppermute | solution.py:25
  157.6 9.0 %collective-permute-start.7 = (f32[272,128]{1,0:T(8,128)S(1)}, f32[272,128]{1,0:T(8,128)S(1)}, u32[]{:S(2)}, u32[]{:S(2)}) collective-permute-start(f32[272,128]{1,0:T(8,128)S(1)} %add.30), channel_id=1, source_target_pairs={{0,8},{1,9},{2,10},{3,11},{4,12},{5,13},{6,14},{7,15},{8,0},{9,1},... | collective-permute-start | bytes 417800 | tf_op jit(solution)/shard_map/ppermute | solution.py:25
  159.3 2.5 %collective-permute-start.1 = (f32[8,1024]{1,0:T(8,128)S(1)}, f32[8,1024]{1,0:T(8,128)S(1)}, u32[]{:S(2)}, u32[]{:S(2)}) collective-permute-start(f32[8,1024]{1,0:T(8,128)S(1)} %get-tuple-element.67), channel_id=1, source_target_pairs={{0,1},{1,2},{2,3},{3,4},{4,5},{5,6},{6,7},{7,8},{8,9},{9,10},{10,1... | collective-permute-start | bytes 98312 | tf_op jit(solution)/shard_map/ppermute | solution.py:31
  (41 other events, 112.1 us)

commit v2 on v1

v2 whole, which is shorter than its diff:
```python
import functools

import jax
import jax.numpy as jnp
from jax import lax
from jax.experimental import pallas as pl
from jax.experimental.pallas import tpu as pltpu
from jax.sharding import PartitionSpec as P

HEADS = 12
HDIM = 64
STATE = 128
LABELS = 16
LANES = 128
HALO = 8
TAGS = 48
FACTS = 40
EPSILON = 1e-05
FAR = -1e30

F32 = jnp.float32
BF16 = jnp.bfloat16


def partner(x, axis, apart):
    return lax.ppermute(x, axis, [(i, i ^ 1 << apart) for i in range(lax.axis_size(axis))])


def passed_along(x, axis, by):
    length = lax.axis_size(axis)
    pairs = [(i, i + by) for i in range(length) if 0 <= i + by < length]
    return lax.ppermute(x, axis, pairs)


def dot(a, b, left=1, right=0):
    return lax.dot_general(a, b, (((left,), (right,)), ((), ())), preferred_element_type=F32)


def pieces(x, count):
    parts = []
    for _ in range(count):
        part = x.astype(BF16)
        parts.append(part)
        x = x - part.astype(F32)
    return parts


def finer(a, x, count, left=1, right=0):
    return sum(dot(a, part, left, right) for part in pieces(x, count))


def iota(shape, axis):
    return lax.broadcasted_iota(jnp.int32, shape, axis)


def spread_heads(x):
    rows = x.shape[0]
    first = iota((rows, LANES), 1) < HDIM
    return jnp.concatenate(
        [
            jnp.where(
                first,
                jnp.broadcast_to(x[:, 2 * pair : 2 * pair + 1], (rows, LANES)),
                jnp.broadcast_to(x[:, 2 * pair + 1 : 2 * pair + 2], (rows, LANES)),
            )
            for pair in range(HEADS // 2)
        ],
        axis=1,
    )


def head_sums(x):
    width = x.shape[1]
    member = (iota((width, LANES), 0) // HDIM == iota((width, LANES), 1)).astype(BF16)
    return sum(dot(part, member) for part in pieces(x, 2))


class Fetched:
    def __init__(self, ref, copy):
        self.ref, self.copy, self.shape = ref, copy, ref.shape

    def ready(self):
        if self.copy is not None:
            self.copy.wait()
            self.copy = None
        return self.ref

    def __getitem__(self, at):
        return self.ready()[at]


class Result:
    def __init__(self, ref, copy):
        self.ref, self.copy, self.shape, self.sent = ref, copy, ref.shape, False

    def __getitem__(self, at):
        return self.ref[at]

    def __setitem__(self, at, value):
        self.ref[at] = value

    def send(self):
        self.copy.start()
        self.sent = True


class Kept:
    def __init__(self, ref):
        self.ref, self.shape = ref, ref.shape

    def __getitem__(self, at):
        return self.ref[at]

    def __setitem__(self, at, value):
        self.ref[at] = value

    def send(self):
        pass


def call(body, outs, *args, scratch=(), scalars=0, fetch=(), leave=(), after=(), wait=()):
    waits = len(after) + len(wait)
    fetch = sorted(fetch)

    def kernel(*refs):
        refs = list(refs)

        def take(count):
            taken = refs[:count]
            del refs[:count]
            return taken

        inputs = take(len(args))
        take(waits)
        results = take(len(outs))
        places, outputs, extra = take(len(fetch)), take(len(leave)), take(len(scratch))
        arrivals, departures = refs
        for i, (at, place) in enumerate(zip(fetch, places)):
            copy = pltpu.make_async_copy(inputs[at], place, arrivals.at[i])
            copy.start()
            inputs[at] = Fetched(place, copy)
        written = []
        for i, result in enumerate(results):
            if i in leave:
                at = leave.index(i)
                copy = pltpu.make_async_copy(outputs[at], result, departures.at[at])
                written.append(Result(outputs[at], copy))
            else:
                written.append(Kept(result))
        body(*inputs, *written, *extra)
        for at in fetch:
            inputs[at].ready()
        gone = [result for result in written if isinstance(result, Result)]
        for result in gone:
            if not result.sent:
                result.send()
        for result in gone:
            result.copy.wait()

    far, close = pltpu.HBM, pltpu.VMEM
    specs, given = [], []
    for i, arg in enumerate(args):
        if i < scalars:
            specs.append(pl.BlockSpec(memory_space=pltpu.SMEM))
            given.append(arg)
        else:
            space = far if i in fetch else close
            specs.append(pl.BlockSpec(memory_space=space))
            given.append(pltpu.with_memory_space_constraint(arg, space))
    for space, arrays in ((close, after), (far, wait)):
        for arg in arrays:
            specs.append(pl.BlockSpec(memory_space=space))
            given.append(pltpu.with_memory_space_constraint(arg, space))
    return pl.pallas_call(
        kernel,
        out_shape=[(far if i in leave else close)(*out) for i, out in enumerate(outs)],
        in_specs=specs,
        out_specs=[pl.BlockSpec(memory_space=far if i in leave else close) for i in range(len(outs))],
        scratch_shapes=[
            *(pltpu.VMEM(args[i].shape, args[i].dtype) for i in fetch),
            *(pltpu.VMEM(*outs[i]) for i in leave),
            *scratch,
            pltpu.SemaphoreType.DMA((max(len(fetch), 1),)),
            pltpu.SemaphoreType.DMA((max(len(leave), 1),)),
        ],
        compiler_params=pltpu.CompilerParams(vmem_limit_bytes=24 * 1024 * 1024),
    )(*given)


def widened(x):
    place = (iota((HEADS, LANES), 0) == iota((HEADS, LANES), 1)).astype(BF16)
    return sum(dot(part, place) for part in pieces(x, 3))


def teacher_kernel(slice_rows, rows, weights, dest, start, size, extra, own):
    count = rows.shape[0]
    row, lane = iota((count, count), 0), iota((count, count), 1)
    named = dest[...].astype(F32)
    facts = jnp.where(
        row == 0, named, jnp.where(row == 1, start[...].astype(F32), size[...].astype(F32))
    ).T
    spans = facts[:, 2:3]
    slot = jnp.sum(
        jnp.where((facts[:, 0:1] == named) & (row < lane), 1.0, 0.0), axis=0, keepdims=True
    ).astype(jnp.int32)
    logits = dot(rows[...], weights[...], 1, 1)
    top = jnp.max(logits, axis=1, keepdims=True)
    shifted = logits - top
    logp = shifted - jnp.log(jnp.sum(jnp.exp(shifted), axis=1, keepdims=True))
    prob = jnp.exp(logp)
    label, spot = iota((LABELS, LANES), 0), iota((LABELS, LANES), 1)
    total = jnp.zeros((STATE, LANES), F32)
    for group in range(2):
        base = TAGS + group * FACTS
        inside = sum(
            dot(part, (spot == label + base + i * LABELS).astype(BF16))
            for i, part in enumerate(pieces(prob, 2))
        )
        spare = base + 2 * LABELS
        inside = jnp.where(lane == spare, facts[:, 1:2], inside)
        inside = jnp.where(lane == spare + 1, spans, inside)
        inside = jnp.where(lane == spare + 2, 1.0, inside)
        where_to = dest[...] * slice_rows + slot - group * slice_rows
        fits = (slot >= group * slice_rows) & (slot < (group + 1) * slice_rows)
        chosen = (iota((STATE, count), 0) == jnp.where(fits, where_to, -1)).astype(F32)
        total = total + dot(chosen.astype(BF16), inside.astype(BF16))
    extra[...] = total.astype(BF16)
    gained = jnp.sum(prob * logp, axis=1, keepdims=True) * spans
    own[...] = jnp.where(lane[0:1] == 0, jnp.sum(gained, axis=0, keepdims=True), 0.0)


def target_kernel(arrived, target):
    length = target.shape[0]
    width = HEADS * HDIM
    count, rows = arrived.shape[0], arrived.shape[1]
    facts = arrived[:, :, width:].astype(F32).reshape(count * rows, LANES).astype(BF16)
    facts_f = facts.astype(F32)
    position = iota((count * rows, length), 1).astype(F32)
    total = jnp.zeros((length, LANES), F32)
    for group in range(2):
        base = TAGS + group * FACTS
        spare = base + 2 * LABELS
        start = facts_f[:, spare : spare + 1]
        stop = start + facts_f[:, spare + 1 : spare + 2]
        covered = jnp.where((position >= start) & (position < stop), 1.0, 0.0).astype(BF16)
        sums = dot(covered, facts, 0, 0)
        lane = iota(sums.shape, 1)
        high = pltpu.roll(sums, LANES - base, 1)
        low = pltpu.roll(sums, LANES - base - LABELS, 1)
        cover = pltpu.roll(sums, (LABELS - spare - 2) % LANES, 1)
        total = total + jnp.where(lane < LABELS, high + low, jnp.where(lane == LABELS, cover, 0.0))
    target[...] = total


def convolved(raw, conv_w, length):
    conv = conv_w[0:1, :] * raw[0:length, :]
    for tap in range(1, conv_w.shape[0]):
        conv = conv + conv_w[tap : tap + 1, :] * raw[pl.ds(tap, length), :]
    return conv


def front_kernel(
    edge, hidden, w_dt, dt_bias, a_log, w_in, conv_w, extra,
    message, mixed_o, raw_o, step_o, run_o, run_t, raw,
):
    length = hidden.shape[0]
    wide = (iota((LANES, HEADS), 0) == iota((LANES, HEADS), 1)).astype(BF16)
    w_dt_wide = dot(wide, w_dt[...]).astype(BF16)
    before = dot(hidden[...], w_dt_wide, 1, 1) + widened(dt_bias[...])
    step = jnp.maximum(before, 0.0) + jnp.log1p(jnp.exp(-jnp.abs(before)))
    step = jnp.where(iota((length, LANES), 1) < HEADS, step, 0.0)
    log_decay = -step * jnp.exp(widened(a_log[...]))
    later = (iota((length, length), 1) >= iota((length, length), 0)).astype(BF16)
    run = finer(later, log_decay, 3)
    step_o[:, 0:LANES] = step
    step_o[:, LANES:] = before
    run_o[...] = run
    run_t[...] = run.T
    for result in (step_o, run_o, run_t):
        result.send()
    weights = w_in[...]
    raw_o[0:length, :] = dot(hidden[...], weights).astype(BF16)
    raw_o[length:, :] = dot(edge[...], weights).astype(BF16)
    raw_o.send()
    raw[...] = raw_o[...].astype(F32)
    conv = convolved(raw, conv_w, length)
    mixed = (conv / (1.0 + jnp.exp(-conv))).astype(BF16)
    mixed_o[...] = mixed
    mixed_o.send()
    width = HEADS * HDIM
    total = run[0:1, :]
    weighted = mixed[:, :width].astype(F32) * spread_heads(step * jnp.exp(total - run))
    state = dot(mixed[:, width : width + STATE], weighted.astype(BF16), 0, 0)
    message[:, :width] = state.astype(BF16)
    high, middle, low = (part.astype(F32) for part in pieces(total, 3))
    tags = high + pltpu.roll(middle, 16, 1) + pltpu.roll(low, 32, 1)
    message[:, width:] = (extra[...].astype(F32) + tags).astype(BF16)


def decay_blocks(run, run_t, head, half):
    top = run[0:half, head : head + 1] - run_t[head : head + 1, :]
    low = run[half:, head : head + 1] - run_t[head : head + 1, half:]
    top_seen = iota(top.shape, 1) >= iota(top.shape, 0)
    low_seen = iota(low.shape, 1) >= iota(low.shape, 0)
    return jnp.exp(jnp.where(top_seen, top, FAR)), jnp.exp(jnp.where(low_seen, low, FAR))


def local_kernel(mixed, step, run, run_t, local):
    length = mixed.shape[0]
    half = length // 2
    width = HEADS * HDIM
    in_map = mixed[:, width : width + STATE]
    out_map = mixed[:, width + STATE :]
    top_scores = dot(out_map[0:half], in_map, 1, 1)
    low_scores = dot(out_map[half:], in_map[half:], 1, 1)
    weighted = (mixed[:, :width].astype(F32) * spread_heads(step[:, 0:LANES])).astype(BF16)
    first = iota((half, LANES), 1) < HDIM
    for pair in range(HEADS // 2):
        lanes = slice(pair * LANES, (pair + 1) * LANES)
        own = weighted[:, lanes]
        tops, lows = [], []
        for head in (2 * pair, 2 * pair + 1):
            top, low = decay_blocks(run, run_t, head, half)
            tops.append(dot((top * top_scores).astype(BF16), own))
            lows.append(dot((low * low_scores).astype(BF16), own[half:]))
        local[0:half, lanes] = jnp.where(first, tops[0], tops[1])
        local[half:, lanes] = jnp.where(first, lows[0], lows[1])


def states_kernel(arrived, onward, decay):
    count = arrived.shape[0]
    width = HEADS * HDIM
    rows = arrived.shape[1]
    keep = iota((rows, LANES), 1) < HEADS
    state = jnp.zeros((rows, width), F32)
    for source in range(count - 1, -1, -1):
        onward[source] = state.astype(BF16)
        tags = arrived[source, :, width:].astype(F32)
        total = tags + pltpu.roll(tags, LANES - 16, 1) + pltpu.roll(tags, LANES - 32, 1)
        factor = spread_heads(jnp.exp(jnp.where(keep, total, 0.0)))
        decay[source] = factor
        state = arrived[source, :, :width].astype(F32) + factor * state


def state_grads_kernel(arrived, decay, onward):
    count = arrived.shape[0]
    state = jnp.zeros(arrived.shape[1:], F32)
    for source in range(count):
        onward[source] = state.astype(BF16)
        state = arrived[source].astype(F32) + decay[source] * state


def middle_kernel(
    state, mixed, run, local, d_skip, gains, w_out, w_cls, target,
    back_state, grad_scanned, normed_o, branch_o, back_branch_o, logits_o, run_grad, small,
):
    length = mixed.shape[0]
    width = HEADS * HDIM
    values = mixed[:, :width].astype(F32)
    out_map = mixed[:, width + STATE :]
    reach = spread_heads(jnp.exp(run[...]))
    carried = dot(out_map, state[...]) * reach
    gain = gains[...].reshape(1, width)
    skip = spread_heads(d_skip[...])
    scanned = local[...] + carried + skip * values
    scale = lax.rsqrt(jnp.mean(scanned * scanned, axis=1, keepdims=True) + EPSILON)
    plain = scanned * scale
    normed = (plain * gain).astype(BF16)
    normed_o[...] = normed
    normed_o.send()
    branch = dot(normed, w_out[...]).astype(BF16)
    branch_o[...] = branch
    branch_o.send()
    label = iota((length, LANES), 1) < LABELS
    wide = (iota((LANES, LABELS), 0) == iota((LANES, LABELS), 1)).astype(BF16)
    weights = dot(wide, w_cls[...]).astype(BF16)
    logits = jnp.where(label, dot(branch, weights, 1, 1), FAR)
    shifted = logits - jnp.max(logits, axis=1, keepdims=True)
    raised = jnp.exp(shifted)
    whole = jnp.sum(raised, axis=1, keepdims=True)
    logp = shifted - jnp.log(whole)
    wanted = target[...]
    cover = wanted[:, LABELS : LABELS + 1]
    back_logits = jnp.where(label, cover * (raised / whole) - wanted, 0.0)
    logits_o[...] = back_logits
    logits_o.send()
    lost = jnp.sum(jnp.where(label, wanted * logp, 0.0), axis=0, keepdims=True)
    back_branch = sum(dot(part, weights) for part in pieces(back_logits, 2)).astype(BF16)
    back_branch_o[...] = back_branch
    back_branch_o.send()
    back_normed = dot(back_branch, w_out[...], 1, 1)
    back_plain = back_normed * gain
    along = jnp.mean(back_plain * plain, axis=1, keepdims=True)
    back = scale * (back_plain - plain * along)
    grad_scanned[...] = back
    grad_scanned.send()
    back_state[...] = dot(out_map, (back * reach).astype(BF16), 0, 0).astype(BF16)
    back_state.send()
    run_grad[...] = head_sums(back * carried)
    small[0:1, :] = jnp.sum(back_normed * plain, axis=0, keepdims=True)
    small[1:2, :] = jnp.sum(back * values, axis=0, keepdims=True)
    small[2:3, :] = jnp.zeros((1, width), F32)
    small[2:3, 0:LANES] = lost
    small[3:, :] = jnp.zeros((5, width), F32)


def halves(full, keep, send, odd, blocks):
    size = full.shape[0] // blocks
    for side in (0, 1):

        @pl.when(odd == side)
        def _():
            for block in range(blocks // 2):
                at = slice(block * size, (block + 1) * size)
                mine = (2 * block + side) * size
                other = (2 * block + 1 - side) * size
                keep[at, :] = full[mine : mine + size, :].astype(BF16)
                send[at, :] = full[other : other + size, :].astype(BF16)


def outward_kernel(blocks, place, normed, back_branch, branch, back_logits, keep, send, cls, full):
    full[...] = dot(normed[...], back_branch[...], 0, 0)
    halves(full, keep, send, place[0] % 2, blocks)
    keep.send()
    send.send()
    parts = pieces(back_logits[...], 2)
    cls[...] = sum(dot(part, branch[...], 0, 0) for part in parts)[0:LABELS]


def local_back_kernel(
    mixed, step, run, run_t, grad_scanned, d_skip, state, carried_grad,
    values_grad, maps, run_grad, step_grad, weighted_grad,
):
    length = mixed.shape[0]
    half = length // 2
    width = HEADS * HDIM
    in_map = mixed[:, width : width + STATE]
    out_map = mixed[:, width + STATE :]
    top_scores = dot(out_map[0:half], in_map, 1, 1)
    low_scores = dot(out_map[half:], in_map[half:], 1, 1)
    values = mixed[:, :width].astype(F32)
    steps = spread_heads(step[:, 0:LANES])
    weighted = (values * steps).astype(BF16)
    lane = iota((length, LANES), 1)
    back_top = jnp.zeros((half, length), F32)
    back_low = jnp.zeros((half, half), F32)
    rows_top = jnp.zeros((half, LANES), F32)
    rows_low = jnp.zeros((half, LANES), F32)
    columns = jnp.zeros((length, LANES), F32)
    columns_low = jnp.zeros((half, LANES), F32)
    for pair in range(HEADS // 2):
        lanes = slice(pair * LANES, (pair + 1) * LANES)
        own = weighted[:, lanes]
        back_f = grad_scanned[:, lanes]
        back = back_f.astype(BF16)
        tops, lows = [], []
        for side in (0, 1):
            head = 2 * pair + side
            top, low = decay_blocks(run, run_t, head, half)
            mine = jnp.where((lane >= HDIM) == (side == 1), back_f, 0.0).astype(BF16)
            mix_top = (top * top_scores).astype(BF16)
            mix_low = (low * low_scores).astype(BF16)
            tops.append(dot(mix_top, back[0:half], 0, 0))
            lows.append(dot(mix_low, back[half:], 0, 0))
            grad_top = top * dot(mine[0:half], own, 1, 1)
            grad_low = low * dot(mine[half:], own[half:], 1, 1)
            back_top = back_top + grad_top
            back_low = back_low + grad_low
            part_top = (grad_top * top_scores).astype(BF16)
            part_low = (grad_low * low_scores).astype(BF16)
            marker = (lane == head).astype(F32).astype(BF16)
            rows_top = rows_top + dot(part_top, marker)
            rows_low = rows_low + dot(part_low, marker[half:])
            columns = columns + dot(part_top, marker[0:half], 0, 0)
            columns_low = columns_low + dot(part_low, marker[half:], 0, 0)
        weighted_grad[0:half, lanes] = jnp.where(lane[0:half] < HDIM, tops[0][0:half], tops[1][0:half])
        weighted_grad[half:, lanes] = jnp.where(
            lane[half:] < HDIM, tops[0][half:] + lows[0], tops[1][half:] + lows[1]
        )
    back_top = back_top.astype(BF16)
    back_low = back_low.astype(BF16)
    values_grad[...] = weighted_grad[...] * steps + spread_heads(d_skip[...]) * grad_scanned[...]
    values_grad.send()
    step_grad[...] = head_sums(weighted_grad[...] * values)
    scaled = (grad_scanned[...] * spread_heads(jnp.exp(run[...]))).astype(BF16)
    from_state = dot(scaled, state[...], 1, 1)
    maps[0:half, STATE:] = dot(back_top, in_map) + from_state[0:half]
    maps[half:, STATE:] = dot(back_low, in_map[half:]) + from_state[half:]
    in_grad = dot(back_top, out_map[0:half], 0, 0)
    maps[0:half, 0:STATE] = in_grad[0:half]
    maps[half:, 0:STATE] = in_grad[half:] + dot(back_low, out_map[half:], 0, 0)
    run_grad[0:half, :] = carried_grad[0:half, :] + rows_top - columns[0:half]
    run_grad[half:, :] = carried_grad[half:, :] + rows_low - columns[half:] - columns_low


def last_kernel(
    blocks, place, state_grad, edge, run, mixed, step, state, run_grad, step_local, a_log, conv_w,
    values_local, maps, raw_b, hidden, small, cls, own,
    keep, send, rim, back_raw_o, step_grad_o, conv_sums, sums, full, padded, raw,
):
    length = mixed.shape[0]
    taps = conv_w.shape[0]
    width = HEADS * HDIM
    total = run[0:1, :]
    tail = spread_heads(jnp.exp(total - run[...]))
    values = mixed[:, :width].astype(F32)
    in_map = mixed[:, width : width + STATE]
    incoming = state_grad[...]
    reached = dot(in_map, incoming) * tail
    steps = spread_heads(step[:, 0:LANES])
    weighted = values * steps
    ended = head_sums(reached * weighted)
    in_grad = dot((weighted * tail).astype(BF16), incoming, 1, 1)
    product = jnp.sum(incoming.astype(F32) * state[...].astype(F32), axis=0, keepdims=True)
    total_grad = jnp.exp(total) * head_sums(jnp.broadcast_to(product, (8, width)))[0:1]
    row, column = iota((length, length), 0), iota((length, length), 1)
    decay_grad = (
        finer((column <= row).astype(BF16), run_grad[...], 3)
        + finer((column > row).astype(BF16), ended, 3)
        + total_grad
    )
    rate = jnp.exp(widened(a_log[...]))
    step_grad = step_local[...] + head_sums(reached * values) - rate * decay_grad
    before = step[:, LANES:]
    step_grad = jnp.where(
        iota((length, LANES), 1) < HEADS, step_grad / (1.0 + jnp.exp(-before)), 0.0
    )
    step_grad_b = step_grad.astype(BF16)
    step_grad_o[...] = step_grad_b
    raw[...] = raw_b[...].astype(F32)
    padded[0:HALO, :] = jnp.zeros((HALO, padded.shape[1]), F32)
    padded[HALO + length :, :] = jnp.zeros((HALO, padded.shape[1]), F32)
    inner = convolved(raw, conv_w, length)
    gate = 1.0 / (1.0 + jnp.exp(-inner))
    slope = gate * (1.0 + inner * (1.0 - gate))
    middle = slice(HALO, HALO + length)
    padded[middle, 0:width] = (values_local[...] + reached * steps) * slope[:, 0:width]
    padded[middle, width : width + STATE] = (maps[:, 0:STATE] + in_grad) * slope[
        :, width : width + STATE
    ]
    padded[middle, width + STATE :] = maps[:, STATE:] * slope[:, width + STATE :]
    rim[...] = padded[length : length + HALO, :]
    rim.send()
    back_raw = jnp.zeros((length + HALO, padded.shape[1]), F32)
    for tap in range(taps):
        back_raw = back_raw + conv_w[tap : tap + 1, :] * padded[pl.ds(HALO - tap, length + HALO), :]
    back_raw_o[...] = back_raw[0:length]
    back_raw_o.send()
    full[...] = dot(hidden[...], back_raw[0:length].astype(BF16), 0, 0) + dot(
        edge[...], back_raw[length:].astype(BF16), 0, 0
    )
    halves(full, keep, send, place[0] % 2, blocks)
    keep.send()
    send.send()
    back_conv = padded[middle, :]
    for tap in range(taps):
        conv_sums[tap : tap + 1, :] = jnp.sum(
            back_conv * raw[pl.ds(tap, length), :], axis=0, keepdims=True
        )
    dt_grad = dot(step_grad_b, hidden[...], 0, 0)
    sums[0:LABELS, :] = dt_grad[0:LABELS]
    sums[LABELS : 2 * LABELS, :] = cls[...]
    base = 2 * LABELS
    sums[base:, :] = jnp.zeros((8, width), F32)
    sums[base : base + 1, :] = small[0:1, :]
    sums[base + 1 : base + 2, 0:LANES] = jnp.sum(step_grad, axis=0, keepdims=True)
    log_decay = -step[:, 0:LANES] * rate
    sums[base + 2 : base + 3, 0:LANES] = jnp.sum(decay_grad * log_decay, axis=0, keepdims=True)
    sums[base + 3 : base + 4, 0:LANES] = head_sums(jnp.broadcast_to(small[1:2, :], (8, width)))[0:1]
    sums[base + 4 : base + 5, 0:LANES] = own[...] - small[2:3, 0:LANES]


def hidden_kernel(rim, back_raw, conv_w, step_grad, w_dt, w_in, out, joined, edge):
    taps = conv_w.shape[0]
    joined[...] = back_raw[...]
    edge[0:HALO, :] = rim[...]
    edge[HALO:, :] = jnp.zeros((HALO, edge.shape[1]), F32)
    head = joined[0:HALO, :]
    for tap in range(taps):
        head = head + conv_w[tap : tap + 1, :] * edge[pl.ds(HALO - tap, HALO), :]
    joined[0:HALO, :] = head
    wide = (iota((LANES, HEADS), 0) == iota((LANES, HEADS), 1)).astype(BF16)
    w_dt_wide = dot(wide, w_dt[...]).astype(BF16)
    out[...] = (
        dot(joined[...].astype(BF16), w_in[...], 1, 1) + dot(step_grad[...], w_dt_wide)
    ).astype(BF16)


def swapped(x, axis="seq"):
    return lax.all_to_all(x, axis, split_axis=0, concat_axis=0, tiled=True)


def pair_kernel(keep, received, both):
    half = keep.shape[0] // 2
    both[0:half, :] = (keep[0:half, :].astype(F32) + received[0:half, :].astype(F32)).astype(BF16)
    both[half:, :] = (keep[half:, :].astype(F32) + received[half:, :].astype(F32)).astype(BF16)


def paired(keep, send, fetch):
    received = partner(send, "seq", 0)
    return call(pair_kernel, [(keep.shape, BF16)], keep, received, fetch=fetch, leave=(0,))[0]


def scattered(both, devices):
    groups = [[i for i in range(devices) if i % 2 == side] for side in (0, 1)]
    parts = lax.all_to_all(
        both, "seq", split_axis=0, concat_axis=0, axis_index_groups=groups, tiled=True
    )
    size = both.shape[0] // (devices // 2)
    return jnp.sum(parts.reshape(devices // 2, size, both.shape[1]).astype(F32), axis=0)


def per_device(
    hidden_in, w_in, w_dt, dt_bias, a_log, conv_w, d_skip, norm_gain, w_out, w_cls,
    teacher_rows, w_teacher, row_dest, row_start, row_len,
):
    devices = lax.axis_size("seq")
    length = hidden_in.shape[0]
    width = HEADS * HDIM
    channels = w_in.shape[1]
    slice_rows = STATE // devices
    row_count = teacher_rows.shape[0]
    place = lax.axis_index("seq").astype(jnp.int32).reshape(1)

    edge = passed_along(hidden_in[:HALO], "seq", -1)
    extra, own = call(
        functools.partial(teacher_kernel, slice_rows),
        [((STATE, LANES), BF16), ((1, LANES), F32)],
        teacher_rows, w_teacher.T, row_dest.reshape(1, row_count),
        row_start.reshape(1, row_count), row_len.reshape(1, row_count),
        fetch=range(5), leave=(1,),
    )
    w_dt_t = w_dt.T
    a_log_row = a_log.reshape(1, HEADS)
    skip_row = d_skip.reshape(1, HEADS)
    message, mixed, raw, step, run, run_t = call(
        front_kernel,
        [
            ((STATE, width + LANES), BF16),
            ((length, channels), BF16),
            ((length + HALO, channels), BF16),
            ((length, 2 * LANES), F32),
            ((length, LANES), F32),
            ((LANES, length), F32),
        ],
        edge, hidden_in, w_dt_t, dt_bias.reshape(1, HEADS), a_log_row, w_in, conv_w, extra,
        scratch=[pltpu.VMEM((length + HALO, channels), F32)], fetch=range(1, 7), leave=(0, 2),
    )
    arrived = swapped(message).reshape(devices, slice_rows, width + LANES)
    (local,) = call(local_kernel, [((length, width), F32)], mixed, step, run, run_t)
    onward, decay = call(
        states_kernel,
        [((devices, slice_rows, width), BF16), ((devices, slice_rows, width), F32)],
        arrived,
        leave=(0,),
        after=[local],
    )
    state = swapped(onward.reshape(STATE, width))
    (target,) = call(target_kernel, [((length, LANES), F32)], arrived)

    back_state, grad_scanned, normed, branch, back_branch, back_logits, carried_grad, small = call(
        middle_kernel,
        [
            ((STATE, width), BF16),
            ((length, width), F32),
            ((length, width), BF16),
            ((length, width), BF16),
            ((length, width), BF16),
            ((length, LANES), F32),
            ((length, LANES), F32),
            ((8, width), F32),
        ],
        state, mixed, run, local, skip_row, norm_gain, w_out, w_cls.T, target,
        fetch=(4, 5, 6, 7), leave=(0, 2, 3, 4, 5, 7),
    )
    back_arrived = swapped(back_state).reshape(devices, slice_rows, width)
    values_local, maps, run_grad, step_local = call(
        local_back_kernel,
        [
            ((length, width), F32),
            ((length, 2 * STATE), F32),
            ((length, LANES), F32),
            ((length, LANES), F32),
        ],
        mixed, step, run, run_t, grad_scanned, skip_row, state, carried_grad,
        scratch=[pltpu.VMEM((length, width), F32)], fetch=(5,),
    )
    (back_onward,) = call(
        state_grads_kernel,
        [((devices, slice_rows, width), BF16)],
        back_arrived, decay,
        leave=(0,), after=[run_grad],
    )
    state_grad = swapped(back_onward.reshape(STATE, width))
    keep_out, send_out, cls = call(
        functools.partial(outward_kernel, devices),
        [((width // 2, width), BF16), ((width // 2, width), BF16), ((LABELS, width), F32)],
        place, normed, back_branch, branch, back_logits,
        scratch=[pltpu.VMEM((width, width), F32)], scalars=1, fetch=range(1, 5), leave=(0, 1, 2), after=[run_grad],
    )
    both_out = paired(keep_out, send_out, (0, 1))
    grad_w_out = scattered(both_out, devices)

    keep_in, send_in, rim, back_raw, step_grad, conv_sums, sums = call(
        functools.partial(last_kernel, devices),
        [
            ((width // 2, channels), BF16),
            ((width // 2, channels), BF16),
            ((HALO, channels), F32),
            ((length, channels), F32),
            ((length, LANES), BF16),
            (conv_w.shape, F32),
            ((2 * LABELS + 8, width), F32),
        ],
        place, state_grad, edge, run, mixed, step, state, run_grad, step_local, a_log_row, conv_w,
        values_local, maps, raw, hidden_in, small, cls, own,
        scratch=[
            pltpu.VMEM((width, channels), F32),
            pltpu.VMEM((length + 2 * HALO, channels), F32),
            pltpu.VMEM((length + HALO, channels), F32),
        ],
        scalars=1, fetch=(9, 10, 13, 14, 15, 16, 17), leave=(1, 2, 3, 4), wait=[both_out],
    )
    grad_w_in = scattered(paired(keep_in, send_in, ()), devices)
    (grad_hidden,) = call(
        hidden_kernel,
        [((length, w_in.shape[0]), BF16)],
        passed_along(rim, "seq", 1), back_raw, conv_w, step_grad, w_dt_t, w_in,
        scratch=[pltpu.VMEM((length, channels), F32), pltpu.VMEM((2 * HALO, channels), F32)],
        fetch=range(1, 6), leave=(0,),
    )
    flat = jnp.concatenate([sums.reshape(-1, LANES), conv_sums.reshape(-1, LANES)], axis=0)
    for bit in range(devices.bit_length() - 1):
        if bit == 2:
            flat, grad_hidden = lax.optimization_barrier((flat, grad_hidden))
        flat = flat + partner(flat, "seq", bit)
    split = sums.size // LANES
    sums = flat[:split].reshape(sums.shape)
    base = 2 * LABELS
    loss = jnp.sum(sums[base + 4, 0:LANES]).reshape(1) / (row_count * devices)
    return (
        grad_hidden,
        grad_w_in,
        grad_w_out,
        flat[split:].reshape(conv_w.shape),
        sums[0:HEADS].T,
        sums[base + 1 : base + 4, 0:HEADS],
        sums[base],
        sums[LABELS : 2 * LABELS].T,
        loss,
    )


def solution(mesh):
    rows = P(("grp", "seq"), None)
    placed = (rows,) + (P(),) * 9 + (rows, P(), rows, P(("grp", "seq")), P(("grp", "seq")))
    part = P("grp", None)
    return jax.shard_map(
        per_device,
        mesh=mesh,
        in_specs=placed,
        out_specs=(rows, rows, rows, part, part, part, P("grp"), part, P("grp")),
        check_vma=False,
    )
```

time: 176 us -> 143 us (0.81)
  local copies, waits for them, and re-layouts: 33.6 us -> 6.42 us
  blocking collectives: 22.2 us -> 0 us
  Pallas kernels: 22.5 us -> 39.3 us
  starting transfers between devices: 35.5 us -> 48.9 us
  other arithmetic: 9.12 us -> 2.2 us
  waiting for transfers between devices: 48.9 us -> 42.4 us
    unnamed x106 -> x23, local copies, waits for them, and re-layouts: 29.5 us -> 2.59 us
    all_gather x1 -> x0, blocking collectives: 22.2 us -> none  [per_device(): everyone = lax.all_gather(packed, 'seq', axis=0, tiled=True)]
    pallas_call x11 -> x13, Pallas kernels: 22.5 us -> 39.3 us  [call(): pl.pallas_call(kernel, out_shape=[(far if i in leave else close)(*out) fo...]
    ppermute x6, starting transfers between devices: 4.73 us -> 17.5 us  [partner(): lax.ppermute(x, axis, [(i, i ^ 1 << apart) for i in range(lax.axis_size(a...]
    all_to_all x2, waiting for transfers between devices: 13.7 us -> 3.87 us  [scattered(): lax.all_to_all(both, 'seq', split_axis=0, concat_axis=0, axis_index_group...]
    all_to_all x4, waiting for transfers between devices: 13.5 us -> 23.3 us  [swapped(): return lax.all_to_all(x, axis, split_axis=0, concat_axis=0, tiled=True)]
    ppermute x6, waiting for transfers between devices: 20.8 us -> 14.4 us  [partner(): lax.ppermute(x, axis, [(i, i ^ 1 << apart) for i in range(lax.axis_size(a...]
    convert_element_type x3 -> x0, other arithmetic: 5.07 us -> none  [the longest x2 5 us: scattered(): both.astype(BF16)]
  transfers between devices with their start and end apart: 14 -> 14, of which waited for: 10 -> 10; matrix products, arithmetic and copies ran while one was open for 7% -> 3% of each run, Pallas kernels for 8% -> 20%
where the time goes in v2:
time: 143 us; the launch traced here: 142 us
  starting transfers between devices  48.9 us (34%)
  waiting for transfers between devices  42.4 us (30%)
  Pallas kernels  39.3 us (27%)
  local copies, waits for them, and re-layouts  6.42 us (4%)
  between operations  2.82 us (2%)
  other arithmetic  2.2 us (2%)
    pallas_call x13, Pallas kernels, call(): pl.pallas_call(kernel, out_shape=[(far if i in leave else close)(*out) fo...  39.3 us
    all_to_all x4, waiting for transfers between devices, swapped(): return lax.all_to_all(x, axis, split_axis=0, concat_axis=0, tiled=True)  23.3 us
    all_to_all x4, starting transfers between devices, swapped(): return lax.all_to_all(x, axis, split_axis=0, concat_axis=0, tiled=True)  21.2 us
    ppermute x6, starting transfers between devices, partner(): lax.ppermute(x, axis, [(i, i ^ 1 << apart) for i in range(lax.axis_size(a...  17.5 us
    ppermute x6, waiting for transfers between devices, partner(): lax.ppermute(x, axis, [(i, i ^ 1 << apart) for i in range(lax.axis_size(a...  14.4 us
    all_to_all x2, starting transfers between devices, scattered(): lax.all_to_all(both, 'seq', split_axis=0, concat_axis=0, axis_index_group...  7.16 us
    all_to_all x2, waiting for transfers between devices, scattered(): lax.all_to_all(both, 'seq', split_axis=0, concat_axis=0, axis_index_group...  3.87 us
    ppermute x2, starting transfers between devices, passed_along(): return lax.ppermute(x, axis, pairs)  3.04 us
  transfers between devices with their start and end apart: 14, of which 10 were waited for; matrix products, arithmetic and copies ran while one was open for 3% of the time, Pallas kernels for 20%

profile of v2, /device:TPU:0, one launch (start us, length us, event | category | flops | bytes accessed | tf_op | source)
XLA Modules:
  0.0 141.9 jit_solution(16876287443323614606)
XLA Ops:
  2.6 2.7 %shard_map.214 = (bf16[128,128]{1,0:T(8,128)(2,1)S(1)}, f32[1,128]{1,0:T(1,128)}) custom-call(bf16[128,4096]{1,0:T(8,128)(2,1)} %refs_0_.1, bf16[16,4096]{1,0:T(8,128)(2,1)} %bitcast.29, s32[1,128]{1,0:T(1,128)} %bitcast.39, s32[1,128]{1,0:T(1,128)} %bitcast.40, s32[1,128]{1,0:T(1,128)} %bitcast.41), custom_call_target="tpu_custom_call" | custom-call | tf_op jit(solution)/shard_map/pallas_call | solution.py:174
  5.3 4.6 %shard_map.215 = (bf16[128,896]{1,0:T(8,128)(2,1)}, bf16[256,1024]{1,0:T(8,128)(2,1)S(1)}, bf16[264,1024]{1,0:T(8,128)(2,1)}, f32[256,256]{1,0:T(8,128)S(1)}, f3...) custom-call(bf16[8,768]{1,0:T(8,128)(2,1)S(1)} %collective-permute-done.refs_0_.refs_2_, bf16[256,768]{1,0:T(8,128)(2,1)} %refs_14_.1, ...), custom_call_target="tpu_custom_call" | custom-call | tf_op jit(solution)/shard_map/pallas_call | solution.py:174
  9.9 8.1 %all-to-all-start = ((bf16[16,8,896]{2,1,0:T(8,128)(2,1)}), bf16[16,8,896]{2,1,0:T(8,128)(2,1)S(1)}, u32[]{:S(2)}, u32[]{:S(2)}) async-start(bf16[16,8,896]{2,1,0:T(8,128)(2,1)} %bitcast.27), calls=%async_computation | async-start | bytes 458752 | tf_op jit(solution)/shard_map/all_to_all | solution.py:590
  19.3 8.2 %all-to-all-done.refs_0_ = bf16[16,8,896]{2,1,0:T(8,128)(2,1)S(1)} async-done(((bf16[16,8,896]{2,1,0:T(8,128)(2,1)}), bf16[16,8,896]{2,1,0:T(8,128)(2,1)S(1)}, u32[]{:S(2)}, u32[]{:S(2)}) %all-to-all-start) | async-done | bytes 229408 | tf_op jit(solution)/shard_map/all_to_all | solution.py:590
  29.9 3.5 %all-to-all-start.1 = ((bf16[16,8,768]{2,1,0:T(8,128)(2,1)}), bf16[16,8,768]{2,1,0:T(8,128)(2,1)S(1)}, u32[]{:S(2)}, u32[]{:S(2)}) async-start(bf16[16,8,768]{2,1,0:T(8,128)(2,1)} %get-tuple-element.49), calls=%async_computation.1 | async-start | bytes 393216 | tf_op jit(solution)/shard_map/all_to_all | solution.py:590
  34.1 8.3 %all-to-all-done.1 = bf16[16,8,768]{2,1,0:T(8,128)(2,1)S(1)} async-done(((bf16[16,8,768]{2,1,0:T(8,128)(2,1)}), bf16[16,8,768]{2,1,0:T(8,128)(2,1)S(1)}, u32[]{:S(2)}, u32[]{:S(2)}) %all-to-all-start.1) | async-done | bytes 196640 | tf_op jit(solution)/shard_map/all_to_all | solution.py:590
  42.4 5.0 %shard_map.219 = (bf16[128,768]{1,0:T(8,128)(2,1)}, f32[256,768]{1,0:T(8,128)S(1)}, bf16[256,768]{1,0:T(8,128)(2,1)}, bf16[256,768]{1,0:T(8,128)(2,1)}, bf16[256...) custom-call(bf16[128,768]{1,0:T(8,128)(2,1)S(1)} %bitcast.21, ...), custom_call_target="tpu_custom_call" | custom-call | tf_op jit(solution)/shard_map/pallas_call | solution.py:174
  47.4 3.7 %all-to-all-start.2 = ((bf16[16,8,768]{2,1,0:T(8,128)(2,1)}), bf16[16,8,768]{2,1,0:T(8,128)(2,1)S(1)}, u32[]{:S(2)}, u32[]{:S(2)}) async-start(bf16[16,8,768]{2,1,0:T(8,128)(2,1)} %bitcast.28), calls=%async_computation.2 | async-start | bytes 393216 | tf_op jit(solution)/shard_map/all_to_all | solution.py:590
  52.9 4.7 %shard_map.220 = (f32[256,768]{1,0:T(8,128)S(1)}, f32[256,256]{1,0:T(8,128)S(1)}, f32[256,128]{1,0:T(8,128)S(1)}, f32[256,128]{1,0:T(8,128)S(1)}) custom-call(bf16[256,1024]{1,0:T(8,128)(2,1)S(1)} %get-tuple-element.45.refs_0_.refs_1_.refs_4_, f32[256,256]{1,0:T(8,128)S(1)} %get-tuple-element.46.refs_1_.refs_5_, ...), custom_call_target="tpu_custom_call" | custom-call | tf_op jit(solution)/shard_map/pallas_call | solution.py:174
  57.6 3.0 %shard_map.222 = (bf16[384,768]{1,0:T(8,128)(2,1)}, bf16[384,768]{1,0:T(8,128)(2,1)}, f32[16,768]{1,0:T(8,128)}) custom-call(s32[1]{0:T(128)} %bitcast.refs_0_, bf16[256,768]{1,0:T(8,128)(2,1)} %get-tuple-element.60.refs_1_, bf16[256,768]{1,0:T(8,128)(2,1)} %get-tuple-element.61.refs_2_, bf16[256,768]{1,0:T(8,128)(2,1)} %get-tuple-element.62.refs_3_, ...), custom_call_target="tpu_custom_call" | custom-call | tf_op jit(solution)/shard_map/pallas_call | solution.py:174
  61.7 5.8 %all-to-all-start.3 = ((bf16[16,8,768]{2,1,0:T(8,128)(2,1)}), bf16[16,8,768]{2,1,0:T(8,128)(2,1)S(1)}, u32[]{:S(2)}, u32[]{:S(2)}) async-start(bf16[16,8,768]{2,1,0:T(8,128)(2,1)} %shard_map.221), calls=%async_computation.3 | async-start | bytes 393216 | tf_op jit(solution)/shard_map/all_to_all | solution.py:590
  67.5 2.3 %shard_map.223.refs_18_ = bf16[384,768]{1,0:T(8,128)(2,1)} custom-call(bf16[384,768]{1,0:T(8,128)(2,1)} %get-tuple-element.66.refs_0_, bf16[384,768]{1,0:T(8,128)(2,1)} %collective-permute-done.1.refs_1_), custom_call_target="tpu_custom_call" | custom-call | tf_op jit(solution)/shard_map/pallas_call | solution.py:174
  69.8 6.7 %all-to-all-done.3 = bf16[16,8,768]{2,1,0:T(8,128)(2,1)S(1)} async-done(((bf16[16,8,768]{2,1,0:T(8,128)(2,1)}), bf16[16,8,768]{2,1,0:T(8,128)(2,1)S(1)}, u32[]{:S(2)}, u32[]{:S(2)}) %all-to-all-start.3) | async-done | bytes 196640 | tf_op jit(solution)/shard_map/all_to_all | solution.py:590
  76.5 3.5 %all-to-all-start.5 = ((bf16[8,48,768]{2,1,0:T(8,128)(2,1)}), bf16[8,48,768]{2,1,0:T(8,128)(2,1)S(1)}, u32[]{:S(2)}, u32[]{:S(2)}) async-start(bf16[8,48,768]{2,1,0:T(8,128)(2,1)} %bitcast.25), calls=%async_computation.5 | async-start | bytes 1179648 | tf_op jit(solution)/shard_map/all_to_all | solution.py:606
  80.1 8.4 %shard_map.224 = (bf16[384,1024]{1,0:T(8,128)(2,1)S(1)}, bf16[384,1024]{1,0:T(8,128)(2,1)}, f32[8,1024]{1,0:T(8,128)}, f32[256,1024]{1,0:T(8,128)}, bf16[256,128...) custom-call(s32[1]{0:T(128)} %bitcast.refs_0_, bf16[128,768]{1,0:T(8,128)(2,1)S(1)} %bitcast.24, ...), custom_call_target="tpu_custom_call" | custom-call | tf_op jit(solution)/shard_map/pallas_call | solution.py:174
  88.6 2.5 %collective-permute-done.5.refs_1_ = bf16[384,1024]{1,0:T(8,128)(2,1)S(1)} collective-permute-done((bf16[384,1024]{1,0:T(8,128)(2,1)}, bf16[384,1024]{1,0:T(8,128)(2,1)S(1)}, u32[]{:S(2)}, u32[]{:S(2)}) %collective-permute-start.5) | collective-permute-done | bytes 786464 | tf_op jit(solution)/shard_map/ppermute | solution.py:26
  92.2 3.9 %all-to-all-done.5 = bf16[8,48,768]{2,1,0:T(8,128)(2,1)S(1)} async-done(((bf16[8,48,768]{2,1,0:T(8,128)(2,1)}), bf16[8,48,768]{2,1,0:T(8,128)(2,1)S(1)}, u32[]{:S(2)}, u32[]{:S(2)}) %all-to-all-start.5) | async-done | bytes 589856 | tf_op jit(solution)/shard_map/all_to_all | solution.py:606
  96.0 3.6 %all-to-all-start.4 = ((bf16[8,48,1024]{2,1,0:T(8,128)(2,1)}), bf16[8,48,1024]{2,1,0:T(8,128)(2,1)S(1)}, u32[]{:S(2)}, u32[]{:S(2)}) async-start(bf16[8,48,1024]{2,1,0:T(8,128)(2,1)} %bitcast.26), calls=%async_computation.4 | async-start | bytes 1572864 | tf_op jit(solution)/shard_map/all_to_all | solution.py:606
  105.9 3.4 %shard_map.225 = bf16[256,768]{1,0:T(8,128)(2,1)} custom-call(f32[8,1024]{1,0:T(8,128)S(1)} %collective-permute-done.4.refs_0_, f32[256,1024]{1,0:T(8,128)} %get-tuple-element.71.refs_1_, f32[4,1024]{1,0:T(4,128)} %refs_2_.1, bf16[256,128]{1,0:T(8,128)(2,1)} %get-tuple-element.72.refs_3_, bf16[12,768]{1,0:T(8,128)(2,1)} %bitcast.31, bf16[768,1024]{1,0:T(8,128)(2,1)} %refs_5_.5), custom_call_target="tpu_custom_call" | custom-call | tf_op jit(solution)/shard_map/pallas_call | solution.py:174
  109.2 2.4 %collective-permute-done.3 = f32[272,128]{1,0:T(8,128)S(1)} collective-permute-done((f32[272,128]{1,0:T(8,128)S(1)}, f32[272,128]{1,0:T(8,128)S(1)}, u32[]{:S(2)}, u32[]{:S(2)}) %collective-permute-start.3) | collective-permute-done | bytes 139296 | tf_op jit(solution)/shard_map/ppermute | solution.py:26
  111.7 7.6 %collective-permute-start.6 = (f32[272,128]{1,0:T(8,128)S(1)}, f32[272,128]{1,0:T(8,128)S(1)}, u32[]{:S(2)}, u32[]{:S(2)}) collective-permute-start(f32[272,128]{1,0:T(8,128)S(1)} %add.13), channel_id=1, source_target_pairs={{0,4},{1,5},{2,6},{3,7},{4,0},{5,1},{6,2},{7,3},{8,12},{9,13},{10,... | collective-permute-start | bytes 417800 | tf_op jit(solution)/shard_map/ppermute | solution.py:26
  119.3 3.7 %collective-permute-done.6 = f32[272,128]{1,0:T(8,128)S(1)} collective-permute-done((f32[272,128]{1,0:T(8,128)S(1)}, f32[272,128]{1,0:T(8,128)S(1)}, u32[]{:S(2)}, u32[]{:S(2)}) %collective-permute-start.6) | collective-permute-done | bytes 139296 | tf_op jit(solution)/shard_map/ppermute | solution.py:26
  123.0 7.4 %collective-permute-start.7 = (f32[272,128]{1,0:T(8,128)S(1)}, f32[272,128]{1,0:T(8,128)S(1)}, u32[]{:S(2)}, u32[]{:S(2)}) collective-permute-start(f32[272,128]{1,0:T(8,128)S(1)} %add.14), channel_id=1, source_target_pairs={{0,8},{1,9},{2,10},{3,11},{4,12},{5,13},{6,14},{7,15},{8,0},{9,1},... | collective-permute-start | bytes 417800 | tf_op jit(solution)/shard_map/ppermute | solution.py:26
  130.4 4.4 %collective-permute-done.7 = f32[272,128]{1,0:T(8,128)S(1)} collective-permute-done((f32[272,128]{1,0:T(8,128)S(1)}, f32[272,128]{1,0:T(8,128)S(1)}, u32[]{:S(2)}, u32[]{:S(2)}) %collective-permute-start.7) | collective-permute-done | bytes 139296 | tf_op jit(solution)/shard_map/ppermute | solution.py:26
  (61 shorter events, 21.6 us)
Async XLA Ops:
  1.4 4.0 %collective-permute-start = (bf16[8,768]{1,0:T(8,128)(2,1)S(1)}, bf16[8,768]{1,0:T(8,128)(2,1)S(1)}, u32[]{:S(2)}, u32[]{:S(2)}) collective-permute-start(bf16[8,768]{1,0:T(8,128)(2,1)S(1)} %slice.34), channel_id=1, source_target_pairs={{1,0},{2,1},{3,2},{4,3},{5,4},{6,5},{7,6},{8,7},{9,8},{10,9},{11,1... | collective-permute-start | bytes 36872 | tf_op jit(solution)/shard_map/ppermute | solution.py:32
  9.9 19.3 %copy-start = (f32[128,256]{1,0:T(8,128)}, f32[128,256]{1,0:T(8,128)S(1)}, u32[]{:S(2)}) copy-start(f32[128,256]{1,0:T(8,128)S(1)} %get-tuple-element.48.refs_3_) | copy-start | bytes 393220
  9.9 17.7 %all-to-all-start = ((bf16[16,8,896]{2,1,0:T(8,128)(2,1)}), bf16[16,8,896]{2,1,0:T(8,128)(2,1)S(1)}, u32[]{:S(2)}, u32[]{:S(2)}) async-start(bf16[16,8,896]{2,1,0:T(8,128)(2,1)} %bitcast.27), calls=%async_computation | async-start | bytes 458752 | tf_op jit(solution)/shard_map/all_to_all | solution.py:590
  29.9 12.5 %all-to-all-start.1 = ((bf16[16,8,768]{2,1,0:T(8,128)(2,1)}), bf16[16,8,768]{2,1,0:T(8,128)(2,1)S(1)}, u32[]{:S(2)}, u32[]{:S(2)}) async-start(bf16[16,8,768]{2,1,0:T(8,128)(2,1)} %get-tuple-element.49), calls=%async_computation.1 | async-start | bytes 393216 | tf_op jit(solution)/shard_map/all_to_all | solution.py:590
  47.4 3.7 %copy-start.8 = (f32[256,128]{1,0:T(8,128)}, f32[256,128]{1,0:T(8,128)S(1)}, u32[]{:S(2)}) copy-start(f32[256,128]{1,0:T(8,128)S(1)} %get-tuple-element.53.refs_7_) | copy-start | bytes 393220
  47.4 13.5 %all-to-all-start.2 = ((bf16[16,8,768]{2,1,0:T(8,128)(2,1)}), bf16[16,8,768]{2,1,0:T(8,128)(2,1)S(1)}, u32[]{:S(2)}, u32[]{:S(2)}) async-start(bf16[16,8,768]{2,1,0:T(8,128)(2,1)} %bitcast.28), calls=%async_computation.2 | async-start | bytes 393216 | tf_op jit(solution)/shard_map/all_to_all | solution.py:590
  51.1 0.9 copy-start.1
  52.0 0.9 copy-start.9
  52.9 8.0 %copy-start.3 = (f32[16,8,768]{2,1,0:T(8,128)S(1)}, f32[16,8,768]{2,1,0:T(8,128)}, u32[]{:S(2)}) copy-start(f32[16,8,768]{2,1,0:T(8,128)} %copy-done.2) | copy-start | bytes 1179652
  57.6 3.0 %copy-start.4 = (f32[256,256]{1,0:T(8,128)}, f32[256,256]{1,0:T(8,128)S(1)}, u32[]{:S(2)}) copy-start(f32[256,256]{1,0:T(8,128)S(1)} %get-tuple-element.57.refs_12_) | copy-start | bytes 786436
  57.6 3.0 %copy-start.6 = (f32[256,128]{1,0:T(8,128)}, f32[256,128]{1,0:T(8,128)S(1)}, u32[]{:S(2)}) copy-start(f32[256,128]{1,0:T(8,128)S(1)} %get-tuple-element.55.refs_8_) | copy-start | bytes 393220
  60.7 6.8 %collective-permute-start.1 = (bf16[384,768]{1,0:T(8,128)(2,1)}, bf16[384,768]{1,0:T(8,128)(2,1)}, u32[]{:S(2)}, u32[]{:S(2)}) collective-permute-start(bf16[384,768]{1,0:T(8,128)(2,1)} %get-tuple-element.67), channel_id=1, source_target_pairs={{0,1},{1,0},{2,3},{3,2},{4,5},{5,4},{6,7},{7,6},{8,9},{9,8},{10,11... | collective-permute-start | bytes 1769480 | tf_op jit(solution)/shard_map/ppermute | solution.py:26
  61.7 14.8 %all-to-all-start.3 = ((bf16[16,8,768]{2,1,0:T(8,128)(2,1)}), bf16[16,8,768]{2,1,0:T(8,128)(2,1)S(1)}, u32[]{:S(2)}, u32[]{:S(2)}) async-start(bf16[16,8,768]{2,1,0:T(8,128)(2,1)} %shard_map.221), calls=%async_computation.3 | async-start | bytes 393216 | tf_op jit(solution)/shard_map/all_to_all | solution.py:590
  67.5 12.5 %copy-start.5 = (f32[256,256]{1,0:T(8,128)S(1)}, f32[256,256]{1,0:T(8,128)}, u32[]{:S(2)}) copy-start(f32[256,256]{1,0:T(8,128)} %copy-done.4) | copy-start | bytes 786436
  67.5 12.5 %copy-start.7 = (f32[256,128]{1,0:T(8,128)S(1)}, f32[256,128]{1,0:T(8,128)}, u32[]{:S(2)}) copy-start(f32[256,128]{1,0:T(8,128)} %copy-done.6) | copy-start | bytes 393220
  76.5 19.5 %all-to-all-start.5 = ((bf16[8,48,768]{2,1,0:T(8,128)(2,1)}), bf16[8,48,768]{2,1,0:T(8,128)(2,1)S(1)}, u32[]{:S(2)}, u32[]{:S(2)}) async-start(bf16[8,48,768]{2,1,0:T(8,128)(2,1)} %bitcast.25), calls=%async_computation.5 | async-start | bytes 1179648 | tf_op jit(solution)/shard_map/all_to_all | solution.py:606
  88.5 2.6 %collective-permute-start.5 = (bf16[384,1024]{1,0:T(8,128)(2,1)}, bf16[384,1024]{1,0:T(8,128)(2,1)S(1)}, u32[]{:S(2)}, u32[]{:S(2)}) collective-permute-start(bf16[384,1024]{1,0:T(8,128)(2,1)} %get-tuple-element.75), channel_id=1, source_target_pairs={{0,1},{1,0},{2,3},{3,2},{4,5},{5,4},{6,7},{7,6},{8,9},{9,8},{10,11... | collective-permute-start | bytes 2359304 | tf_op jit(solution)/shard_map/ppermute | solution.py:26
  92.2 11.1 %copy-start.10 = (f32[8,1024]{1,0:T(8,128)S(1)}, f32[8,1024]{1,0:T(8,128)}, u32[]{:S(2)}) copy-start(f32[8,1024]{1,0:T(8,128)} %get-tuple-element.70) | copy-start | bytes 98308
  96.0 44.0 %all-to-all-start.4 = ((bf16[8,48,1024]{2,1,0:T(8,128)(2,1)}), bf16[8,48,1024]{2,1,0:T(8,128)(2,1)S(1)}, u32[]{:S(2)}, u32[]{:S(2)}) async-start(bf16[8,48,1024]{2,1,0:T(8,128)(2,1)} %bitcast.26), calls=%async_computation.4 | async-start | bytes 1572864 | tf_op jit(solution)/shard_map/all_to_all | solution.py:606
  99.7 1.4 %collective-permute-start.2 = (f32[272,128]{1,0:T(8,128)S(1)}, f32[272,128]{1,0:T(8,128)S(1)}, u32[]{:S(2)}, u32[]{:S(2)}) collective-permute-start(f32[272,128]{1,0:T(8,128)S(1)} %constant_dynamic-update-slice_fusion), channel_id=1, source_target_pairs={{0,1},{1,0},{2,3},{3,2},{4,5},{5,4},{6,7},{7,6},{8,9},{9,8},{10,11... | collective-permute-start | bytes 417800 | tf_op jit(solution)/shard_map/ppermute | solution.py:26
  101.2 10.5 %collective-permute-start.3 = (f32[272,128]{1,0:T(8,128)S(1)}, f32[272,128]{1,0:T(8,128)S(1)}, u32[]{:S(2)}, u32[]{:S(2)}) collective-permute-start(f32[272,128]{1,0:T(8,128)S(1)} %add.12), channel_id=1, source_target_pairs={{0,2},{1,3},{2,0},{3,1},{4,6},{5,7},{6,4},{7,5},{8,10},{9,11},{10,... | collective-permute-start | bytes 417800 | tf_op jit(solution)/shard_map/ppermute | solution.py:26
  103.2 2.6 %collective-permute-start.4 = (f32[8,1024]{1,0:T(8,128)S(1)}, f32[8,1024]{1,0:T(8,128)S(1)}, u32[]{:S(2)}, u32[]{:S(2)}) collective-permute-start(f32[8,1024]{1,0:T(8,128)S(1)} %copy-done.10), channel_id=1, source_target_pairs={{0,1},{1,2},{2,3},{3,4},{4,5},{5,6},{6,7},{7,8},{8,9},{9,10},{10,1... | collective-permute-start | bytes 98312 | tf_op jit(solution)/shard_map/ppermute | solution.py:32
  111.7 11.3 %collective-permute-start.6 = (f32[272,128]{1,0:T(8,128)S(1)}, f32[272,128]{1,0:T(8,128)S(1)}, u32[]{:S(2)}, u32[]{:S(2)}) collective-permute-start(f32[272,128]{1,0:T(8,128)S(1)} %add.13), channel_id=1, source_target_pairs={{0,4},{1,5},{2,6},{3,7},{4,0},{5,1},{6,2},{7,3},{8,12},{9,13},{10,... | collective-permute-start | bytes 417800 | tf_op jit(solution)/shard_map/ppermute | solution.py:26
  123.0 11.9 %collective-permute-start.7 = (f32[272,128]{1,0:T(8,128)S(1)}, f32[272,128]{1,0:T(8,128)S(1)}, u32[]{:S(2)}, u32[]{:S(2)}) collective-permute-start(f32[272,128]{1,0:T(8,128)S(1)} %add.14), channel_id=1, source_target_pairs={{0,8},{1,9},{2,10},{3,11},{4,12},{5,13},{6,14},{7,15},{8,0},{9,1},... | collective-permute-start | bytes 417800 | tf_op jit(solution)/shard_map/ppermute | solution.py:26
  (1 other events, 0.8 us)

commit v3 on v2

--- a/solution.py
+++ b/solution.py
@@ -337,17 +337,18 @@
         onward[source] = state.astype(BF16)
         tags = arrived[source, :, width:].astype(F32)
         total = tags + pltpu.roll(tags, LANES - 16, 1) + pltpu.roll(tags, LANES - 32, 1)
-        factor = spread_heads(jnp.exp(jnp.where(keep, total, 0.0)))
+        factor = jnp.exp(jnp.where(keep, total, 0.0))
         decay[source] = factor
-        state = arrived[source, :, :width].astype(F32) + factor * state
-
-
-def state_grads_kernel(arrived, decay, onward):
-    count = arrived.shape[0]
+        state = arrived[source, :, :width].astype(F32) + spread_heads(factor) * state
+
+
+def state_grads_kernel(arrived, decay, early, onward):
+    count, rows, width = arrived.shape
     state = jnp.zeros(arrived.shape[1:], F32)
     for source in range(count):
-        onward[source] = state.astype(BF16)
-        state = arrived[source].astype(F32) + decay[source] * state
+        onward[source, :, :width] = state.astype(BF16)
+        onward[source, :, width:] = early[source * rows : (source + 1) * rows, :].astype(BF16)
+        state = arrived[source].astype(F32) + spread_heads(decay[source]) * state
 
 
 def middle_kernel(
@@ -418,17 +419,26 @@
                 send[at, :] = full[other : other + size, :].astype(BF16)
 
 
-def outward_kernel(blocks, place, normed, back_branch, branch, back_logits, keep, send, cls, full):
+def outward_kernel(
+    blocks, place, normed, back_branch, branch, back_logits, small, keep, send, early, full
+):
     full[...] = dot(normed[...], back_branch[...], 0, 0)
     halves(full, keep, send, place[0] % 2, blocks)
     keep.send()
     send.send()
     parts = pieces(back_logits[...], 2)
-    cls[...] = sum(dot(part, branch[...], 0, 0) for part in parts)[0:LABELS]
+    cls = sum(dot(part, branch[...], 0, 0) for part in parts)[0:LABELS]
+    count = cls.shape[1] // LANES
+    early[count * LABELS :, :] = jnp.zeros((early.shape[0] - count * LABELS, LANES), F32)
+    for block in range(count):
+        lanes = slice(block * LANES, (block + 1) * LANES)
+        early[block * LABELS : (block + 1) * LABELS, :] = cls[:, lanes]
+        at = count * LABELS + block
+        early[at : at + 1, :] = small[0:1, lanes]
 
 
 def local_back_kernel(
-    mixed, step, run, run_t, grad_scanned, d_skip, state, carried_grad,
+    mixed, step, run, grad_scanned, d_skip, state, carried_grad,
     values_grad, maps, run_grad, step_grad, weighted_grad,
 ):
     length = mixed.shape[0]
@@ -441,6 +451,7 @@
     values = mixed[:, :width].astype(F32)
     steps = spread_heads(step[:, 0:LANES])
     weighted = (values * steps).astype(BF16)
+    run_t = run[...].T
     lane = iota((length, LANES), 1)
     back_top = jnp.zeros((half, length), F32)
     back_low = jnp.zeros((half, half), F32)
@@ -495,8 +506,8 @@
 
 def last_kernel(
     blocks, place, state_grad, edge, run, mixed, step, state, run_grad, step_local, a_log, conv_w,
-    values_local, maps, raw_b, hidden, small, cls, own,
-    keep, send, rim, back_raw_o, step_grad_o, conv_sums, sums, full, padded, raw,
+    values_local, maps, raw_b, hidden, small, own,
+    keep, send, rim, back_raw_o, step_grad_o, late, full, padded, raw,
 ):
     length = mixed.shape[0]
     taps = conv_w.shape[0]
@@ -505,7 +516,7 @@
     tail = spread_heads(jnp.exp(total - run[...]))
     values = mixed[:, :width].astype(F32)
     in_map = mixed[:, width : width + STATE]
-    incoming = state_grad[...]
+    incoming = state_grad[:, :width]
     reached = dot(in_map, incoming) * tail
     steps = spread_heads(step[:, 0:LANES])
     weighted = values * steps
@@ -553,21 +564,29 @@
     keep.send()
     send.send()
     back_conv = padded[middle, :]
+    spare = late.shape[0] - taps
     for tap in range(taps):
-        conv_sums[tap : tap + 1, :] = jnp.sum(
+        late[spare + tap : spare + tap + 1, :] = jnp.sum(
             back_conv * raw[pl.ds(tap, length), :], axis=0, keepdims=True
         )
-    dt_grad = dot(step_grad_b, hidden[...], 0, 0)
-    sums[0:LABELS, :] = dt_grad[0:LABELS]
-    sums[LABELS : 2 * LABELS, :] = cls[...]
-    base = 2 * LABELS
-    sums[base:, :] = jnp.zeros((8, width), F32)
-    sums[base : base + 1, :] = small[0:1, :]
-    sums[base + 1 : base + 2, 0:LANES] = jnp.sum(step_grad, axis=0, keepdims=True)
+    late[0:HEADS, 0:width] = dot(step_grad_b, hidden[...], 0, 0)[0:HEADS]
+    late[0:HEADS, width:] = jnp.zeros((HEADS, late.shape[1] - width), F32)
     log_decay = -step[:, 0:LANES] * rate
-    sums[base + 2 : base + 3, 0:LANES] = jnp.sum(decay_grad * log_decay, axis=0, keepdims=True)
-    sums[base + 3 : base + 4, 0:LANES] = head_sums(jnp.broadcast_to(small[1:2, :], (8, width)))[0:1]
-    sums[base + 4 : base + 5, 0:LANES] = own[...] - small[2:3, 0:LANES]
+    facts = jnp.sum(step_grad, axis=0, keepdims=True)
+    facts = facts + pltpu.roll(jnp.sum(decay_grad * log_decay, axis=0, keepdims=True), 16, 1)
+    skips = head_sums(jnp.broadcast_to(small[1:2, :], (8, width)))[0:1]
+    lost = jnp.sum(own[...] - small[2:3, 0:LANES], axis=1, keepdims=True)
+    lane = iota((1, LANES), 1)
+    facts = facts + pltpu.roll(skips, 32, 1) + jnp.where(lane == 48, lost, 0.0)
+    late[HEADS - 4 : HEADS - 3, width : width + LANES] = facts
+    shares = state_grad[:, width:].astype(F32)
+    rows = shares.shape[0] // blocks
+    share = sum(shares[source * rows : (source + 1) * rows] for source in range(blocks))
+    for side in (0, 1):
+
+        @pl.when(place[0] % 2 == side)
+        def _():
+            late[0:rows, width + side * LANES : width + (side + 1) * LANES] = share
 
 
 def hidden_kernel(rim, back_raw, conv_w, step_grad, w_dt, w_in, out, joined, edge):
@@ -601,13 +620,57 @@
     return call(pair_kernel, [(keep.shape, BF16)], keep, received, fetch=fetch, leave=(0,))[0]
 
 
-def scattered(both, devices):
+def joint_kernel(blocks, keep, received, late, late_received, both):
+    size = keep.shape[0] // blocks
+    rows, width = late.shape[0], HEADS * HDIM
+    sums = late[...] + late_received[...]
+    facts = sums[:, width : width + LANES]
+    rest = pltpu.roll(facts - facts.astype(BF16).astype(F32), 1, 0)
+    row = iota(facts.shape, 0)
+    facts = jnp.where(row == HEADS - 3, rest, facts)
+    sums = jnp.concatenate([sums[:, :width], facts, sums[:, width + LANES :]], axis=1).astype(BF16)
+    for block in range(blocks):
+        base, at = block * (size + rows), slice(block * size, (block + 1) * size)
+        both[base : base + size, :] = (
+            keep[at, :].astype(F32) + received[at, :].astype(F32)
+        ).astype(BF16)
+        both[base + size : base + size + rows, :] = sums
+
+
+def joint_sums_kernel(
+    share, rows_in_all, parts, grad_w_in, grad_conv, grad_dt_t, grad_heads, gain, cls_t, loss, early
+):
+    total = parts[0].astype(F32)
+    for chip in range(1, parts.shape[0]):
+        total = total + parts[chip].astype(F32)
+    size, taps, width = grad_w_in.shape[0], grad_conv.shape[0], HEADS * HDIM
+    grad_w_in[...] = total[0:size]
+    grad_conv[...] = total[size + HEADS : size + HEADS + taps]
+    grad_dt_t[...] = total[size : size + HEADS, 0:width]
+    at = size + HEADS - 4
+    facts = total[at : at + 1, width : width + LANES] + total[at + 1 : at + 2, width : width + LANES]
+    for row in range(3):
+        moved = pltpu.roll(facts, (LANES - 16 * row) % LANES, 1) if row else facts
+        grad_heads[row : row + 1, :] = moved[:, 0:HEADS]
+    loss[...] = pltpu.roll(facts, LANES - 48, 1)[:, 0:1] / rows_in_all
+    for chip in range(parts.shape[0]):
+        for side in (0, 1):
+            base = (2 * chip + side) * share
+            lanes = slice(width + side * LANES, width + (side + 1) * LANES)
+            early[base : base + share, :] = parts[chip][size : size + share, lanes].astype(F32)
+    count = width // LANES
+    for block in range(count):
+        lanes = slice(block * LANES, (block + 1) * LANES)
+        cls_t[:, lanes] = early[block * LABELS : (block + 1) * LABELS, :]
+        gain[:, lanes] = early[count * LABELS + block : count * LABELS + block + 1, :]
+
+
+def exchanged(both, devices):
     groups = [[i for i in range(devices) if i % 2 == side] for side in (0, 1)]
     parts = lax.all_to_all(
         both, "seq", split_axis=0, concat_axis=0, axis_index_groups=groups, tiled=True
     )
-    size = both.shape[0] // (devices // 2)
-    return jnp.sum(parts.reshape(devices // 2, size, both.shape[1]).astype(F32), axis=0)
+    return parts.reshape(devices // 2, -1, both.shape[1])
 
 
 def per_device(
@@ -650,7 +713,7 @@
     (local,) = call(local_kernel, [((length, width), F32)], mixed, step, run, run_t)
     onward, decay = call(
         states_kernel,
-        [((devices, slice_rows, width), BF16), ((devices, slice_rows, width), F32)],
+        [((devices, slice_rows, width), BF16), ((devices, slice_rows, LANES), F32)],
         arrived,
         leave=(0,),
         after=[local],
@@ -671,7 +734,7 @@
             ((8, width), F32),
         ],
         state, mixed, run, local, skip_row, norm_gain, w_out, w_cls.T, target,
-        fetch=(4, 5, 6, 7), leave=(0, 2, 3, 4, 5, 7),
+        fetch=(4, 5, 6, 7), leave=(0, 2, 3, 4, 5, 6, 7),
     )
     back_arrived = swapped(back_state).reshape(devices, slice_rows, width)
     values_local, maps, run_grad, step_local = call(
@@ -682,26 +745,27 @@
             ((length, LANES), F32),
             ((length, LANES), F32),
         ],
-        mixed, step, run, run_t, grad_scanned, skip_row, state, carried_grad,
-        scratch=[pltpu.VMEM((length, width), F32)], fetch=(5,),
+        mixed, step, run, grad_scanned, skip_row, state, carried_grad,
+        scratch=[pltpu.VMEM((length, width), F32)], fetch=(4, 6), leave=(1, 3),
+    )
+    keep_out, send_out, early = call(
+        functools.partial(outward_kernel, devices),
+        [((width // 2, width), BF16), ((width // 2, width), BF16), ((STATE, LANES), F32)],
+        place, normed, back_branch, branch, back_logits, small,
+        scratch=[pltpu.VMEM((width, width), F32)],
+        scalars=1, fetch=range(1, 6), leave=(0, 1), after=[run_grad],
     )
     (back_onward,) = call(
         state_grads_kernel,
-        [((devices, slice_rows, width), BF16)],
-        back_arrived, decay,
-        leave=(0,), after=[run_grad],
-    )
-    state_grad = swapped(back_onward.reshape(STATE, width))
-    keep_out, send_out, cls = call(
-        functools.partial(outward_kernel, devices),
-        [((width // 2, width), BF16), ((width // 2, width), BF16), ((LABELS, width), F32)],
-        place, normed, back_branch, branch, back_logits,
-        scratch=[pltpu.VMEM((width, width), F32)], scalars=1, fetch=range(1, 5), leave=(0, 1, 2), after=[run_grad],
-    )
-    both_out = paired(keep_out, send_out, (0, 1))
-    grad_w_out = scattered(both_out, devices)
-
-    keep_in, send_in, rim, back_raw, step_grad, conv_sums, sums = call(
+        [((devices, slice_rows, width + LANES), BF16)],
+        back_arrived, decay, early,
+        leave=(0,),
+    )
+    state_grad = swapped(back_onward.reshape(STATE, width + LANES))
+    both_out = paired(keep_out, send_out, (0,))
+    grad_w_out = jnp.sum(exchanged(both_out, devices).astype(F32), axis=0)
+
+    keep_in, send_in, rim, back_raw, step_grad, late = call(
         functools.partial(last_kernel, devices),
         [
             ((width // 2, channels), BF16),
@@ -709,19 +773,25 @@
             ((HALO, channels), F32),
             ((length, channels), F32),
             ((length, LANES), BF16),
-            (conv_w.shape, F32),
-            ((2 * LABELS + 8, width), F32),
+            ((HEADS + conv_w.shape[0], channels), F32),
         ],
         place, state_grad, edge, run, mixed, step, state, run_grad, step_local, a_log_row, conv_w,
-        values_local, maps, raw, hidden_in, small, cls, own,
+        values_local, maps, raw, hidden_in, small, own,
         scratch=[
             pltpu.VMEM((width, channels), F32),
             pltpu.VMEM((length + 2 * HALO, channels), F32),
             pltpu.VMEM((length + HALO, channels), F32),
         ],
-        scalars=1, fetch=(9, 10, 13, 14, 15, 16, 17), leave=(1, 2, 3, 4), wait=[both_out],
-    )
-    grad_w_in = scattered(paired(keep_in, send_in, ()), devices)
+        scalars=1, fetch=(8, 9, 10, 12, 13, 14, 15, 16), leave=(1, 2, 3, 4), wait=[both_out],
+    )
+    chips = devices // 2
+    (both_in,) = call(
+        functools.partial(joint_kernel, chips),
+        [((width // 2 + chips * late.shape[0], channels), BF16)],
+        keep_in, partner(send_in, "seq", 0), late, partner(late, "seq", 0),
+        leave=(0,),
+    )
+    parts = exchanged(both_in, devices)
     (grad_hidden,) = call(
         hidden_kernel,
         [((length, w_in.shape[0]), BF16)],
@@ -729,25 +799,30 @@
         scratch=[pltpu.VMEM((length, channels), F32), pltpu.VMEM((2 * HALO, channels), F32)],
         fetch=range(1, 6), leave=(0,),
     )
-    flat = jnp.concatenate([sums.reshape(-1, LANES), conv_sums.reshape(-1, LANES)], axis=0)
-    for bit in range(devices.bit_length() - 1):
-        if bit == 2:
-            flat, grad_hidden = lax.optimization_barrier((flat, grad_hidden))
-        flat = flat + partner(flat, "seq", bit)
-    split = sums.size // LANES
-    sums = flat[:split].reshape(sums.shape)
-    base = 2 * LABELS
-    loss = jnp.sum(sums[base + 4, 0:LANES]).reshape(1) / (row_count * devices)
+    grad_w_in, grad_conv, grad_dt_t, grad_heads, gain, cls_t, loss = call(
+        functools.partial(joint_sums_kernel, slice_rows, float(row_count * devices)),
+        [
+            ((width // devices, channels), F32),
+            (conv_w.shape, F32),
+            ((HEADS, width), F32),
+            ((3, HEADS), F32),
+            ((1, width), F32),
+            ((LABELS, width), F32),
+            ((1, 1), F32),
+        ],
+        parts,
+        scratch=[pltpu.VMEM((STATE, LANES), F32)], leave=range(7),
+    )
     return (
         grad_hidden,
         grad_w_in,
         grad_w_out,
-        flat[split:].reshape(conv_w.shape),
-        sums[0:HEADS].T,
-        sums[base + 1 : base + 4, 0:HEADS],
-        sums[base],
-        sums[LABELS : 2 * LABELS].T,
-        loss,
+        grad_conv,
+        grad_dt_t.T,
+        grad_heads,
+        gain.reshape(width),
+        cls_t.T,
+        loss.reshape(1),
     )
 
 

time: 143 us -> 129 us (0.902)
  the two profiles are of different devices: /device:TPU:0 before, /device:TPU:18 now
where the time goes in v3:
time: 129 us; the launch traced here: 128 us
  waiting for transfers between devices  44.5 us (34%)
  Pallas kernels  40.3 us (31%)
  starting transfers between devices  40.1 us (31%)
  other arithmetic  2.02 us (2%)
    pallas_call x14, Pallas kernels, call(): pl.pallas_call(kernel, out_shape=[(far if i in leave else close)(*out) fo...  40.3 us
    ppermute x2, waiting for transfers between devices, passed_along(): return lax.ppermute(x, axis, pairs)  22.9 us
    all_to_all x4, starting transfers between devices, swapped(): return lax.all_to_all(x, axis, split_axis=0, concat_axis=0, tiled=True)  22.6 us
    all_to_all x4, waiting for transfers between devices, swapped(): return lax.all_to_all(x, axis, split_axis=0, concat_axis=0, tiled=True)  18 us
    all_to_all x2, starting transfers between devices, exchanged(): lax.all_to_all(both, 'seq', split_axis=0, concat_axis=0, axis_index_group...  12.1 us
    ppermute x2, starting transfers between devices, passed_along(): return lax.ppermute(x, axis, pairs)  4.65 us
  transfers between devices with their start and end apart: 11, of which 7 were waited for; matrix products, arithmetic and copies ran while one was open for 1% of the time, Pallas kernels for 22%

profile of v3, /device:TPU:18, one launch (start us, length us, event | category | flops | bytes accessed | tf_op | source)
XLA Modules:
  0.0 128.5 jit_solution(4984948650985831062)
XLA Ops:
  1.4 2.7 %collective-permute-start = (bf16[8,768]{1,0:T(8,128)(2,1)S(1)}, bf16[8,768]{1,0:T(8,128)(2,1)S(1)}, u32[]{:S(2)}, u32[]{:S(2)}) collective-permute-start(bf16[8,768]{1,0:T(8,128)(2,1)S(1)} %slice.3), channel_id=1, source_target_pairs={{1,0},{2,1},{3,2},{4,3},{5,4},{6,5},{7,6},{8,7},{9,8},{10,9},{11,1... | collective-permute-start | bytes 36872 | tf_op jit(solution)/shard_map/ppermute | solution.py:32
  4.1 2.7 %shard_map.214 = (bf16[128,128]{1,0:T(8,128)(2,1)S(1)}, f32[1,128]{1,0:T(1,128)}) custom-call(bf16[128,4096]{1,0:T(8,128)(2,1)} %refs_0_.1, bf16[16,4096]{1,0:T(8,128)(2,1)} %bitcast.27, s32[1,128]{1,0:T(1,128)} %bitcast.35, s32[1,128]{1,0:T(1,128)} %bitcast.36, s32[1,128]{1,0:T(1,128)} %bitcast.37), custom_call_target="tpu_custom_call" | custom-call | tf_op jit(solution)/shard_map/pallas_call | solution.py:174
  6.8 4.6 %shard_map.215 = (bf16[128,896]{1,0:T(8,128)(2,1)}, bf16[256,1024]{1,0:T(8,128)(2,1)S(1)}, bf16[264,1024]{1,0:T(8,128)(2,1)}, f32[256,256]{1,0:T(8,128)S(1)}, f3...) custom-call(bf16[8,768]{1,0:T(8,128)(2,1)S(1)} %collective-permute-done.refs_0_.refs_2_, bf16[256,768]{1,0:T(8,128)(2,1)} %refs_14_.1, ...), custom_call_target="tpu_custom_call" | custom-call | tf_op jit(solution)/shard_map/pallas_call | solution.py:174
  11.3 5.5 %all-to-all-start = ((bf16[16,8,896]{2,1,0:T(8,128)(2,1)}), bf16[16,8,896]{2,1,0:T(8,128)(2,1)S(1)}, u32[]{:S(2)}, u32[]{:S(2)}) async-start(bf16[16,8,896]{2,1,0:T(8,128)(2,1)} %bitcast.25), calls=%async_computation | async-start | bytes 458752 | tf_op jit(solution)/shard_map/all_to_all | solution.py:609
  18.1 6.3 %all-to-all-done.refs_0_ = bf16[16,8,896]{2,1,0:T(8,128)(2,1)S(1)} async-done(((bf16[16,8,896]{2,1,0:T(8,128)(2,1)}), bf16[16,8,896]{2,1,0:T(8,128)(2,1)S(1)}, u32[]{:S(2)}, u32[]{:S(2)}) %all-to-all-start) | async-done | bytes 229408 | tf_op jit(solution)/shard_map/all_to_all | solution.py:609
  24.4 1.5 %shard_map.217 = (bf16[16,8,768]{2,1,0:T(8,128)(2,1)}, f32[16,8,128]{2,1,0:T(8,128)S(1)}) custom-call(bf16[16,8,896]{2,1,0:T(8,128)(2,1)S(1)} %all-to-all-done.refs_0_, f32[256,768]{1,0:T(8,128)S(1)} %shard_map.216.refs_1_.refs_3_), custom_call_target="tpu_custom_call" | custom-call | tf_op jit(solution)/shard_map/pallas_call | solution.py:174
  25.9 5.4 %all-to-all-start.1 = ((bf16[16,8,768]{2,1,0:T(8,128)(2,1)}), bf16[16,8,768]{2,1,0:T(8,128)(2,1)S(1)}, u32[]{:S(2)}, u32[]{:S(2)}) async-start(bf16[16,8,768]{2,1,0:T(8,128)(2,1)} %get-tuple-element.53), calls=%async_computation.1 | async-start | bytes 393216 | tf_op jit(solution)/shard_map/all_to_all | solution.py:609
  31.9 6.2 %all-to-all-done.1 = bf16[16,8,768]{2,1,0:T(8,128)(2,1)S(1)} async-done(((bf16[16,8,768]{2,1,0:T(8,128)(2,1)}), bf16[16,8,768]{2,1,0:T(8,128)(2,1)S(1)}, u32[]{:S(2)}, u32[]{:S(2)}) %all-to-all-start.1) | async-done | bytes 196640 | tf_op jit(solution)/shard_map/all_to_all | solution.py:609
  38.2 5.0 %shard_map.219 = (bf16[128,768]{1,0:T(8,128)(2,1)}, f32[256,768]{1,0:T(8,128)S(1)}, bf16[256,768]{1,0:T(8,128)(2,1)}, bf16[256,768]{1,0:T(8,128)(2,1)}, bf16[256...) custom-call(bf16[128,768]{1,0:T(8,128)(2,1)S(1)} %bitcast.19, ...), custom_call_target="tpu_custom_call" | custom-call | tf_op jit(solution)/shard_map/pallas_call | solution.py:174
  43.2 5.7 %all-to-all-start.2 = ((bf16[16,8,768]{2,1,0:T(8,128)(2,1)}), bf16[16,8,768]{2,1,0:T(8,128)(2,1)S(1)}, u32[]{:S(2)}, u32[]{:S(2)}) async-start(bf16[16,8,768]{2,1,0:T(8,128)(2,1)} %bitcast.26), calls=%async_computation.2 | async-start | bytes 393216 | tf_op jit(solution)/shard_map/all_to_all | solution.py:609
  48.8 5.3 %shard_map.220 = (f32[256,768]{1,0:T(8,128)S(1)}, f32[256,256]{1,0:T(8,128)}, f32[256,128]{1,0:T(8,128)S(1)}, f32[256,128]{1,0:T(8,128)}) custom-call(bf16[256,1024]{1,0:T(8,128)(2,1)S(1)} %get-tuple-element.49.refs_0_.refs_1_.refs_4_, f32[256,256]{1,0:T(8,128)S(1)} %get-tuple-element.50.refs_1_.refs_5_, f32[256,128]{1,0:T(8,128)S(1)} %get-tuple-element.51.refs_2_.refs_3_, ...), custom_call_target="tpu_custom_call" | custom-call | tf_op jit(solution)/shard_map/pallas_call | solution.py:174
  54.1 2.9 %shard_map.221 = (bf16[384,768]{1,0:T(8,128)(2,1)}, bf16[384,768]{1,0:T(8,128)(2,1)}, f32[128,128]{1,0:T(8,128)S(1)}) custom-call(s32[1]{0:T(128)} %bitcast.refs_0_, bf16[256,768]{1,0:T(8,128)(2,1)} %get-tuple-element.56.refs_1_, bf16[256,768]{1,0:T(8,128)(2,1)} %get-tuple-element.57.refs_2_, bf16[256,768]{1,0:T(8,128)(2,1)} %get-tuple-element.58.refs_3_, ...), custom_call_target="tpu_custom_call" | custom-call | tf_op jit(solution)/shard_map/pallas_call | solution.py:174
  58.4 6.1 %all-to-all-start.3 = ((bf16[16,8,896]{2,1,0:T(8,128)(2,1)}), bf16[16,8,896]{2,1,0:T(8,128)(2,1)S(1)}, u32[]{:S(2)}, u32[]{:S(2)}) async-start(bf16[16,8,896]{2,1,0:T(8,128)(2,1)} %shard_map.222), calls=%async_computation.3 | async-start | bytes 458752 | tf_op jit(solution)/shard_map/all_to_all | solution.py:609
  64.4 2.0 %shard_map.223.refs_17_ = bf16[384,768]{1,0:T(8,128)(2,1)} custom-call(bf16[384,768]{1,0:T(8,128)(2,1)} %get-tuple-element.70.refs_0_, bf16[384,768]{1,0:T(8,128)(2,1)S(1)} %collective-permute-done.1.refs_1_), custom_call_target="tpu_custom_call" | custom-call | tf_op jit(solution)/shard_map/pallas_call | solution.py:174
  66.5 5.5 %all-to-all-done.3 = bf16[16,8,896]{2,1,0:T(8,128)(2,1)S(1)} async-done(((bf16[16,8,896]{2,1,0:T(8,128)(2,1)}), bf16[16,8,896]{2,1,0:T(8,128)(2,1)S(1)}, u32[]{:S(2)}, u32[]{:S(2)}) %all-to-all-start.3) | async-done | bytes 229408 | tf_op jit(solution)/shard_map/all_to_all | solution.py:609
  72.0 5.5 %all-to-all-start.5 = ((bf16[8,48,768]{2,1,0:T(8,128)(2,1)}), bf16[8,48,768]{2,1,0:T(8,128)(2,1)S(1)}, u32[]{:S(2)}, u32[]{:S(2)}) async-start(bf16[8,48,768]{2,1,0:T(8,128)(2,1)} %bitcast.23), calls=%async_computation.5 | async-start | bytes 1179648 | tf_op jit(solution)/shard_map/all_to_all | solution.py:670
  77.5 7.9 %shard_map.224 = (bf16[384,1024]{1,0:T(8,128)(2,1)S(1)}, bf16[384,1024]{1,0:T(8,128)(2,1)}, f32[8,1024]{1,0:T(8,128)}, f32[256,1024]{1,0:T(8,128)}, bf16[256,128]{1,0:T(8,128)(2,1)}, /*index=5*/f32[16,1024]{1,0:T(8,128)S(1)}) custom-call(s32[1]{0:T(128)} %bitcast.refs_0_, bf16[128,896]{1,0:T(8,128)(2,1)S(1)} %bitcast.22, ...), custom_call_target="tpu_custom_call" | custom-call | tf_op jit(solution)/shard_map/pallas_call | solution.py:174
  85.9 1.6 %collective-permute-done.4.refs_3_ = f32[16,1024]{1,0:T(8,128)S(1)} collective-permute-done((f32[16,1024]{1,0:T(8,128)S(1)}, f32[16,1024]{1,0:T(8,128)S(1)}, u32[]{:S(2)}, u32[]{:S(2)}) %collective-permute-start.4) | collective-permute-done | bytes 65568 | tf_op jit(solution)/shard_map/ppermute | solution.py:26
  89.2 1.5 %all-to-all-done.5 = bf16[8,48,768]{2,1,0:T(8,128)(2,1)S(1)} async-done(((bf16[8,48,768]{2,1,0:T(8,128)(2,1)}), bf16[8,48,768]{2,1,0:T(8,128)(2,1)S(1)}, u32[]{:S(2)}, u32[]{:S(2)}) %all-to-all-start.5) | async-done | bytes 589856 | tf_op jit(solution)/shard_map/all_to_all | solution.py:670
  90.7 6.6 %all-to-all-start.4 = ((bf16[8,64,1024]{2,1,0:T(8,128)(2,1)}), bf16[8,64,1024]{2,1,0:T(8,128)(2,1)S(1)}, u32[]{:S(2)}, u32[]{:S(2)}) async-start(bf16[8,64,1024]{2,1,0:T(8,128)(2,1)} %bitcast.24), calls=%async_computation.4 | async-start | bytes 2097152 | tf_op jit(solution)/shard_map/all_to_all | solution.py:670
  97.3 1.9 %collective-permute-start.2 = (f32[8,1024]{1,0:T(8,128)S(1)}, f32[8,1024]{1,0:T(8,128)S(1)}, u32[]{:S(2)}, u32[]{:S(2)}) collective-permute-start(f32[8,1024]{1,0:T(8,128)S(1)} %copy-done), channel_id=1, source_target_pairs={{0,1},{1,2},{2,3},{3,4},{4,5},{5,6},{6,7},{7,8},{8,9},{9,10},{10,1... | collective-permute-start | bytes 98312 | tf_op jit(solution)/shard_map/ppermute | solution.py:32
  99.2 22.9 %collective-permute-done.2.refs_0_ = f32[8,1024]{1,0:T(8,128)S(1)} collective-permute-done((f32[8,1024]{1,0:T(8,128)S(1)}, f32[8,1024]{1,0:T(8,128)S(1)}, u32[]{:S(2)}, u32[]{:S(2)}) %collective-permute-start.2) | collective-permute-done | bytes 32800 | tf_op jit(solution)/shard_map/ppermute | solution.py:32
  122.1 3.4 %shard_map.225 = bf16[256,768]{1,0:T(8,128)(2,1)} custom-call(f32[8,1024]{1,0:T(8,128)S(1)} %collective-permute-done.2.refs_0_, f32[256,1024]{1,0:T(8,128)} %get-tuple-element.73.refs_1_, f32[4,1024]{1,0:T(4,128)} %refs_2_.1, bf16[256,128]{1,0:T(8,128)(2,1)} %get-tuple-element.74.refs_3_, bf16[12,768]{1,0:T(8,128)(2,1)} %bitcast.29, bf16[768,1024]{1,0:T(8,128)(2,1)} %refs_5_.5), custom_call_target="tpu_custom_call" | custom-call | tf_op jit(solution)/shard_map/pallas_call | solution.py:174
  127.2 1.3 reduce
  (17 shorter events, 7.9 us)
Async XLA Ops:
  1.4 5.4 %collective-permute-start = (bf16[8,768]{1,0:T(8,128)(2,1)S(1)}, bf16[8,768]{1,0:T(8,128)(2,1)S(1)}, u32[]{:S(2)}, u32[]{:S(2)}) collective-permute-start(bf16[8,768]{1,0:T(8,128)(2,1)S(1)} %slice.3), channel_id=1, source_target_pairs={{1,0},{2,1},{3,2},{4,3},{5,4},{6,5},{7,6},{8,7},{9,8},{10,9},{11,1... | collective-permute-start | bytes 36872 | tf_op jit(solution)/shard_map/ppermute | solution.py:32
  11.3 13.0 %all-to-all-start = ((bf16[16,8,896]{2,1,0:T(8,128)(2,1)}), bf16[16,8,896]{2,1,0:T(8,128)(2,1)S(1)}, u32[]{:S(2)}, u32[]{:S(2)}) async-start(bf16[16,8,896]{2,1,0:T(8,128)(2,1)} %bitcast.25), calls=%async_computation | async-start | bytes 458752 | tf_op jit(solution)/shard_map/all_to_all | solution.py:609
  25.9 12.3 %all-to-all-start.1 = ((bf16[16,8,768]{2,1,0:T(8,128)(2,1)}), bf16[16,8,768]{2,1,0:T(8,128)(2,1)S(1)}, u32[]{:S(2)}, u32[]{:S(2)}) async-start(bf16[16,8,768]{2,1,0:T(8,128)(2,1)} %get-tuple-element.53), calls=%async_computation.1 | async-start | bytes 393216 | tf_op jit(solution)/shard_map/all_to_all | solution.py:609
  43.2 14.1 %all-to-all-start.2 = ((bf16[16,8,768]{2,1,0:T(8,128)(2,1)}), bf16[16,8,768]{2,1,0:T(8,128)(2,1)S(1)}, u32[]{:S(2)}, u32[]{:S(2)}) async-start(bf16[16,8,768]{2,1,0:T(8,128)(2,1)} %bitcast.26), calls=%async_computation.2 | async-start | bytes 393216 | tf_op jit(solution)/shard_map/all_to_all | solution.py:609
  57.0 7.4 %collective-permute-start.1 = (bf16[384,768]{1,0:T(8,128)(2,1)}, bf16[384,768]{1,0:T(8,128)(2,1)S(1)}, u32[]{:S(2)}, u32[]{:S(2)}) collective-permute-start(bf16[384,768]{1,0:T(8,128)(2,1)} %get-tuple-element.71), channel_id=1, source_target_pairs={{0,1},{1,0},{2,3},{3,2},{4,5},{5,4},{6,7},{7,6},{8,9},{9,8},{10,11... | collective-permute-start | bytes 1769480 | tf_op jit(solution)/shard_map/ppermute | solution.py:26
  58.4 13.6 %all-to-all-start.3 = ((bf16[16,8,896]{2,1,0:T(8,128)(2,1)}), bf16[16,8,896]{2,1,0:T(8,128)(2,1)S(1)}, u32[]{:S(2)}, u32[]{:S(2)}) async-start(bf16[16,8,896]{2,1,0:T(8,128)(2,1)} %shard_map.222), calls=%async_computation.3 | async-start | bytes 458752 | tf_op jit(solution)/shard_map/all_to_all | solution.py:609
  72.0 18.7 %all-to-all-start.5 = ((bf16[8,48,768]{2,1,0:T(8,128)(2,1)}), bf16[8,48,768]{2,1,0:T(8,128)(2,1)S(1)}, u32[]{:S(2)}, u32[]{:S(2)}) async-start(bf16[8,48,768]{2,1,0:T(8,128)(2,1)} %bitcast.23), calls=%async_computation.5 | async-start | bytes 1179648 | tf_op jit(solution)/shard_map/all_to_all | solution.py:670
  85.4 2.7 %collective-permute-start.3 = (bf16[384,1024]{1,0:T(8,128)(2,1)}, bf16[384,1024]{1,0:T(8,128)(2,1)S(1)}, u32[]{:S(2)}, u32[]{:S(2)}) collective-permute-start(bf16[384,1024]{1,0:T(8,128)(2,1)} %get-tuple-element.76), channel_id=1, source_target_pairs={{0,1},{1,0},{2,3},{3,2},{4,5},{5,4},{6,7},{7,6},{8,9},{9,8},{10,11... | collective-permute-start | bytes 2359304 | tf_op jit(solution)/shard_map/ppermute | solution.py:26
  85.4 2.1 %collective-permute-start.4 = (f32[16,1024]{1,0:T(8,128)S(1)}, f32[16,1024]{1,0:T(8,128)S(1)}, u32[]{:S(2)}, u32[]{:S(2)}) collective-permute-start(f32[16,1024]{1,0:T(8,128)S(1)} %get-tuple-element.77.refs_2_), channel_id=1, source_target_pairs={{0,1},{1,0},{2,3},{3,2},{4,5},{5,4},{6,7},{7,6},{8,9},{9,8},{10,11... | collective-permute-start | bytes 196616 | tf_op jit(solution)/shard_map/ppermute | solution.py:26
  89.2 8.1 %copy-start = (f32[8,1024]{1,0:T(8,128)S(1)}, f32[8,1024]{1,0:T(8,128)}, u32[]{:S(2)}) copy-start(f32[8,1024]{1,0:T(8,128)} %get-tuple-element.72) | copy-start | bytes 98308
  90.7 35.6 %all-to-all-start.4 = ((bf16[8,64,1024]{2,1,0:T(8,128)(2,1)}), bf16[8,64,1024]{2,1,0:T(8,128)(2,1)S(1)}, u32[]{:S(2)}, u32[]{:S(2)}) async-start(bf16[8,64,1024]{2,1,0:T(8,128)(2,1)} %bitcast.24), calls=%async_computation.4 | async-start | bytes 2097152 | tf_op jit(solution)/shard_map/all_to_all | solution.py:670
  97.3 24.8 %collective-permute-start.2 = (f32[8,1024]{1,0:T(8,128)S(1)}, f32[8,1024]{1,0:T(8,128)S(1)}, u32[]{:S(2)}, u32[]{:S(2)}) collective-permute-start(f32[8,1024]{1,0:T(8,128)S(1)} %copy-done), channel_id=1, source_target_pairs={{0,1},{1,2},{2,3},{3,4},{4,5},{5,6},{6,7},{7,8},{8,9},{9,10},{10,1... | collective-permute-start | bytes 98312 | tf_op jit(solution)/shard_map/ppermute | solution.py:32

commit v4 on v3

--- a/solution.py
+++ b/solution.py
@@ -229,7 +229,7 @@
     own[...] = jnp.where(lane[0:1] == 0, jnp.sum(gained, axis=0, keepdims=True), 0.0)
 
 
-def target_kernel(arrived, target):
+def target_kernel(arrived, w_cls, w_out, target, joined_high, joined_low):
     length = target.shape[0]
     width = HEADS * HDIM
     count, rows = arrived.shape[0], arrived.shape[1]
@@ -250,6 +250,9 @@
         cover = pltpu.roll(sums, (LABELS - spare - 2) % LANES, 1)
         total = total + jnp.where(lane < LABELS, high + low, jnp.where(lane == LABELS, cover, 0.0))
     target[...] = total
+    place = (iota((LANES, LABELS), 0) == iota((LANES, LABELS), 1)).astype(BF16)
+    joined = dot(dot(place, w_cls[...]).astype(BF16), w_out[...], 1, 1)
+    joined_high[...], joined_low[...] = pieces(joined, 2)
 
 
 def convolved(raw, conv_w, length):
@@ -352,8 +355,8 @@
 
 
 def middle_kernel(
-    state, mixed, run, local, d_skip, gains, w_out, w_cls, target,
-    back_state, grad_scanned, normed_o, branch_o, back_branch_o, logits_o, run_grad, small,
+    state, mixed, run, local, d_skip, gains, high, low, target,
+    back_state, grad_scanned, normed_o, logits_o, run_grad, small,
 ):
     length = mixed.shape[0]
     width = HEADS * HDIM
@@ -369,13 +372,8 @@
     normed = (plain * gain).astype(BF16)
     normed_o[...] = normed
     normed_o.send()
-    branch = dot(normed, w_out[...]).astype(BF16)
-    branch_o[...] = branch
-    branch_o.send()
     label = iota((length, LANES), 1) < LABELS
-    wide = (iota((LANES, LABELS), 0) == iota((LANES, LABELS), 1)).astype(BF16)
-    weights = dot(wide, w_cls[...]).astype(BF16)
-    logits = jnp.where(label, dot(branch, weights, 1, 1), FAR)
+    logits = jnp.where(label, dot(normed, high[...], 1, 1) + dot(normed, low[...], 1, 1), FAR)
     shifted = logits - jnp.max(logits, axis=1, keepdims=True)
     raised = jnp.exp(shifted)
     whole = jnp.sum(raised, axis=1, keepdims=True)
@@ -386,23 +384,21 @@
     logits_o[...] = back_logits
     logits_o.send()
     lost = jnp.sum(jnp.where(label, wanted * logp, 0.0), axis=0, keepdims=True)
-    back_branch = sum(dot(part, weights) for part in pieces(back_logits, 2)).astype(BF16)
-    back_branch_o[...] = back_branch
-    back_branch_o.send()
-    back_normed = dot(back_branch, w_out[...], 1, 1)
+    back_high, back_low = pieces(back_logits, 2)
+    back_normed = dot(back_high, high[...]) + dot(back_low, high[...]) + dot(back_high, low[...])
     back_plain = back_normed * gain
     along = jnp.mean(back_plain * plain, axis=1, keepdims=True)
     back = scale * (back_plain - plain * along)
     grad_scanned[...] = back
-    grad_scanned.send()
     back_state[...] = dot(out_map, (back * reach).astype(BF16), 0, 0).astype(BF16)
     back_state.send()
-    run_grad[...] = head_sums(back * carried)
     small[0:1, :] = jnp.sum(back_normed * plain, axis=0, keepdims=True)
     small[1:2, :] = jnp.sum(back * values, axis=0, keepdims=True)
     small[2:3, :] = jnp.zeros((1, width), F32)
     small[2:3, 0:LANES] = lost
     small[3:, :] = jnp.zeros((5, width), F32)
+    small.send()
+    run_grad[...] = head_sums(back * carried)
 
 
 def halves(full, keep, send, odd, blocks):
@@ -419,27 +415,9 @@
                 send[at, :] = full[other : other + size, :].astype(BF16)
 
 
-def outward_kernel(
-    blocks, place, normed, back_branch, branch, back_logits, small, keep, send, early, full
-):
-    full[...] = dot(normed[...], back_branch[...], 0, 0)
-    halves(full, keep, send, place[0] % 2, blocks)
-    keep.send()
-    send.send()
-    parts = pieces(back_logits[...], 2)
-    cls = sum(dot(part, branch[...], 0, 0) for part in parts)[0:LABELS]
-    count = cls.shape[1] // LANES
-    early[count * LABELS :, :] = jnp.zeros((early.shape[0] - count * LABELS, LANES), F32)
-    for block in range(count):
-        lanes = slice(block * LANES, (block + 1) * LANES)
-        early[block * LABELS : (block + 1) * LABELS, :] = cls[:, lanes]
-        at = count * LABELS + block
-        early[at : at + 1, :] = small[0:1, lanes]
-
-
 def local_back_kernel(
-    mixed, step, run, grad_scanned, d_skip, state, carried_grad,
-    values_grad, maps, run_grad, step_grad, weighted_grad,
+    mixed, step, run, grad_scanned, d_skip, state, carried_grad, normed, back_logits, small,
+    values_grad, maps, run_grad, step_grad, early, weighted_grad,
 ):
     length = mixed.shape[0]
     half = length // 2
@@ -502,6 +480,14 @@
     maps[half:, 0:STATE] = in_grad[half:] + dot(back_low, out_map[half:], 0, 0)
     run_grad[0:half, :] = carried_grad[0:half, :] + rows_top - columns[0:half]
     run_grad[half:, :] = carried_grad[half:, :] + rows_low - columns[half:] - columns_low
+    product = sum(dot(part, normed[...], 0, 0) for part in pieces(back_logits[...], 2))[0:LABELS]
+    count = width // LANES
+    early[count * LABELS :, :] = jnp.zeros((early.shape[0] - count * LABELS, LANES), F32)
+    for block in range(count):
+        lanes = slice(block * LANES, (block + 1) * LANES)
+        early[block * LABELS : (block + 1) * LABELS, :] = product[:, lanes]
+        at = count * LABELS + block
+        early[at : at + 1, :] = small[0:1, lanes]
 
 
 def last_kernel(
@@ -520,7 +506,8 @@
     reached = dot(in_map, incoming) * tail
     steps = spread_heads(step[:, 0:LANES])
     weighted = values * steps
-    ended = head_sums(reached * weighted)
+    reaching = head_sums(reached * values)
+    ended = reaching * step[:, 0:LANES]
     in_grad = dot((weighted * tail).astype(BF16), incoming, 1, 1)
     product = jnp.sum(incoming.astype(F32) * state[...].astype(F32), axis=0, keepdims=True)
     total_grad = jnp.exp(total) * head_sums(jnp.broadcast_to(product, (8, width)))[0:1]
@@ -531,7 +518,7 @@
         + total_grad
     )
     rate = jnp.exp(widened(a_log[...]))
-    step_grad = step_local[...] + head_sums(reached * values) - rate * decay_grad
+    step_grad = step_local[...] + reaching - rate * decay_grad
     before = step[:, LANES:]
     step_grad = jnp.where(
         iota((length, LANES), 1) < HEADS, step_grad / (1.0 + jnp.exp(-before)), 0.0
@@ -609,17 +596,6 @@
     return lax.all_to_all(x, axis, split_axis=0, concat_axis=0, tiled=True)
 
 
-def pair_kernel(keep, received, both):
-    half = keep.shape[0] // 2
-    both[0:half, :] = (keep[0:half, :].astype(F32) + received[0:half, :].astype(F32)).astype(BF16)
-    both[half:, :] = (keep[half:, :].astype(F32) + received[half:, :].astype(F32)).astype(BF16)
-
-
-def paired(keep, send, fetch):
-    received = partner(send, "seq", 0)
-    return call(pair_kernel, [(keep.shape, BF16)], keep, received, fetch=fetch, leave=(0,))[0]
-
-
 def joint_kernel(blocks, keep, received, late, late_received, both):
     size = keep.shape[0] // blocks
     rows, width = late.shape[0], HEADS * HDIM
@@ -638,7 +614,8 @@
 
 
 def joint_sums_kernel(
-    share, rows_in_all, parts, grad_w_in, grad_conv, grad_dt_t, grad_heads, gain, cls_t, loss, early
+    share, rows_in_all, place, parts, w_out, w_cls,
+    grad_w_in, grad_conv, grad_dt_t, grad_heads, gain, cls_t, loss, grad_w_out, early, product,
 ):
     total = parts[0].astype(F32)
     for chip in range(1, parts.shape[0]):
@@ -661,8 +638,12 @@
     count = width // LANES
     for block in range(count):
         lanes = slice(block * LANES, (block + 1) * LANES)
-        cls_t[:, lanes] = early[block * LABELS : (block + 1) * LABELS, :]
-        gain[:, lanes] = early[count * LABELS + block : count * LABELS + block + 1, :]
+        product[:, lanes] = early[block * LABELS : (block + 1) * LABELS, :].astype(BF16)
+        gain[lanes] = early[count * LABELS + block, :]
+    cls_t[...] = dot(product[...], w_out[...])
+    own = (iota((size, width), 1) == iota((size, width), 0) + place[0] * size).astype(F32)
+    rows = dot(own.astype(BF16), product[...], 1, 1).astype(BF16)
+    grad_w_out[...] = dot(rows, w_cls[...])
 
 
 def exchanged(both, devices):
@@ -719,41 +700,38 @@
         after=[local],
     )
     state = swapped(onward.reshape(STATE, width))
-    (target,) = call(target_kernel, [((length, LANES), F32)], arrived)
-
-    back_state, grad_scanned, normed, branch, back_branch, back_logits, carried_grad, small = call(
+    target, labels_high, labels_low = call(
+        target_kernel,
+        [((length, LANES), F32), ((LANES, width), BF16), ((LANES, width), BF16)],
+        arrived, w_cls.T, w_out,
+        fetch=(1, 2),
+    )
+
+    back_state, grad_scanned, normed, back_logits, carried_grad, small = call(
         middle_kernel,
         [
             ((STATE, width), BF16),
             ((length, width), F32),
             ((length, width), BF16),
-            ((length, width), BF16),
-            ((length, width), BF16),
             ((length, LANES), F32),
             ((length, LANES), F32),
             ((8, width), F32),
         ],
-        state, mixed, run, local, skip_row, norm_gain, w_out, w_cls.T, target,
-        fetch=(4, 5, 6, 7), leave=(0, 2, 3, 4, 5, 6, 7),
+        state, mixed, run, local, skip_row, norm_gain, labels_high, labels_low, target,
+        fetch=(4, 5), leave=(0, 2, 3, 5),
     )
     back_arrived = swapped(back_state).reshape(devices, slice_rows, width)
-    values_local, maps, run_grad, step_local = call(
+    values_local, maps, run_grad, step_local, early = call(
         local_back_kernel,
         [
             ((length, width), F32),
             ((length, 2 * STATE), F32),
             ((length, LANES), F32),
             ((length, LANES), F32),
+            ((STATE, LANES), F32),
         ],
-        mixed, step, run, grad_scanned, skip_row, state, carried_grad,
-        scratch=[pltpu.VMEM((length, width), F32)], fetch=(4, 6), leave=(1, 3),
-    )
-    keep_out, send_out, early = call(
-        functools.partial(outward_kernel, devices),
-        [((width // 2, width), BF16), ((width // 2, width), BF16), ((STATE, LANES), F32)],
-        place, normed, back_branch, branch, back_logits, small,
-        scratch=[pltpu.VMEM((width, width), F32)],
-        scalars=1, fetch=range(1, 6), leave=(0, 1), after=[run_grad],
+        mixed, step, run, grad_scanned, skip_row, state, carried_grad, normed, back_logits, small,
+        scratch=[pltpu.VMEM((length, width), F32)], fetch=(4, 7, 8, 9), leave=(1, 3),
     )
     (back_onward,) = call(
         state_grads_kernel,
@@ -762,8 +740,6 @@
         leave=(0,),
     )
     state_grad = swapped(back_onward.reshape(STATE, width + LANES))
-    both_out = paired(keep_out, send_out, (0,))
-    grad_w_out = jnp.sum(exchanged(both_out, devices).astype(F32), axis=0)
 
     keep_in, send_in, rim, back_raw, step_grad, late = call(
         functools.partial(last_kernel, devices),
@@ -782,7 +758,7 @@
             pltpu.VMEM((length + 2 * HALO, channels), F32),
             pltpu.VMEM((length + HALO, channels), F32),
         ],
-        scalars=1, fetch=(8, 9, 10, 12, 13, 14, 15, 16), leave=(1, 2, 3, 4), wait=[both_out],
+        scalars=1, fetch=(8, 9, 10, 12, 13, 14, 15, 16), leave=(1, 2, 3, 4),
     )
     chips = devices // 2
     (both_in,) = call(
@@ -799,19 +775,21 @@
         scratch=[pltpu.VMEM((length, channels), F32), pltpu.VMEM((2 * HALO, channels), F32)],
         fetch=range(1, 6), leave=(0,),
     )
-    grad_w_in, grad_conv, grad_dt_t, grad_heads, gain, cls_t, loss = call(
+    grad_w_in, grad_conv, grad_dt_t, grad_heads, gain, cls_t, loss, grad_w_out = call(
         functools.partial(joint_sums_kernel, slice_rows, float(row_count * devices)),
         [
             ((width // devices, channels), F32),
             (conv_w.shape, F32),
             ((HEADS, width), F32),
             ((3, HEADS), F32),
-            ((1, width), F32),
+            ((width,), F32),
             ((LABELS, width), F32),
             ((1, 1), F32),
+            ((width // devices, width), F32),
         ],
-        parts,
-        scratch=[pltpu.VMEM((STATE, LANES), F32)], leave=range(7),
+        place, parts, w_out, w_cls.T,
+        scratch=[pltpu.VMEM((STATE, LANES), F32), pltpu.VMEM((LABELS, width), BF16)],
+        scalars=1, leave=range(8),
     )
     return (
         grad_hidden,
@@ -820,7 +798,7 @@
         grad_conv,
         grad_dt_t.T,
         grad_heads,
-        gain.reshape(width),
+        gain,
         cls_t.T,
         loss.reshape(1),
     )

time: 129 us -> 118 us (0.915)
  the two profiles are of different devices: /device:TPU:18 before, /device:TPU:0 now
where the time goes in v4:
time: 118 us; the launch traced here: 116 us
  waiting for transfers between devices  48.7 us (41%)
  Pallas kernels  36.6 us (31%)
  starting transfers between devices  26.5 us (22%)
  local copies, waits for them, and re-layouts  3.18 us (3%)
    pallas_call x12, Pallas kernels, call(): pl.pallas_call(kernel, out_shape=[(far if i in leave else close)(*out) fo...  36.6 us
    all_to_all x4, waiting for transfers between devices, swapped(): return lax.all_to_all(x, axis, split_axis=0, concat_axis=0, tiled=True)  25.8 us
    all_to_all x1, waiting for transfers between devices, exchanged(): lax.all_to_all(both, 'seq', split_axis=0, concat_axis=0, axis_index_group...  19.9 us
    all_to_all x4, starting transfers between devices, swapped(): return lax.all_to_all(x, axis, split_axis=0, concat_axis=0, tiled=True)  19 us
    all_to_all x1, starting transfers between devices, exchanged(): lax.all_to_all(both, 'seq', split_axis=0, concat_axis=0, axis_index_group...  3.57 us
    ppermute x2, starting transfers between devices, passed_along(): return lax.ppermute(x, axis, pairs)  3.32 us
    unnamed x14, local copies, waits for them, and re-layouts  2.47 us
  transfers between devices with their start and end apart: 9, of which 8 were waited for; matrix products, arithmetic and copies ran while one was open for 0% of the time, Pallas kernels for 13%

profile of v4, /device:TPU:0, one launch (start us, length us, event | category | flops | bytes accessed | tf_op | source)
XLA Modules:
  0.0 115.9 jit_solution(18185725748541166956)
XLA Ops:
  1.4 1.3 %collective-permute-start = (bf16[8,768]{1,0:T(8,128)(2,1)S(1)}, bf16[8,768]{1,0:T(8,128)(2,1)S(1)}, u32[]{:S(2)}, u32[]{:S(2)}) collective-permute-start(bf16[8,768]{1,0:T(8,128)(2,1)S(1)} %slice.3), channel_id=1, source_target_pairs={{1,0},{2,1},{3,2},{4,3},{5,4},{6,5},{7,6},{8,7},{9,8},{10,9},{11,1... | collective-permute-start | bytes 36872 | tf_op jit(solution)/shard_map/ppermute | solution.py:32
  2.6 2.7 %shard_map.214 = (bf16[128,128]{1,0:T(8,128)(2,1)S(1)}, f32[1,128]{1,0:T(1,128)}) custom-call(bf16[128,4096]{1,0:T(8,128)(2,1)} %refs_0_.1, bf16[16,4096]{1,0:T(8,128)(2,1)} %bitcast.27, s32[1,128]{1,0:T(1,128)} %bitcast.34, s32[1,128]{1,0:T(1,128)} %bitcast.35, s32[1,128]{1,0:T(1,128)} %bitcast.36), custom_call_target="tpu_custom_call" | custom-call | tf_op jit(solution)/shard_map/pallas_call | solution.py:174
  5.3 4.6 %shard_map.215 = (bf16[128,896]{1,0:T(8,128)(2,1)}, bf16[256,1024]{1,0:T(8,128)(2,1)S(1)}, bf16[264,1024]{1,0:T(8,128)(2,1)}, f32[256,256]{1,0:T(8,128)S(1)}, f3...) custom-call(bf16[8,768]{1,0:T(8,128)(2,1)S(1)} %collective-permute-done.refs_0_.refs_2_, bf16[256,768]{1,0:T(8,128)(2,1)} %refs_14_.1, ...), custom_call_target="tpu_custom_call" | custom-call | tf_op jit(solution)/shard_map/pallas_call | solution.py:174
  10.0 8.1 %all-to-all-start = ((bf16[16,8,896]{2,1,0:T(8,128)(2,1)}), bf16[16,8,896]{2,1,0:T(8,128)(2,1)S(1)}, u32[]{:S(2)}, u32[]{:S(2)}) async-start(bf16[16,8,896]{2,1,0:T(8,128)(2,1)} %bitcast.25), calls=%async_computation | async-start | bytes 458752 | tf_op jit(solution)/shard_map/all_to_all | solution.py:596
  18.1 1.3 %shard_map.216.refs_1_.refs_3_ = f32[256,768]{1,0:T(8,128)S(1)} custom-call(bf16[256,1024]{1,0:T(8,128)(2,1)S(1)} %get-tuple-element.49.refs_0_.refs_1_.refs_4_, f32[256,256]{1,0:T(8,128)S(1)} %get-tuple-element.50.refs_1_.refs_5_, f32[256,128]{1,0:T(8,128)S(1)} %get-tuple-element.51.refs_2_.refs_3_, f32[128,256]{1,0:T(8,128)S(1)} %get-tuple-element.52.refs_3_), custom_call_target="tpu_custom_call" | custom-call | tf_op jit(solution)/shard_map/pallas_call | solution.py:174
  19.4 8.2 %all-to-all-done.refs_0_ = bf16[16,8,896]{2,1,0:T(8,128)(2,1)S(1)} async-done(((bf16[16,8,896]{2,1,0:T(8,128)(2,1)}), bf16[16,8,896]{2,1,0:T(8,128)(2,1)S(1)}, u32[]{:S(2)}, u32[]{:S(2)}) %all-to-all-start) | async-done | bytes 229408 | tf_op jit(solution)/shard_map/all_to_all | solution.py:596
  27.6 1.5 %shard_map.217 = (bf16[16,8,768]{2,1,0:T(8,128)(2,1)}, f32[16,8,128]{2,1,0:T(8,128)S(1)}) custom-call(bf16[16,8,896]{2,1,0:T(8,128)(2,1)S(1)} %all-to-all-done.refs_0_, f32[256,768]{1,0:T(8,128)S(1)} %shard_map.216.refs_1_.refs_3_), custom_call_target="tpu_custom_call" | custom-call | tf_op jit(solution)/shard_map/pallas_call | solution.py:174
  29.1 3.5 %all-to-all-start.1 = ((bf16[16,8,768]{2,1,0:T(8,128)(2,1)}), bf16[16,8,768]{2,1,0:T(8,128)(2,1)S(1)}, u32[]{:S(2)}, u32[]{:S(2)}) async-start(bf16[16,8,768]{2,1,0:T(8,128)(2,1)} %get-tuple-element.53), calls=%async_computation.1 | async-start | bytes 393216 | tf_op jit(solution)/shard_map/all_to_all | solution.py:596
  32.7 2.4 %shard_map.218 = (f32[256,128]{1,0:T(8,128)S(1)}, bf16[128,768]{1,0:T(8,128)(2,1)S(1)}, bf16[128,768]{1,0:T(8,128)(2,1)S(1)}) custom-call(bf16[16,8,896]{2,1,0:T(8,128)(2,1)S(1)} %all-to-all-done.refs_0_, bf16[16,768]{1,0:T(8,128)(2,1)} %bitcast.22, bf16[768,768]{1,0:T(8,128)(2,1)} %refs_2_.5), custom_call_target="tpu_custom_call" | custom-call | tf_op jit(solution)/shard_map/pallas_call | solution.py:174
  35.7 5.9 %all-to-all-done.1 = bf16[16,8,768]{2,1,0:T(8,128)(2,1)S(1)} async-done(((bf16[16,8,768]{2,1,0:T(8,128)(2,1)}), bf16[16,8,768]{2,1,0:T(8,128)(2,1)S(1)}, u32[]{:S(2)}, u32[]{:S(2)}) %all-to-all-start.1) | async-done | bytes 196640 | tf_op jit(solution)/shard_map/all_to_all | solution.py:596
  42.5 4.0 %shard_map.219 = (bf16[128,768]{1,0:T(8,128)(2,1)}, f32[256,768]{1,0:T(8,128)S(1)}, bf16[256,768]{1,0:T(8,128)(2,1)}, f32[256,128]{1,0:T(8,128)}, f32[256,128]{1,0:T(8,128)S(1)}, /*index=5*/f32[8,768]{1,0:T(8,128)}) custom-call(bf16[128,768]{1,0:T(8,128)(2,1)S(1)} %bitcast.18, bf16[256,1024]{1,0:T(8,128)(2,1)S(1)} %get-tuple-element.49.refs_0_.refs_1_.refs_4_, ...), custom_call_target="tpu_custom_call" | custom-call | tf_op jit(solution)/shard_map/pallas_call | solution.py:174
  46.5 3.7 %all-to-all-start.2 = ((bf16[16,8,768]{2,1,0:T(8,128)(2,1)}), bf16[16,8,768]{2,1,0:T(8,128)(2,1)S(1)}, u32[]{:S(2)}, u32[]{:S(2)}) async-start(bf16[16,8,768]{2,1,0:T(8,128)(2,1)} %bitcast.26), calls=%async_computation.2 | async-start | bytes 393216 | tf_op jit(solution)/shard_map/all_to_all | solution.py:596
  51.1 5.7 %shard_map.220 = (f32[256,768]{1,0:T(8,128)S(1)}, f32[256,256]{1,0:T(8,128)}, f32[256,128]{1,0:T(8,128)S(1)}, f32[256,128]{1,0:T(8,128)}, f32[128,128]{1,0:T(8,128)S(1)}) custom-call(bf16[256,1024]{1,0:T(8,128)(2,1)S(1)} %get-tuple-element.49.refs_0_.refs_1_.refs_4_, f32[256,256]{1,0:T(8,128)S(1)} %get-tuple-element.50.refs_1_.refs_5_, ...), custom_call_target="tpu_custom_call" | custom-call | tf_op jit(solution)/shard_map/pallas_call | solution.py:174
  56.8 2.2 %all-to-all-done.2.refs_0_ = bf16[16,8,768]{2,1,0:T(8,128)(2,1)S(1)} async-done(((bf16[16,8,768]{2,1,0:T(8,128)(2,1)}), bf16[16,8,768]{2,1,0:T(8,128)(2,1)S(1)}, u32[]{:S(2)}, u32[]{:S(2)}) %all-to-all-start.2) | async-done | bytes 196640 | tf_op jit(solution)/shard_map/all_to_all | solution.py:596
  60.1 3.6 %all-to-all-start.3 = ((bf16[16,8,896]{2,1,0:T(8,128)(2,1)}), bf16[16,8,896]{2,1,0:T(8,128)(2,1)S(1)}, u32[]{:S(2)}, u32[]{:S(2)}) async-start(bf16[16,8,896]{2,1,0:T(8,128)(2,1)} %shard_map.221), calls=%async_computation.3 | async-start | bytes 458752 | tf_op jit(solution)/shard_map/all_to_all | solution.py:596
  63.7 9.5 %all-to-all-done.3 = bf16[16,8,896]{2,1,0:T(8,128)(2,1)S(1)} async-done(((bf16[16,8,896]{2,1,0:T(8,128)(2,1)}), bf16[16,8,896]{2,1,0:T(8,128)(2,1)S(1)}, u32[]{:S(2)}, u32[]{:S(2)}) %all-to-all-start.3) | async-done | bytes 229408 | tf_op jit(solution)/shard_map/all_to_all | solution.py:596
  73.2 7.5 %shard_map.222 = (bf16[384,1024]{1,0:T(8,128)(2,1)S(1)}, bf16[384,1024]{1,0:T(8,128)(2,1)}, f32[8,1024]{1,0:T(8,128)}, f32[256,1024]{1,0:T(8,128)}, bf16[256,128]{1,0:T(8,128)(2,1)}, /*index=5*/f32[16,1024]{1,0:T(8,128)S(1)}) custom-call(s32[1]{0:T(128)} %bitcast.refs_0_, bf16[128,896]{1,0:T(8,128)(2,1)S(1)} %bitcast.21, ...), custom_call_target="tpu_custom_call" | custom-call | tf_op jit(solution)/shard_map/pallas_call | solution.py:174
  81.3 1.6 %collective-permute-done.3.refs_3_ = f32[16,1024]{1,0:T(8,128)S(1)} collective-permute-done((f32[16,1024]{1,0:T(8,128)S(1)}, f32[16,1024]{1,0:T(8,128)S(1)}, u32[]{:S(2)}, u32[]{:S(2)}) %collective-permute-start.3) | collective-permute-done | bytes 65568 | tf_op jit(solution)/shard_map/ppermute | solution.py:26
  83.4 1.2 %shard_map.224 = bf16[512,1024]{1,0:T(8,128)(2,1)} custom-call(bf16[384,1024]{1,0:T(8,128)(2,1)S(1)} %get-tuple-element.74.refs_0_, bf16[384,1024]{1,0:T(8,128)(2,1)S(1)} %collective-permute-done.2.refs_1_, f32[16,1024]{1,0:T(8,128)S(1)} %get-tuple-element.76.refs_2_, f32[16,1024]{1,0:T(8,128)S(1)} %collective-permute-done.3.refs_3_), custom_call_target="tpu_custom_call" | custom-call | tf_op jit(solution)/shard_map/pallas_call | solution.py:174
  84.6 3.6 %all-to-all-start.4 = ((bf16[8,64,1024]{2,1,0:T(8,128)(2,1)}), bf16[8,64,1024]{2,1,0:T(8,128)(2,1)S(1)}, u32[]{:S(2)}, u32[]{:S(2)}) async-start(bf16[8,64,1024]{2,1,0:T(8,128)(2,1)} %bitcast.24), calls=%async_computation.4 | async-start | bytes 2097152 | tf_op jit(solution)/shard_map/all_to_all | solution.py:651
  88.2 2.0 %collective-permute-start.1 = (f32[8,1024]{1,0:T(8,128)S(1)}, f32[8,1024]{1,0:T(8,128)S(1)}, u32[]{:S(2)}, u32[]{:S(2)}) collective-permute-start(f32[8,1024]{1,0:T(8,128)S(1)} %copy-done.6), channel_id=1, source_target_pairs={{0,1},{1,2},{2,3},{3,4},{4,5},{5,6},{6,7},{7,8},{8,9},{9,10},{10,1... | collective-permute-start | bytes 98312 | tf_op jit(solution)/shard_map/ppermute | solution.py:32
  91.1 3.5 %shard_map.223 = bf16[256,768]{1,0:T(8,128)(2,1)} custom-call(f32[8,1024]{1,0:T(8,128)S(1)} %collective-permute-done.1.refs_0_, f32[256,1024]{1,0:T(8,128)} %get-tuple-element.72.refs_1_, f32[4,1024]{1,0:T(4,128)} %refs_2_.4, bf16[256,128]{1,0:T(8,128)(2,1)} %get-tuple-element.73.refs_3_, bf16[12,768]{1,0:T(8,128)(2,1)} %bitcast.29, bf16[768,1024]{1,0:T(8,128)(2,1)} %refs_5_.5), custom_call_target="tpu_custom_call" | custom-call | tf_op jit(solution)/shard_map/pallas_call | solution.py:174
  94.6 19.9 %all-to-all-done.4.refs_1_ = bf16[8,64,1024]{2,1,0:T(8,128)(2,1)S(1)} async-done(((bf16[8,64,1024]{2,1,0:T(8,128)(2,1)}), bf16[8,64,1024]{2,1,0:T(8,128)(2,1)S(1)}, u32[]{:S(2)}, u32[]{:S(2)}) %all-to-all-start.4) | async-done | bytes 1048608 | tf_op jit(solution)/shard_map/all_to_all | solution.py:651
  114.5 1.3 %shard_map.225 = (f32[48,1024]{1,0:T(8,128)}, f32[4,1024]{1,0:T(4,128)}, f32[12,768]{1,0:T(8,128)}, f32[3,12]{1,0:T(4,128)}, f32[768]{0:T(1024)}, /*index=5*/f32...) custom-call(s32[1]{0:T(128)} %bitcast.refs_0_, bf16[8,64,1024]{2,1,0:T(8,128)(2,1)S(1)} %all-to-all-done.4.refs_1_, ...), custom_call_target="tpu_custom_call" | custom-call | tf_op jit(solution)/shard_map/pallas_call | solution.py:174
  (21 shorter events, 6.1 us)
Async XLA Ops:
  1.4 4.0 %collective-permute-start = (bf16[8,768]{1,0:T(8,128)(2,1)S(1)}, bf16[8,768]{1,0:T(8,128)(2,1)S(1)}, u32[]{:S(2)}, u32[]{:S(2)}) collective-permute-start(bf16[8,768]{1,0:T(8,128)(2,1)S(1)} %slice.3), channel_id=1, source_target_pairs={{1,0},{2,1},{3,2},{4,3},{5,4},{6,5},{7,6},{8,7},{9,8},{10,9},{11,1... | collective-permute-start | bytes 36872 | tf_op jit(solution)/shard_map/ppermute | solution.py:32
  10.0 17.7 %all-to-all-start = ((bf16[16,8,896]{2,1,0:T(8,128)(2,1)}), bf16[16,8,896]{2,1,0:T(8,128)(2,1)S(1)}, u32[]{:S(2)}, u32[]{:S(2)}) async-start(bf16[16,8,896]{2,1,0:T(8,128)(2,1)} %bitcast.25), calls=%async_computation | async-start | bytes 458752 | tf_op jit(solution)/shard_map/all_to_all | solution.py:596
  29.1 12.5 %all-to-all-start.1 = ((bf16[16,8,768]{2,1,0:T(8,128)(2,1)}), bf16[16,8,768]{2,1,0:T(8,128)(2,1)S(1)}, u32[]{:S(2)}, u32[]{:S(2)}) async-start(bf16[16,8,768]{2,1,0:T(8,128)(2,1)} %get-tuple-element.53), calls=%async_computation.1 | async-start | bytes 393216 | tf_op jit(solution)/shard_map/all_to_all | solution.py:596
  35.1 0.7 copy-start.3
  41.6 0.9 copy-start.4
  46.5 3.7 %copy-start.1 = (f32[256,128]{1,0:T(8,128)}, f32[256,128]{1,0:T(8,128)S(1)}, u32[]{:S(2)}) copy-start(f32[256,128]{1,0:T(8,128)S(1)} %get-tuple-element.60.refs_6_) | copy-start | bytes 393220
  46.5 12.5 %all-to-all-start.2 = ((bf16[16,8,768]{2,1,0:T(8,128)(2,1)}), bf16[16,8,768]{2,1,0:T(8,128)(2,1)S(1)}, u32[]{:S(2)}, u32[]{:S(2)}) async-start(bf16[16,8,768]{2,1,0:T(8,128)(2,1)} %bitcast.26), calls=%async_computation.2 | async-start | bytes 393216 | tf_op jit(solution)/shard_map/all_to_all | solution.py:596
  50.2 0.9 copy-start.2
  60.1 13.1 %all-to-all-start.3 = ((bf16[16,8,896]{2,1,0:T(8,128)(2,1)}), bf16[16,8,896]{2,1,0:T(8,128)(2,1)S(1)}, u32[]{:S(2)}, u32[]{:S(2)}) async-start(bf16[16,8,896]{2,1,0:T(8,128)(2,1)} %shard_map.221), calls=%async_computation.3 | async-start | bytes 458752 | tf_op jit(solution)/shard_map/all_to_all | solution.py:596
  80.7 2.7 %collective-permute-start.2 = (bf16[384,1024]{1,0:T(8,128)(2,1)}, bf16[384,1024]{1,0:T(8,128)(2,1)S(1)}, u32[]{:S(2)}, u32[]{:S(2)}) collective-permute-start(bf16[384,1024]{1,0:T(8,128)(2,1)} %get-tuple-element.75), channel_id=1, source_target_pairs={{0,1},{1,0},{2,3},{3,2},{4,5},{5,4},{6,7},{7,6},{8,9},{9,8},{10,11... | collective-permute-start | bytes 2359304 | tf_op jit(solution)/shard_map/ppermute | solution.py:26
  80.8 2.1 %collective-permute-start.3 = (f32[16,1024]{1,0:T(8,128)S(1)}, f32[16,1024]{1,0:T(8,128)S(1)}, u32[]{:S(2)}, u32[]{:S(2)}) collective-permute-start(f32[16,1024]{1,0:T(8,128)S(1)} %get-tuple-element.76.refs_2_), channel_id=1, source_target_pairs={{0,1},{1,0},{2,3},{3,2},{4,5},{5,4},{6,7},{7,6},{8,9},{9,8},{10,11... | collective-permute-start | bytes 196616 | tf_op jit(solution)/shard_map/ppermute | solution.py:26
  84.6 3.6 %copy-start.6 = (f32[8,1024]{1,0:T(8,128)S(1)}, f32[8,1024]{1,0:T(8,128)}, u32[]{:S(2)}) copy-start(f32[8,1024]{1,0:T(8,128)} %get-tuple-element.71) | copy-start | bytes 98308
  84.6 29.8 %all-to-all-start.4 = ((bf16[8,64,1024]{2,1,0:T(8,128)(2,1)}), bf16[8,64,1024]{2,1,0:T(8,128)(2,1)S(1)}, u32[]{:S(2)}, u32[]{:S(2)}) async-start(bf16[8,64,1024]{2,1,0:T(8,128)(2,1)} %bitcast.24), calls=%async_computation.4 | async-start | bytes 2097152 | tf_op jit(solution)/shard_map/all_to_all | solution.py:651
  88.2 2.9 %collective-permute-start.1 = (f32[8,1024]{1,0:T(8,128)S(1)}, f32[8,1024]{1,0:T(8,128)S(1)}, u32[]{:S(2)}, u32[]{:S(2)}) collective-permute-start(f32[8,1024]{1,0:T(8,128)S(1)} %copy-done.6), channel_id=1, source_target_pairs={{0,1},{1,2},{2,3},{3,4},{4,5},{5,6},{6,7},{7,8},{8,9},{9,10},{10,1... | collective-permute-start | bytes 98312 | tf_op jit(solution)/shard_map/ppermute | solution.py:32
  91.1 23.4 %copy-start = (bf16[768,768]{1,0:T(8,128)(2,1)S(1)}, bf16[768,768]{1,0:T(8,128)(2,1)}, u32[]{:S(2)}) copy-start(bf16[768,768]{1,0:T(8,128)(2,1)} %refs_2_.5) | copy-start | bytes 3538948
  91.1 23.4 %copy-start.5 = (bf16[768,16]{0,1:T(8,128)(2,1)S(1)}, bf16[768,16]{0,1:T(8,128)(2,1)}, u32[]{:S(2)}) copy-start(bf16[768,16]{0,1:T(8,128)(2,1)} %param.24) | copy-start | bytes 73732

commit v5 on v4

--- a/solution.py
+++ b/solution.py
@@ -118,7 +118,7 @@
         pass
 
 
-def call(body, outs, *args, scratch=(), scalars=0, fetch=(), leave=(), after=(), wait=()):
+def call(body, outs, *args, scratch=(), scalars=0, fetch=(), leave=(), after=(), wait=(), into=()):
     waits = len(after) + len(wait)
     fetch = sorted(fetch)
 
@@ -133,7 +133,8 @@
         inputs = take(len(args))
         take(waits)
         results = take(len(outs))
-        places, outputs, extra = take(len(fetch)), take(len(leave)), take(len(scratch))
+        places, outputs, extra = take(len(fetch) - len(into)), take(len(leave)), take(len(scratch))
+        places = places + results[len(results) - len(into) :]
         arrivals, departures = refs
         for i, (at, place) in enumerate(zip(fetch, places)):
             copy = pltpu.make_async_copy(inputs[at], place, arrivals.at[i])
@@ -177,7 +178,7 @@
         in_specs=specs,
         out_specs=[pl.BlockSpec(memory_space=far if i in leave else close) for i in range(len(outs))],
         scratch_shapes=[
-            *(pltpu.VMEM(args[i].shape, args[i].dtype) for i in fetch),
+            *(pltpu.VMEM(args[i].shape, args[i].dtype) for i in fetch[: len(fetch) - len(into)]),
             *(pltpu.VMEM(*outs[i]) for i in leave),
             *scratch,
             pltpu.SemaphoreType.DMA((max(len(fetch), 1),)),
@@ -192,7 +193,7 @@
     return sum(dot(part, place) for part in pieces(x, 3))
 
 
-def teacher_kernel(slice_rows, rows, weights, dest, start, size, extra, own):
+def teacher_kernel(slice_rows, rows, weights, dest, start, size, hidden, w_in, extra, own, *brought):
     count = rows.shape[0]
     row, lane = iota((count, count), 0), iota((count, count), 1)
     named = dest[...].astype(F32)
@@ -267,6 +268,10 @@
     message, mixed_o, raw_o, step_o, run_o, run_t, raw,
 ):
     length = hidden.shape[0]
+    weights = w_in[...]
+    raw_o[0:length, :] = dot(hidden[...], weights).astype(BF16)
+    raw_o[length:, :] = dot(edge[...], weights).astype(BF16)
+    raw_o.send()
     wide = (iota((LANES, HEADS), 0) == iota((LANES, HEADS), 1)).astype(BF16)
     w_dt_wide = dot(wide, w_dt[...]).astype(BF16)
     before = dot(hidden[...], w_dt_wide, 1, 1) + widened(dt_bias[...])
@@ -281,10 +286,6 @@
     run_t[...] = run.T
     for result in (step_o, run_o, run_t):
         result.send()
-    weights = w_in[...]
-    raw_o[0:length, :] = dot(hidden[...], weights).astype(BF16)
-    raw_o[length:, :] = dot(edge[...], weights).astype(BF16)
-    raw_o.send()
     raw[...] = raw_o[...].astype(F32)
     conv = convolved(raw, conv_w, length)
     mixed = (conv / (1.0 + jnp.exp(-conv))).astype(BF16)
@@ -308,7 +309,10 @@
     return jnp.exp(jnp.where(top_seen, top, FAR)), jnp.exp(jnp.where(low_seen, low, FAR))
 
 
-def local_kernel(mixed, step, run, run_t, local):
+def local_kernel(
+    mixed, step, run, run_t, d_skip, raw_b, conv_w, hidden,
+    local, slope, tail_values, tail_steps, tail_weighted, hidden_t, raw,
+):
     length = mixed.shape[0]
     half = length // 2
     width = HEADS * HDIM
@@ -328,6 +332,22 @@
             lows.append(dot((low * low_scores).astype(BF16), own[half:]))
         local[0:half, lanes] = jnp.where(first, tops[0], tops[1])
         local[half:, lanes] = jnp.where(first, lows[0], lows[1])
+    local[...] = local[...] + spread_heads(d_skip[...]) * mixed[:, :width].astype(F32)
+    hidden_t[...] = hidden[...].astype(F32).T.astype(BF16)
+    hidden_t.send()
+    tail = spread_heads(jnp.exp(run[0:1, :] - run[...]))
+    steps = spread_heads(step[:, 0:LANES])
+    reaching = tail * mixed[:, :width].astype(F32)
+    tail_values[...] = reaching
+    tail_values.send()
+    tail_steps[...] = tail * steps
+    tail_steps.send()
+    tail_weighted[...] = (reaching * steps).astype(BF16)
+    tail_weighted.send()
+    raw[...] = raw_b[...].astype(F32)
+    inner = convolved(raw, conv_w, length)
+    gate = 1.0 / (1.0 + jnp.exp(-inner))
+    slope[...] = gate * (1.0 + inner * (1.0 - gate))
 
 
 def states_kernel(arrived, onward, decay):
@@ -355,7 +375,7 @@
 
 
 def middle_kernel(
-    state, mixed, run, local, d_skip, gains, high, low, target,
+    state, mixed, run, local, gains, high, low, target,
     back_state, grad_scanned, normed_o, logits_o, run_grad, small,
 ):
     length = mixed.shape[0]
@@ -364,11 +384,10 @@
     out_map = mixed[:, width + STATE :]
     reach = spread_heads(jnp.exp(run[...]))
     carried = dot(out_map, state[...]) * reach
-    gain = gains[...].reshape(1, width)
-    skip = spread_heads(d_skip[...])
-    scanned = local[...] + carried + skip * values
+    scanned = local[...] + carried
     scale = lax.rsqrt(jnp.mean(scanned * scanned, axis=1, keepdims=True) + EPSILON)
     plain = scanned * scale
+    gain = gains[...].reshape(1, width)
     normed = (plain * gain).astype(BF16)
     normed_o[...] = normed
     normed_o.send()
@@ -491,32 +510,28 @@
 
 
 def last_kernel(
-    blocks, place, state_grad, edge, run, mixed, step, state, run_grad, step_local, a_log, conv_w,
-    values_local, maps, raw_b, hidden, small, own,
+    blocks, place, state_grad, edge, run, mixed, step, state, run_grad,
+    tail_values, tail_weighted, step_local, a_log, conv_w, tail_steps, values_local, maps, slope, hidden_t,
+    raw_b, small, own,
     keep, send, rim, back_raw_o, step_grad_o, late, full, padded, raw,
 ):
     length = mixed.shape[0]
     taps = conv_w.shape[0]
     width = HEADS * HDIM
     total = run[0:1, :]
-    tail = spread_heads(jnp.exp(total - run[...]))
-    values = mixed[:, :width].astype(F32)
     in_map = mixed[:, width : width + STATE]
     incoming = state_grad[:, :width]
-    reached = dot(in_map, incoming) * tail
-    steps = spread_heads(step[:, 0:LANES])
-    weighted = values * steps
-    reaching = head_sums(reached * values)
-    ended = reaching * step[:, 0:LANES]
-    in_grad = dot((weighted * tail).astype(BF16), incoming, 1, 1)
+    reached = dot(in_map, incoming)
     product = jnp.sum(incoming.astype(F32) * state[...].astype(F32), axis=0, keepdims=True)
     total_grad = jnp.exp(total) * head_sums(jnp.broadcast_to(product, (8, width)))[0:1]
     row, column = iota((length, length), 0), iota((length, length), 1)
-    decay_grad = (
-        finer((column <= row).astype(BF16), run_grad[...], 3)
-        + finer((column > row).astype(BF16), ended, 3)
-        + total_grad
-    )
+    decay_grad = finer((column <= row).astype(BF16), run_grad[...], 3) + total_grad
+    padded[0:HALO, :] = jnp.zeros((HALO, padded.shape[1]), F32)
+    padded[HALO + length :, :] = jnp.zeros((HALO, padded.shape[1]), F32)
+    reaching = head_sums(reached * tail_values[...])
+    ended = reaching * step[:, 0:LANES]
+    in_grad = dot(tail_weighted[...], incoming, 1, 1)
+    decay_grad = decay_grad + finer((column > row).astype(BF16), ended, 3)
     rate = jnp.exp(widened(a_log[...]))
     step_grad = step_local[...] + reaching - rate * decay_grad
     before = step[:, LANES:]
@@ -525,14 +540,8 @@
     )
     step_grad_b = step_grad.astype(BF16)
     step_grad_o[...] = step_grad_b
-    raw[...] = raw_b[...].astype(F32)
-    padded[0:HALO, :] = jnp.zeros((HALO, padded.shape[1]), F32)
-    padded[HALO + length :, :] = jnp.zeros((HALO, padded.shape[1]), F32)
-    inner = convolved(raw, conv_w, length)
-    gate = 1.0 / (1.0 + jnp.exp(-inner))
-    slope = gate * (1.0 + inner * (1.0 - gate))
     middle = slice(HALO, HALO + length)
-    padded[middle, 0:width] = (values_local[...] + reached * steps) * slope[:, 0:width]
+    padded[middle, 0:width] = (values_local[...] + reached * tail_steps[...]) * slope[:, 0:width]
     padded[middle, width : width + STATE] = (maps[:, 0:STATE] + in_grad) * slope[
         :, width : width + STATE
     ]
@@ -543,20 +552,20 @@
     for tap in range(taps):
         back_raw = back_raw + conv_w[tap : tap + 1, :] * padded[pl.ds(HALO - tap, length + HALO), :]
     back_raw_o[...] = back_raw[0:length]
+    full[...] = dot(hidden_t[...], back_raw[0:length].astype(BF16)) + dot(
+        edge[...], back_raw[length:].astype(BF16), 0, 0
+    )
+    halves(full, keep, send, place[0] % 2, blocks)
+    send.send()
     back_raw_o.send()
-    full[...] = dot(hidden[...], back_raw[0:length].astype(BF16), 0, 0) + dot(
-        edge[...], back_raw[length:].astype(BF16), 0, 0
-    )
-    halves(full, keep, send, place[0] % 2, blocks)
-    keep.send()
-    send.send()
     back_conv = padded[middle, :]
+    raw[...] = raw_b[...].astype(F32)
     spare = late.shape[0] - taps
     for tap in range(taps):
         late[spare + tap : spare + tap + 1, :] = jnp.sum(
             back_conv * raw[pl.ds(tap, length), :], axis=0, keepdims=True
         )
-    late[0:HEADS, 0:width] = dot(step_grad_b, hidden[...], 0, 0)[0:HEADS]
+    late[0:HEADS, 0:width] = dot(step_grad_b, hidden_t[...], 0, 1)[0:HEADS]
     late[0:HEADS, width:] = jnp.zeros((HEADS, late.shape[1] - width), F32)
     log_decay = -step[:, 0:LANES] * rate
     facts = jnp.sum(step_grad, axis=0, keepdims=True)
@@ -667,12 +676,17 @@
     place = lax.axis_index("seq").astype(jnp.int32).reshape(1)
 
     edge = passed_along(hidden_in[:HALO], "seq", -1)
-    extra, own = call(
+    extra, own, hidden_near, w_in_near = call(
         functools.partial(teacher_kernel, slice_rows),
-        [((STATE, LANES), BF16), ((1, LANES), F32)],
+        [
+            ((STATE, LANES), BF16),
+            ((1, LANES), F32),
+            (hidden_in.shape, BF16),
+            (w_in.shape, BF16),
+        ],
         teacher_rows, w_teacher.T, row_dest.reshape(1, row_count),
-        row_start.reshape(1, row_count), row_len.reshape(1, row_count),
-        fetch=range(5), leave=(1,),
+        row_start.reshape(1, row_count), row_len.reshape(1, row_count), hidden_in, w_in,
+        fetch=range(7), leave=(1,), into=(5, 6),
     )
     w_dt_t = w_dt.T
     a_log_row = a_log.reshape(1, HEADS)
@@ -687,11 +701,24 @@
             ((length, LANES), F32),
             ((LANES, length), F32),
         ],
-        edge, hidden_in, w_dt_t, dt_bias.reshape(1, HEADS), a_log_row, w_in, conv_w, extra,
-        scratch=[pltpu.VMEM((length + HALO, channels), F32)], fetch=range(1, 7), leave=(0, 2),
+        edge, hidden_near, w_dt_t, dt_bias.reshape(1, HEADS), a_log_row, w_in_near, conv_w, extra,
+        scratch=[pltpu.VMEM((length + HALO, channels), F32)], fetch=(2, 3, 4, 6), leave=(0, 2),
     )
     arrived = swapped(message).reshape(devices, slice_rows, width + LANES)
-    (local,) = call(local_kernel, [((length, width), F32)], mixed, step, run, run_t)
+    local, slope, tail_values, tail_steps, tail_weighted, hidden_t = call(
+        local_kernel,
+        [
+            ((length, width), F32),
+            ((length, channels), F32),
+            ((length, width), F32),
+            ((length, width), F32),
+            ((length, width), BF16),
+            ((hidden_in.shape[1], length), BF16),
+        ],
+        mixed, step, run, run_t, skip_row, raw, conv_w, hidden_in,
+        scratch=[pltpu.VMEM((length + HALO, channels), F32)],
+        fetch=(4, 5, 6, 7), leave=(1, 2, 3, 4, 5),
+    )
     onward, decay = call(
         states_kernel,
         [((devices, slice_rows, width), BF16), ((devices, slice_rows, LANES), F32)],
@@ -704,7 +731,7 @@
         target_kernel,
         [((length, LANES), F32), ((LANES, width), BF16), ((LANES, width), BF16)],
         arrived, w_cls.T, w_out,
-        fetch=(1, 2),
+        fetch=(1, 2), leave=(0,),
     )
 
     back_state, grad_scanned, normed, back_logits, carried_grad, small = call(
@@ -717,8 +744,8 @@
             ((length, LANES), F32),
             ((8, width), F32),
         ],
-        state, mixed, run, local, skip_row, norm_gain, labels_high, labels_low, target,
-        fetch=(4, 5), leave=(0, 2, 3, 5),
+        state, mixed, run, local, norm_gain, labels_high, labels_low, target,
+        fetch=(4, 7), leave=(0, 2, 3, 5),
     )
     back_arrived = swapped(back_state).reshape(devices, slice_rows, width)
     values_local, maps, run_grad, step_local, early = call(
@@ -751,14 +778,15 @@
             ((length, LANES), BF16),
             ((HEADS + conv_w.shape[0], channels), F32),
         ],
-        place, state_grad, edge, run, mixed, step, state, run_grad, step_local, a_log_row, conv_w,
-        values_local, maps, raw, hidden_in, small, own,
+        place, state_grad, edge, run, mixed, step, state, run_grad,
+        tail_values, tail_weighted, step_local, a_log_row, conv_w, tail_steps, values_local, maps, slope,
+        hidden_t, raw, small, own,
         scratch=[
             pltpu.VMEM((width, channels), F32),
             pltpu.VMEM((length + 2 * HALO, channels), F32),
             pltpu.VMEM((length + HALO, channels), F32),
         ],
-        scalars=1, fetch=(8, 9, 10, 12, 13, 14, 15, 16), leave=(1, 2, 3, 4),
+        scalars=1, fetch=(8, 9, 10, 11, 12, 13, 15, 16, 17, 18, 19, 20), leave=(1, 2, 3, 4),
     )
     chips = devices // 2
     (both_in,) = call(

time: 118 us -> 116 us (0.983)
  waiting for transfers between devices: 48.7 us -> 45.8 us
  Pallas kernels: 36.6 us -> 38.8 us
  local copies, waits for them, and re-layouts: 3.18 us -> 1.63 us
    all_to_all x4, waiting for transfers between devices: 25.8 us -> 23 us  [swapped(): return lax.all_to_all(x, axis, split_axis=0, concat_axis=0, tiled=True)]
    pallas_call x12, Pallas kernels: 36.6 us -> 38.8 us  [call(): pl.pallas_call(kernel, out_shape=[(far if i in leave else close)(*out) fo...]
    unnamed x14 -> x10, local copies, waits for them, and re-layouts: 2.47 us -> 0.92 us
  transfers between devices with their start and end apart: 9 -> 9, of which waited for: 8 -> 8; matrix products, arithmetic and copies ran while one was open for 0% -> 0% of each run, Pallas kernels for 13% -> 17%
where the time goes in v5:
time: 116 us; the launch traced here: 114 us
  waiting for transfers between devices  45.8 us (39%)
  Pallas kernels  38.8 us (33%)
  starting transfers between devices  26.4 us (23%)
  local copies, waits for them, and re-layouts  1.63 us (1%)
    pallas_call x12, Pallas kernels, call(): pl.pallas_call(kernel, out_shape=[(far if i in leave else close)(*out) fo...  38.8 us
    all_to_all x4, waiting for transfers between devices, swapped(): return lax.all_to_all(x, axis, split_axis=0, concat_axis=0, tiled=True)  23 us
    all_to_all x1, waiting for transfers between devices, exchanged(): lax.all_to_all(both, 'seq', split_axis=0, concat_axis=0, axis_index_group...  19.9 us
    all_to_all x4, starting transfers between devices, swapped(): return lax.all_to_all(x, axis, split_axis=0, concat_axis=0, tiled=True)  19 us
    all_to_all x1, starting transfers between devices, exchanged(): lax.all_to_all(both, 'seq', split_axis=0, concat_axis=0, axis_index_group...  3.57 us
    ppermute x2, starting transfers between devices, passed_along(): return lax.ppermute(x, axis, pairs)  3.32 us
  transfers between devices with their start and end apart: 9, of which 8 were waited for; matrix products, arithmetic and copies ran while one was open for 0% of the time, Pallas kernels for 17%

profile of v5, /device:TPU:0, one launch (start us, length us, event | category | flops | bytes accessed | tf_op | source)
XLA Modules:
  0.0 113.7 jit_solution(5766942546259706800)
XLA Ops:
  1.4 1.3 %collective-permute-start = (bf16[8,768]{1,0:T(8,128)(2,1)S(1)}, bf16[8,768]{1,0:T(8,128)(2,1)S(1)}, u32[]{:S(2)}, u32[]{:S(2)}) collective-permute-start(bf16[8,768]{1,0:T(8,128)(2,1)S(1)} %slice.3), channel_id=1, source_target_pairs={{1,0},{2,1},{3,2},{4,3},{5,4},{6,5},{7,6},{8,7},{9,8},{10,9},{11,1... | collective-permute-start | bytes 36872 | tf_op jit(solution)/shard_map/ppermute | solution.py:32
  2.6 2.9 %shard_map.214 = (bf16[128,128]{1,0:T(8,128)(2,1)S(1)}, f32[1,128]{1,0:T(1,128)}, bf16[256,768]{1,0:T(8,128)(2,1)S(1)}, bf16[768,1024]{1,0:T(8,128)(2,1)S(1)}) custom-call(bf16[128,4096]{1,0:T(8,128)(2,1)} %refs_0_.1, bf16[16,4096]{1,0:T(8,128)(2,1)} %bitcast.27, s32[1,128]{1,0:T(1,128)} %bitcast.34, s32[1,128]{1,0:T(1,128)} %bitcast.35, s32[1,128]{1,0:T(1,128)} %bitcast.36, ...), custom_call_target="tpu_custom_call" | custom-call | tf_op jit(solution)/shard_map/pallas_call | solution.py:175
  5.5 4.2 %shard_map.215 = (bf16[128,896]{1,0:T(8,128)(2,1)}, bf16[256,1024]{1,0:T(8,128)(2,1)S(1)}, bf16[264,1024]{1,0:T(8,128)(2,1)}, f32[256,256]{1,0:T(8,128)S(1)}, f3...) custom-call(bf16[8,768]{1,0:T(8,128)(2,1)S(1)} %collective-permute-done.refs_0_.refs_2_, ...), custom_call_target="tpu_custom_call" | custom-call | tf_op jit(solution)/shard_map/pallas_call | solution.py:175
  9.7 8.1 %all-to-all-start = ((bf16[16,8,896]{2,1,0:T(8,128)(2,1)}), bf16[16,8,896]{2,1,0:T(8,128)(2,1)S(1)}, u32[]{:S(2)}, u32[]{:S(2)}) async-start(bf16[16,8,896]{2,1,0:T(8,128)(2,1)} %bitcast.25), calls=%async_computation | async-start | bytes 458752 | tf_op jit(solution)/shard_map/all_to_all | solution.py:605
  17.8 5.2 %shard_map.216 = (f32[256,768]{1,0:T(8,128)S(1)}, f32[256,1024]{1,0:T(8,128)}, f32[256,768]{1,0:T(8,128)}, f32[256,768]{1,0:T(8,128)}, bf16[256,768]{1,0:T(8,128)(2,1)}, /*index=5*/bf16[768,256]{1,0:T(8,128)(2,1)}) custom-call(bf16[256,1024]{1,0:T(8,128)(2,1)S(1)} %get-tuple-element.59.refs_0_.refs_1_.refs_4_, ...), custom_call_target="tpu_custom_call" | custom-call | tf_op jit(solution)/shard_map/pallas_call | solution.py:175
  23.1 4.3 %all-to-all-done.refs_0_ = bf16[16,8,896]{2,1,0:T(8,128)(2,1)S(1)} async-done(((bf16[16,8,896]{2,1,0:T(8,128)(2,1)}), bf16[16,8,896]{2,1,0:T(8,128)(2,1)S(1)}, u32[]{:S(2)}, u32[]{:S(2)}) %all-to-all-start) | async-done | bytes 229408 | tf_op jit(solution)/shard_map/all_to_all | solution.py:605
  27.4 1.5 %shard_map.217 = (bf16[16,8,768]{2,1,0:T(8,128)(2,1)}, f32[16,8,128]{2,1,0:T(8,128)S(1)}) custom-call(bf16[16,8,896]{2,1,0:T(8,128)(2,1)S(1)} %all-to-all-done.refs_0_, f32[256,768]{1,0:T(8,128)S(1)} %get-tuple-element.64.refs_1_.refs_3_), custom_call_target="tpu_custom_call" | custom-call | tf_op jit(solution)/shard_map/pallas_call | solution.py:175
  28.9 3.5 %all-to-all-start.1 = ((bf16[16,8,768]{2,1,0:T(8,128)(2,1)}), bf16[16,8,768]{2,1,0:T(8,128)(2,1)S(1)}, u32[]{:S(2)}, u32[]{:S(2)}) async-start(bf16[16,8,768]{2,1,0:T(8,128)(2,1)} %get-tuple-element.65), calls=%async_computation.1 | async-start | bytes 393216 | tf_op jit(solution)/shard_map/all_to_all | solution.py:605
  32.4 2.0 %shard_map.218 = (f32[256,128]{1,0:T(8,128)}, bf16[128,768]{1,0:T(8,128)(2,1)S(1)}, bf16[128,768]{1,0:T(8,128)(2,1)S(1)}) custom-call(bf16[16,8,896]{2,1,0:T(8,128)(2,1)S(1)} %all-to-all-done.refs_0_, bf16[16,768]{1,0:T(8,128)(2,1)} %bitcast.22, bf16[768,768]{1,0:T(8,128)(2,1)} %refs_2_.5), custom_call_target="tpu_custom_call" | custom-call | tf_op jit(solution)/shard_map/pallas_call | solution.py:175
  34.4 7.0 %all-to-all-done.1 = bf16[16,8,768]{2,1,0:T(8,128)(2,1)S(1)} async-done(((bf16[16,8,768]{2,1,0:T(8,128)(2,1)}), bf16[16,8,768]{2,1,0:T(8,128)(2,1)S(1)}, u32[]{:S(2)}, u32[]{:S(2)}) %all-to-all-start.1) | async-done | bytes 196640 | tf_op jit(solution)/shard_map/all_to_all | solution.py:605
  41.4 4.1 %shard_map.219 = (bf16[128,768]{1,0:T(8,128)(2,1)}, f32[256,768]{1,0:T(8,128)S(1)}, bf16[256,768]{1,0:T(8,128)(2,1)}, f32[256,128]{1,0:T(8,128)}, f32[256,128]{1,0:T(8,128)S(1)}, /*index=5*/f32[8,768]{1,0:T(8,128)}) custom-call(bf16[128,768]{1,0:T(8,128)(2,1)S(1)} %bitcast.18, bf16[256,1024]{1,0:T(8,128)(2,1)S(1)} %get-tuple-element.59.refs_0_.refs_1_.refs_4_, ...), custom_call_target="tpu_custom_call" | custom-call | tf_op jit(solution)/shard_map/pallas_call | solution.py:175
  45.5 3.7 %all-to-all-start.2 = ((bf16[16,8,768]{2,1,0:T(8,128)(2,1)}), bf16[16,8,768]{2,1,0:T(8,128)(2,1)S(1)}, u32[]{:S(2)}, u32[]{:S(2)}) async-start(bf16[16,8,768]{2,1,0:T(8,128)(2,1)} %bitcast.26), calls=%async_computation.2 | async-start | bytes 393216 | tf_op jit(solution)/shard_map/all_to_all | solution.py:605
  50.1 5.6 %shard_map.220 = (f32[256,768]{1,0:T(8,128)S(1)}, f32[256,256]{1,0:T(8,128)}, f32[256,128]{1,0:T(8,128)S(1)}, f32[256,128]{1,0:T(8,128)}, f32[128,128]{1,0:T(8,128)S(1)}) custom-call(bf16[256,1024]{1,0:T(8,128)(2,1)S(1)} %get-tuple-element.59.refs_0_.refs_1_.refs_4_, f32[256,256]{1,0:T(8,128)S(1)} %get-tuple-element.60.refs_1_.refs_5_, ...), custom_call_target="tpu_custom_call" | custom-call | tf_op jit(solution)/shard_map/pallas_call | solution.py:175
  55.8 2.2 %all-to-all-done.2.refs_0_ = bf16[16,8,768]{2,1,0:T(8,128)(2,1)S(1)} async-done(((bf16[16,8,768]{2,1,0:T(8,128)(2,1)}), bf16[16,8,768]{2,1,0:T(8,128)(2,1)S(1)}, u32[]{:S(2)}, u32[]{:S(2)}) %all-to-all-start.2) | async-done | bytes 196640 | tf_op jit(solution)/shard_map/all_to_all | solution.py:605
  59.1 3.6 %all-to-all-start.3 = ((bf16[16,8,896]{2,1,0:T(8,128)(2,1)}), bf16[16,8,896]{2,1,0:T(8,128)(2,1)S(1)}, u32[]{:S(2)}, u32[]{:S(2)}) async-start(bf16[16,8,896]{2,1,0:T(8,128)(2,1)} %shard_map.221), calls=%async_computation.3 | async-start | bytes 458752 | tf_op jit(solution)/shard_map/all_to_all | solution.py:605
  62.7 9.5 %all-to-all-done.3 = bf16[16,8,896]{2,1,0:T(8,128)(2,1)S(1)} async-done(((bf16[16,8,896]{2,1,0:T(8,128)(2,1)}), bf16[16,8,896]{2,1,0:T(8,128)(2,1)S(1)}, u32[]{:S(2)}, u32[]{:S(2)}) %all-to-all-start.3) | async-done | bytes 229408 | tf_op jit(solution)/shard_map/all_to_all | solution.py:605
  72.2 6.2 %shard_map.222 = (bf16[384,1024]{1,0:T(8,128)(2,1)S(1)}, bf16[384,1024]{1,0:T(8,128)(2,1)}, f32[8,1024]{1,0:T(8,128)}, f32[256,1024]{1,0:T(8,128)}, bf16[256,128]{1,0:T(8,128)(2,1)}, /*index=5*/f32[16,1024]{1,0:T(8,128)S(1)}) custom-call(s32[1]{0:T(128)} %bitcast.refs_0_, bf16[128,896]{1,0:T(8,128)(2,1)S(1)} %bitcast.21, ...), custom_call_target="tpu_custom_call" | custom-call | tf_op jit(solution)/shard_map/pallas_call | solution.py:175
  79.0 1.6 %collective-permute-done.3.refs_3_ = f32[16,1024]{1,0:T(8,128)S(1)} collective-permute-done((f32[16,1024]{1,0:T(8,128)S(1)}, f32[16,1024]{1,0:T(8,128)S(1)}, u32[]{:S(2)}, u32[]{:S(2)}) %collective-permute-start.3) | collective-permute-done | bytes 65568 | tf_op jit(solution)/shard_map/ppermute | solution.py:26
  81.1 1.3 %shard_map.224 = bf16[512,1024]{1,0:T(8,128)(2,1)} custom-call(bf16[384,1024]{1,0:T(8,128)(2,1)S(1)} %get-tuple-element.90.refs_0_, bf16[384,1024]{1,0:T(8,128)(2,1)S(1)} %collective-permute-done.2.refs_1_, f32[16,1024]{1,0:T(8,128)S(1)} %get-tuple-element.92.refs_2_, f32[16,1024]{1,0:T(8,128)S(1)} %collective-permute-done.3.refs_3_), custom_call_target="tpu_custom_call" | custom-call | tf_op jit(solution)/shard_map/pallas_call | solution.py:175
  82.4 3.6 %all-to-all-start.4 = ((bf16[8,64,1024]{2,1,0:T(8,128)(2,1)}), bf16[8,64,1024]{2,1,0:T(8,128)(2,1)S(1)}, u32[]{:S(2)}, u32[]{:S(2)}) async-start(bf16[8,64,1024]{2,1,0:T(8,128)(2,1)} %bitcast.24), calls=%async_computation.4 | async-start | bytes 2097152 | tf_op jit(solution)/shard_map/all_to_all | solution.py:660
  85.9 2.0 %collective-permute-start.1 = (f32[8,1024]{1,0:T(8,128)S(1)}, f32[8,1024]{1,0:T(8,128)S(1)}, u32[]{:S(2)}, u32[]{:S(2)}) collective-permute-start(f32[8,1024]{1,0:T(8,128)S(1)} %copy-done.4), channel_id=1, source_target_pairs={{0,1},{1,2},{2,3},{3,4},{4,5},{5,6},{6,7},{7,8},{8,9},{9,10},{10,1... | collective-permute-start | bytes 98312 | tf_op jit(solution)/shard_map/ppermute | solution.py:32
  88.8 3.5 %shard_map.223 = bf16[256,768]{1,0:T(8,128)(2,1)} custom-call(f32[8,1024]{1,0:T(8,128)S(1)} %collective-permute-done.1.refs_0_, f32[256,1024]{1,0:T(8,128)} %get-tuple-element.88.refs_1_, f32[4,1024]{1,0:T(4,128)} %refs_2_.4, bf16[256,128]{1,0:T(8,128)(2,1)} %get-tuple-element.89.refs_3_, bf16[12,768]{1,0:T(8,128)(2,1)} %bitcast.29, bf16[768,1024]{1,0:T(8,128)(2,1)} %refs_5_.3), custom_call_target="tpu_custom_call" | custom-call | tf_op jit(solution)/shard_map/pallas_call | solution.py:175
  92.3 19.9 %all-to-all-done.4.refs_1_ = bf16[8,64,1024]{2,1,0:T(8,128)(2,1)S(1)} async-done(((bf16[8,64,1024]{2,1,0:T(8,128)(2,1)}), bf16[8,64,1024]{2,1,0:T(8,128)(2,1)S(1)}, u32[]{:S(2)}, u32[]{:S(2)}) %all-to-all-start.4) | async-done | bytes 1048608 | tf_op jit(solution)/shard_map/all_to_all | solution.py:660
  112.2 1.3 %shard_map.225 = (f32[48,1024]{1,0:T(8,128)}, f32[4,1024]{1,0:T(4,128)}, f32[12,768]{1,0:T(8,128)}, f32[3,12]{1,0:T(4,128)}, f32[768]{0:T(1024)}, /*index=5*/f32...) custom-call(s32[1]{0:T(128)} %bitcast.refs_0_, bf16[8,64,1024]{2,1,0:T(8,128)(2,1)S(1)} %all-to-all-done.4.refs_1_, ...), custom_call_target="tpu_custom_call" | custom-call | tf_op jit(solution)/shard_map/pallas_call | solution.py:175
  (17 shorter events, 4.6 us)
Async XLA Ops:
  1.4 4.2 %collective-permute-start = (bf16[8,768]{1,0:T(8,128)(2,1)S(1)}, bf16[8,768]{1,0:T(8,128)(2,1)S(1)}, u32[]{:S(2)}, u32[]{:S(2)}) collective-permute-start(bf16[8,768]{1,0:T(8,128)(2,1)S(1)} %slice.3), channel_id=1, source_target_pairs={{1,0},{2,1},{3,2},{4,3},{5,4},{6,5},{7,6},{8,7},{9,8},{10,9},{11,1... | collective-permute-start | bytes 36872 | tf_op jit(solution)/shard_map/ppermute | solution.py:32
  9.7 17.7 %all-to-all-start = ((bf16[16,8,896]{2,1,0:T(8,128)(2,1)}), bf16[16,8,896]{2,1,0:T(8,128)(2,1)S(1)}, u32[]{:S(2)}, u32[]{:S(2)}) async-start(bf16[16,8,896]{2,1,0:T(8,128)(2,1)} %bitcast.25), calls=%async_computation | async-start | bytes 458752 | tf_op jit(solution)/shard_map/all_to_all | solution.py:605
  28.9 12.5 %all-to-all-start.1 = ((bf16[16,8,768]{2,1,0:T(8,128)(2,1)}), bf16[16,8,768]{2,1,0:T(8,128)(2,1)S(1)}, u32[]{:S(2)}, u32[]{:S(2)}) async-start(bf16[16,8,768]{2,1,0:T(8,128)(2,1)} %get-tuple-element.65), calls=%async_computation.1 | async-start | bytes 393216 | tf_op jit(solution)/shard_map/all_to_all | solution.py:605
  45.5 3.7 %copy-start.1 = (f32[256,128]{1,0:T(8,128)}, f32[256,128]{1,0:T(8,128)S(1)}, u32[]{:S(2)}) copy-start(f32[256,128]{1,0:T(8,128)S(1)} %get-tuple-element.72.refs_6_) | copy-start | bytes 393220
  45.5 12.5 %all-to-all-start.2 = ((bf16[16,8,768]{2,1,0:T(8,128)(2,1)}), bf16[16,8,768]{2,1,0:T(8,128)(2,1)S(1)}, u32[]{:S(2)}, u32[]{:S(2)}) async-start(bf16[16,8,768]{2,1,0:T(8,128)(2,1)} %bitcast.26), calls=%async_computation.2 | async-start | bytes 393216 | tf_op jit(solution)/shard_map/all_to_all | solution.py:605
  49.2 0.9 copy-start.2
  59.1 13.1 %all-to-all-start.3 = ((bf16[16,8,896]{2,1,0:T(8,128)(2,1)}), bf16[16,8,896]{2,1,0:T(8,128)(2,1)S(1)}, u32[]{:S(2)}, u32[]{:S(2)}) async-start(bf16[16,8,896]{2,1,0:T(8,128)(2,1)} %shard_map.221), calls=%async_computation.3 | async-start | bytes 458752 | tf_op jit(solution)/shard_map/all_to_all | solution.py:605
  78.4 2.7 %collective-permute-start.2 = (bf16[384,1024]{1,0:T(8,128)(2,1)}, bf16[384,1024]{1,0:T(8,128)(2,1)S(1)}, u32[]{:S(2)}, u32[]{:S(2)}) collective-permute-start(bf16[384,1024]{1,0:T(8,128)(2,1)} %get-tuple-element.91), channel_id=1, source_target_pairs={{0,1},{1,0},{2,3},{3,2},{4,5},{5,4},{6,7},{7,6},{8,9},{9,8},{10,11... | collective-permute-start | bytes 2359304 | tf_op jit(solution)/shard_map/ppermute | solution.py:26
  78.5 2.1 %collective-permute-start.3 = (f32[16,1024]{1,0:T(8,128)S(1)}, f32[16,1024]{1,0:T(8,128)S(1)}, u32[]{:S(2)}, u32[]{:S(2)}) collective-permute-start(f32[16,1024]{1,0:T(8,128)S(1)} %get-tuple-element.92.refs_2_), channel_id=1, source_target_pairs={{0,1},{1,0},{2,3},{3,2},{4,5},{5,4},{6,7},{7,6},{8,9},{9,8},{10,11... | collective-permute-start | bytes 196616 | tf_op jit(solution)/shard_map/ppermute | solution.py:26
  82.3 3.6 %copy-start.4 = (f32[8,1024]{1,0:T(8,128)S(1)}, f32[8,1024]{1,0:T(8,128)}, u32[]{:S(2)}) copy-start(f32[8,1024]{1,0:T(8,128)} %get-tuple-element.87) | copy-start | bytes 98308
  82.4 29.8 %all-to-all-start.4 = ((bf16[8,64,1024]{2,1,0:T(8,128)(2,1)}), bf16[8,64,1024]{2,1,0:T(8,128)(2,1)S(1)}, u32[]{:S(2)}, u32[]{:S(2)}) async-start(bf16[8,64,1024]{2,1,0:T(8,128)(2,1)} %bitcast.24), calls=%async_computation.4 | async-start | bytes 2097152 | tf_op jit(solution)/shard_map/all_to_all | solution.py:660
  85.9 2.9 %collective-permute-start.1 = (f32[8,1024]{1,0:T(8,128)S(1)}, f32[8,1024]{1,0:T(8,128)S(1)}, u32[]{:S(2)}, u32[]{:S(2)}) collective-permute-start(f32[8,1024]{1,0:T(8,128)S(1)} %copy-done.4), channel_id=1, source_target_pairs={{0,1},{1,2},{2,3},{3,4},{4,5},{5,6},{6,7},{7,8},{8,9},{9,10},{10,1... | collective-permute-start | bytes 98312 | tf_op jit(solution)/shard_map/ppermute | solution.py:32
  88.8 23.4 %copy-start = (bf16[768,768]{1,0:T(8,128)(2,1)S(1)}, bf16[768,768]{1,0:T(8,128)(2,1)}, u32[]{:S(2)}) copy-start(bf16[768,768]{1,0:T(8,128)(2,1)} %refs_2_.5) | copy-start | bytes 3538948
  88.8 23.4 %copy-start.3 = (bf16[768,16]{0,1:T(8,128)(2,1)S(1)}, bf16[768,16]{0,1:T(8,128)(2,1)}, u32[]{:S(2)}) copy-start(bf16[768,16]{0,1:T(8,128)(2,1)} %param.24) | copy-start | bytes 73732

commit v6 on v5

--- a/solution.py
+++ b/solution.py
@@ -13,6 +13,7 @@
 LABELS = 16
 LANES = 128
 HALO = 8
+CHUNK = 64
 TAGS = 48
 FACTS = 40
 EPSILON = 1e-05
@@ -310,8 +311,8 @@
 
 
 def local_kernel(
-    mixed, step, run, run_t, d_skip, raw_b, conv_w, hidden,
-    local, slope, tail_values, tail_steps, tail_weighted, hidden_t, raw,
+    blocks, place, mixed, step, run, run_t, edge, d_skip, raw_b, conv_w, hidden,
+    local, slope, tail_values, tail_steps, tail_weighted, keep_t, send_t, raw, turned,
 ):
     length = mixed.shape[0]
     half = length // 2
@@ -333,8 +334,12 @@
         local[0:half, lanes] = jnp.where(first, tops[0], tops[1])
         local[half:, lanes] = jnp.where(first, lows[0], lows[1])
     local[...] = local[...] + spread_heads(d_skip[...]) * mixed[:, :width].astype(F32)
-    hidden_t[...] = hidden[...].astype(F32).T.astype(BF16)
-    hidden_t.send()
+    turned[:, 0:length] = hidden[...].astype(F32).T
+    rest = jnp.zeros((LANES - HALO, turned.shape[0]), F32)
+    turned[:, length:] = jnp.concatenate([edge[...].astype(F32), rest], axis=0).T
+    halves(turned, keep_t, send_t, place[0] % 2, blocks)
+    keep_t.send()
+    send_t.send()
     tail = spread_heads(jnp.exp(run[0:1, :] - run[...]))
     steps = spread_heads(step[:, 0:LANES])
     reaching = tail * mixed[:, :width].astype(F32)
@@ -510,10 +515,10 @@
 
 
 def last_kernel(
-    blocks, place, state_grad, edge, run, mixed, step, state, run_grad,
-    tail_values, tail_weighted, step_local, a_log, conv_w, tail_steps, values_local, maps, slope, hidden_t,
-    raw_b, small, own,
-    keep, send, rim, back_raw_o, step_grad_o, late, full, padded, raw,
+    blocks, place, state_grad, run, mixed, step, state, run_grad,
+    tail_values, tail_weighted, step_local, a_log, conv_w, tail_steps, values_local, maps, slope, send_t,
+    keep_t, hidden, raw_b, small, own,
+    keep, send, rim, back_raw_o, step_grad_o, late, padded, raw, back_raw_b,
 ):
     length = mixed.shape[0]
     taps = conv_w.shape[0]
@@ -541,31 +546,42 @@
     step_grad_b = step_grad.astype(BF16)
     step_grad_o[...] = step_grad_b
     middle = slice(HALO, HALO + length)
-    padded[middle, 0:width] = (values_local[...] + reached * tail_steps[...]) * slope[:, 0:width]
-    padded[middle, width : width + STATE] = (maps[:, 0:STATE] + in_grad) * slope[
-        :, width : width + STATE
-    ]
-    padded[middle, width + STATE :] = maps[:, STATE:] * slope[:, width + STATE :]
+    for at in range(0, length, CHUNK):
+        rows, moved = slice(at, at + CHUNK), slice(HALO + at, HALO + at + CHUNK)
+        padded[moved, 0:width] = (
+            values_local[rows, :] + reached[rows, :] * tail_steps[rows, :]
+        ) * slope[rows, 0:width]
+        padded[moved, width : width + STATE] = (maps[rows, 0:STATE] + in_grad[rows, :]) * slope[
+            rows, width : width + STATE
+        ]
+        padded[moved, width + STATE :] = maps[rows, STATE:] * slope[rows, width + STATE :]
     rim[...] = padded[length : length + HALO, :]
     rim.send()
-    back_raw = jnp.zeros((length + HALO, padded.shape[1]), F32)
-    for tap in range(taps):
-        back_raw = back_raw + conv_w[tap : tap + 1, :] * padded[pl.ds(HALO - tap, length + HALO), :]
-    back_raw_o[...] = back_raw[0:length]
-    full[...] = dot(hidden_t[...], back_raw[0:length].astype(BF16)) + dot(
-        edge[...], back_raw[length:].astype(BF16), 0, 0
-    )
-    halves(full, keep, send, place[0] % 2, blocks)
+    for at in range(0, length + HALO, CHUNK):
+        size = min(CHUNK, length + HALO - at)
+        part = conv_w[0:1, :] * padded[pl.ds(HALO + at, size), :]
+        for tap in range(1, taps):
+            part = part + conv_w[tap : tap + 1, :] * padded[pl.ds(HALO + at - tap, size), :]
+        if at < length:
+            back_raw_o[at : at + size, :] = part
+        back_raw_b[at : at + size, :] = part.astype(BF16)
+    back_raw_b[length + HALO :, :] = jnp.zeros((LANES - HALO, padded.shape[1]), BF16)
+    send[...] = dot(send_t[...], back_raw_b[...]).astype(BF16)
     send.send()
+    keep[...] = dot(keep_t[...], back_raw_b[...]).astype(BF16)
     back_raw_o.send()
-    back_conv = padded[middle, :]
     raw[...] = raw_b[...].astype(F32)
     spare = late.shape[0] - taps
+    conv_sums = [jnp.zeros((1, padded.shape[1]), F32)] * taps
+    for at in range(0, length, CHUNK):
+        back_conv = padded[HALO + at : HALO + at + CHUNK, :]
+        for tap in range(taps):
+            conv_sums[tap] = conv_sums[tap] + jnp.sum(
+                back_conv * raw[pl.ds(at + tap, CHUNK), :], axis=0, keepdims=True
+            )
     for tap in range(taps):
-        late[spare + tap : spare + tap + 1, :] = jnp.sum(
-            back_conv * raw[pl.ds(tap, length), :], axis=0, keepdims=True
-        )
-    late[0:HEADS, 0:width] = dot(step_grad_b, hidden_t[...], 0, 1)[0:HEADS]
+        late[spare + tap : spare + tap + 1, :] = conv_sums[tap]
+    late[0:HEADS, 0:width] = dot(step_grad_b, hidden[...], 0, 0)[0:HEADS]
     late[0:HEADS, width:] = jnp.zeros((HEADS, late.shape[1] - width), F32)
     log_decay = -step[:, 0:LANES] * rate
     facts = jnp.sum(step_grad, axis=0, keepdims=True)
@@ -705,19 +721,23 @@
         scratch=[pltpu.VMEM((length + HALO, channels), F32)], fetch=(2, 3, 4, 6), leave=(0, 2),
     )
     arrived = swapped(message).reshape(devices, slice_rows, width + LANES)
-    local, slope, tail_values, tail_steps, tail_weighted, hidden_t = call(
-        local_kernel,
+    local, slope, tail_values, tail_steps, tail_weighted, keep_t, send_t = call(
+        functools.partial(local_kernel, devices),
         [
             ((length, width), F32),
             ((length, channels), F32),
             ((length, width), F32),
             ((length, width), F32),
             ((length, width), BF16),
-            ((hidden_in.shape[1], length), BF16),
-        ],
-        mixed, step, run, run_t, skip_row, raw, conv_w, hidden_in,
-        scratch=[pltpu.VMEM((length + HALO, channels), F32)],
-        fetch=(4, 5, 6, 7), leave=(1, 2, 3, 4, 5),
+            ((width // 2, length + LANES), BF16),
+            ((width // 2, length + LANES), BF16),
+        ],
+        place, mixed, step, run, run_t, edge, skip_row, raw, conv_w, hidden_in,
+        scratch=[
+            pltpu.VMEM((length + HALO, channels), F32),
+            pltpu.VMEM((width, length + LANES), F32),
+        ],
+        scalars=1, fetch=(6, 7, 8, 9), leave=(1, 2, 3, 4, 5, 6),
     )
     onward, decay = call(
         states_kernel,
@@ -778,15 +798,15 @@
             ((length, LANES), BF16),
             ((HEADS + conv_w.shape[0], channels), F32),
         ],
-        place, state_grad, edge, run, mixed, step, state, run_grad,
+        place, state_grad, run, mixed, step, state, run_grad,
         tail_values, tail_weighted, step_local, a_log_row, conv_w, tail_steps, values_local, maps, slope,
-        hidden_t, raw, small, own,
+        send_t, keep_t, hidden_in, raw, small, own,
         scratch=[
-            pltpu.VMEM((width, channels), F32),
             pltpu.VMEM((length + 2 * HALO, channels), F32),
             pltpu.VMEM((length + HALO, channels), F32),
-        ],
-        scalars=1, fetch=(8, 9, 10, 11, 12, 13, 15, 16, 17, 18, 19, 20), leave=(1, 2, 3, 4),
+            pltpu.VMEM((length + LANES, channels), BF16),
+        ],
+        scalars=1, fetch=(7, 8, 9, 10, 11, 12, 14, 15, 16, 17, 18, 19, 20, 21), leave=(1, 2, 3, 4),
     )
     chips = devices // 2
     (both_in,) = call(

time: 116 us -> 115 us (level)
  blocking collectives: 0 us -> 13 us
  waiting for transfers between devices: 45.8 us -> 37 us
  starting transfers between devices: 26.4 us -> 22.8 us
    all_to_all x0 -> x1, blocking collectives: none -> 13 us  [swapped(): return lax.all_to_all(x, axis, split_axis=0, concat_axis=0, tiled=True)]
    all_to_all x4 -> x3, waiting for transfers between devices: 23 us -> 14.2 us  [swapped(): return lax.all_to_all(x, axis, split_axis=0, concat_axis=0, tiled=True)]
    all_to_all x4 -> x3, starting transfers between devices: 19 us -> 15.4 us  [swapped(): return lax.all_to_all(x, axis, split_axis=0, concat_axis=0, tiled=True)]
  transfers between devices with their start and end apart: 9 -> 8, of which waited for: 8 -> 7; matrix products, arithmetic and copies ran while one was open for 0% -> 0% of each run, Pallas kernels for 17% -> 17%
where the time goes in v6:
time: 115 us; the launch traced here: 113 us
  Pallas kernels  38.8 us (34%)
  waiting for transfers between devices  37 us (32%)
  starting transfers between devices  22.8 us (20%)
  blocking collectives  13 us (11%)
    pallas_call x12, Pallas kernels, call(): pl.pallas_call(kernel, out_shape=[(far if i in leave else close)(*out) fo...  38.8 us
    all_to_all x1, waiting for transfers between devices, exchanged(): lax.all_to_all(both, 'seq', split_axis=0, concat_axis=0, axis_index_group...  19.9 us
    all_to_all x3, starting transfers between devices, swapped(): return lax.all_to_all(x, axis, split_axis=0, concat_axis=0, tiled=True)  15.4 us
    all_to_all x3, waiting for transfers between devices, swapped(): return lax.all_to_all(x, axis, split_axis=0, concat_axis=0, tiled=True)  14.2 us
    all_to_all x1, blocking collectives, swapped(): return lax.all_to_all(x, axis, split_axis=0, concat_axis=0, tiled=True)  13 us
    all_to_all x1, starting transfers between devices, exchanged(): lax.all_to_all(both, 'seq', split_axis=0, concat_axis=0, axis_index_group...  3.57 us
    ppermute x2, starting transfers between devices, passed_along(): return lax.ppermute(x, axis, pairs)  3.32 us
  transfers between devices with their start and end apart: 8, of which 7 were waited for; matrix products, arithmetic and copies ran while one was open for 0% of the time, Pallas kernels for 17%

profile of v6, /device:TPU:0, one launch (start us, length us, event | category | flops | bytes accessed | tf_op | source)
XLA Modules:
  0.0 113.4 jit_solution(15821597652225082285)
XLA Ops:
  1.4 1.3 %collective-permute-start = (bf16[8,768]{1,0:T(8,128)(2,1)S(1)}, bf16[8,768]{1,0:T(8,128)(2,1)S(1)}, u32[]{:S(2)}, u32[]{:S(2)}) collective-permute-start(bf16[8,768]{1,0:T(8,128)(2,1)S(1)} %slice.3), channel_id=1, source_target_pairs={{1,0},{2,1},{3,2},{4,3},{5,4},{6,5},{7,6},{8,7},{9,8},{10,9},{11,1... | collective-permute-start | bytes 36872 | tf_op jit(solution)/shard_map/ppermute | solution.py:33
  2.6 2.9 %shard_map.214 = (bf16[128,128]{1,0:T(8,128)(2,1)S(1)}, f32[1,128]{1,0:T(1,128)}, bf16[256,768]{1,0:T(8,128)(2,1)S(1)}, bf16[768,1024]{1,0:T(8,128)(2,1)S(1)}) custom-call(bf16[128,4096]{1,0:T(8,128)(2,1)} %refs_0_.1, bf16[16,4096]{1,0:T(8,128)(2,1)} %bitcast.27, s32[1,128]{1,0:T(1,128)} %bitcast.34, s32[1,128]{1,0:T(1,128)} %bitcast.35, s32[1,128]{1,0:T(1,128)} %bitcast.36, ...), custom_call_target="tpu_custom_call" | custom-call | tf_op jit(solution)/shard_map/pallas_call | solution.py:176
  5.5 4.2 %shard_map.215 = (bf16[128,896]{1,0:T(8,128)(2,1)}, bf16[256,1024]{1,0:T(8,128)(2,1)S(1)}, bf16[264,1024]{1,0:T(8,128)(2,1)}, f32[256,256]{1,0:T(8,128)S(1)}, f3...) custom-call(bf16[8,768]{1,0:T(8,128)(2,1)S(1)} %collective-permute-done.refs_0_.refs_5_, ...), custom_call_target="tpu_custom_call" | custom-call | tf_op jit(solution)/shard_map/pallas_call | solution.py:176
  9.7 8.1 %all-to-all-start = ((bf16[16,8,896]{2,1,0:T(8,128)(2,1)}), bf16[16,8,896]{2,1,0:T(8,128)(2,1)S(1)}, u32[]{:S(2)}, u32[]{:S(2)}) async-start(bf16[16,8,896]{2,1,0:T(8,128)(2,1)} %bitcast.25), calls=%async_computation | async-start | bytes 458752 | tf_op jit(solution)/shard_map/all_to_all | solution.py:621
  17.9 5.5 %shard_map.216 = (f32[256,768]{1,0:T(8,128)S(1)}, f32[256,1024]{1,0:T(8,128)}, f32[256,768]{1,0:T(8,128)}, f32[256,768]{1,0:T(8,128)}, bf16[256,768]{1,0:T(8,128...) custom-call(s32[1]{0:T(128)} %bitcast.refs_0_, ...), custom_call_target="tpu_custom_call" | custom-call | tf_op jit(solution)/shard_map/pallas_call | solution.py:176
  23.3 4.0 %all-to-all-done.refs_0_ = bf16[16,8,896]{2,1,0:T(8,128)(2,1)S(1)} async-done(((bf16[16,8,896]{2,1,0:T(8,128)(2,1)}), bf16[16,8,896]{2,1,0:T(8,128)(2,1)S(1)}, u32[]{:S(2)}, u32[]{:S(2)}) %all-to-all-start) | async-done | bytes 229408 | tf_op jit(solution)/shard_map/all_to_all | solution.py:621
  27.4 1.5 %shard_map.217 = (bf16[16,8,768]{2,1,0:T(8,128)(2,1)}, f32[16,8,128]{2,1,0:T(8,128)S(1)}) custom-call(bf16[16,8,896]{2,1,0:T(8,128)(2,1)S(1)} %all-to-all-done.refs_0_, f32[256,768]{1,0:T(8,128)S(1)} %get-tuple-element.65.refs_1_.refs_3_), custom_call_target="tpu_custom_call" | custom-call | tf_op jit(solution)/shard_map/pallas_call | solution.py:176
  28.9 3.5 %all-to-all-start.1 = ((bf16[16,8,768]{2,1,0:T(8,128)(2,1)}), bf16[16,8,768]{2,1,0:T(8,128)(2,1)S(1)}, u32[]{:S(2)}, u32[]{:S(2)}) async-start(bf16[16,8,768]{2,1,0:T(8,128)(2,1)} %get-tuple-element.66), calls=%async_computation.1 | async-start | bytes 393216 | tf_op jit(solution)/shard_map/all_to_all | solution.py:621
  32.4 2.0 %shard_map.218 = (f32[256,128]{1,0:T(8,128)}, bf16[128,768]{1,0:T(8,128)(2,1)S(1)}, bf16[128,768]{1,0:T(8,128)(2,1)S(1)}) custom-call(bf16[16,8,896]{2,1,0:T(8,128)(2,1)S(1)} %all-to-all-done.refs_0_, bf16[16,768]{1,0:T(8,128)(2,1)} %bitcast.22, bf16[768,768]{1,0:T(8,128)(2,1)} %refs_2_.5), custom_call_target="tpu_custom_call" | custom-call | tf_op jit(solution)/shard_map/pallas_call | solution.py:176
  34.4 7.0 %all-to-all-done.1 = bf16[16,8,768]{2,1,0:T(8,128)(2,1)S(1)} async-done(((bf16[16,8,768]{2,1,0:T(8,128)(2,1)}), bf16[16,8,768]{2,1,0:T(8,128)(2,1)S(1)}, u32[]{:S(2)}, u32[]{:S(2)}) %all-to-all-start.1) | async-done | bytes 196640 | tf_op jit(solution)/shard_map/all_to_all | solution.py:621
  41.4 4.0 %shard_map.219 = (bf16[128,768]{1,0:T(8,128)(2,1)}, f32[256,768]{1,0:T(8,128)S(1)}, bf16[256,768]{1,0:T(8,128)(2,1)}, f32[256,128]{1,0:T(8,128)}, f32[256,128]{1,0:T(8,128)S(1)}, /*index=5*/f32[8,768]{1,0:T(8,128)}) custom-call(bf16[128,768]{1,0:T(8,128)(2,1)S(1)} %bitcast.18, bf16[256,1024]{1,0:T(8,128)(2,1)S(1)} %get-tuple-element.60.refs_1_.refs_0_.refs_3_, ...), custom_call_target="tpu_custom_call" | custom-call | tf_op jit(solution)/shard_map/pallas_call | solution.py:176
  45.4 3.7 %all-to-all-start.2 = ((bf16[16,8,768]{2,1,0:T(8,128)(2,1)}), bf16[16,8,768]{2,1,0:T(8,128)(2,1)S(1)}, u32[]{:S(2)}, u32[]{:S(2)}) async-start(bf16[16,8,768]{2,1,0:T(8,128)(2,1)} %bitcast.26), calls=%async_computation.2 | async-start | bytes 393216 | tf_op jit(solution)/shard_map/all_to_all | solution.py:621
  49.2 5.6 %shard_map.220 = (f32[256,768]{1,0:T(8,128)S(1)}, f32[256,256]{1,0:T(8,128)}, f32[256,128]{1,0:T(8,128)S(1)}, f32[256,128]{1,0:T(8,128)}, f32[128,128]{1,0:T(8,128)S(1)}) custom-call(bf16[256,1024]{1,0:T(8,128)(2,1)S(1)} %get-tuple-element.60.refs_1_.refs_0_.refs_3_, f32[256,256]{1,0:T(8,128)S(1)} %get-tuple-element.61.refs_2_.refs_1_.refs_4_, ...), custom_call_target="tpu_custom_call" | custom-call | tf_op jit(solution)/shard_map/pallas_call | solution.py:176
  54.7 3.2 %all-to-all-done.2.refs_0_ = bf16[16,8,768]{2,1,0:T(8,128)(2,1)S(1)} async-done(((bf16[16,8,768]{2,1,0:T(8,128)(2,1)}), bf16[16,8,768]{2,1,0:T(8,128)(2,1)S(1)}, u32[]{:S(2)}, u32[]{:S(2)}) %all-to-all-start.2) | async-done | bytes 196640 | tf_op jit(solution)/shard_map/all_to_all | solution.py:621
  57.9 1.1 shard_map.221
  59.0 13.0 %all_to_all.43 = bf16[16,8,896]{2,1,0:T(8,128)(2,1)S(1)} all-to-all(bf16[16,8,896]{2,1,0:T(8,128)(2,1)} %shard_map.221), channel_id=1, replica_groups=mesh['grp'=2,'seq'=16] {'seq'}, dimensions={0} | all-to-all | bytes 458752 | tf_op jit(solution)/shard_map/all_to_all | solution.py:621
  72.0 6.2 %shard_map.222 = (bf16[384,1024]{1,0:T(8,128)(2,1)S(1)}, bf16[384,1024]{1,0:T(8,128)(2,1)}, f32[8,1024]{1,0:T(8,128)}, f32[256,1024]{1,0:T(8,128)}, bf16[256,128]{1,0:T(8,128)(2,1)}, /*index=5*/f32[16,1024]{1,0:T(8,128)S(1)}) custom-call(s32[1]{0:T(128)} %bitcast.refs_0_, bf16[128,896]{1,0:T(8,128)(2,1)S(1)} %bitcast.21, ...), custom_call_target="tpu_custom_call" | custom-call | tf_op jit(solution)/shard_map/pallas_call | solution.py:176
  78.8 1.6 %collective-permute-done.3.refs_3_ = f32[16,1024]{1,0:T(8,128)S(1)} collective-permute-done((f32[16,1024]{1,0:T(8,128)S(1)}, f32[16,1024]{1,0:T(8,128)S(1)}, u32[]{:S(2)}, u32[]{:S(2)}) %collective-permute-start.3) | collective-permute-done | bytes 65568 | tf_op jit(solution)/shard_map/ppermute | solution.py:27
  80.8 1.2 %shard_map.224 = bf16[512,1024]{1,0:T(8,128)(2,1)} custom-call(bf16[384,1024]{1,0:T(8,128)(2,1)S(1)} %get-tuple-element.92.refs_0_, bf16[384,1024]{1,0:T(8,128)(2,1)S(1)} %collective-permute-done.2.refs_1_, f32[16,1024]{1,0:T(8,128)S(1)} %get-tuple-element.94.refs_2_, f32[16,1024]{1,0:T(8,128)S(1)} %collective-permute-done.3.refs_3_), custom_call_target="tpu_custom_call" | custom-call | tf_op jit(solution)/shard_map/pallas_call | solution.py:176
  82.1 3.6 %all-to-all-start.4 = ((bf16[8,64,1024]{2,1,0:T(8,128)(2,1)}), bf16[8,64,1024]{2,1,0:T(8,128)(2,1)S(1)}, u32[]{:S(2)}, u32[]{:S(2)}) async-start(bf16[8,64,1024]{2,1,0:T(8,128)(2,1)} %bitcast.24), calls=%async_computation.4 | async-start | bytes 2097152 | tf_op jit(solution)/shard_map/all_to_all | solution.py:676
  85.7 2.0 %collective-permute-start.1 = (f32[8,1024]{1,0:T(8,128)S(1)}, f32[8,1024]{1,0:T(8,128)S(1)}, u32[]{:S(2)}, u32[]{:S(2)}) collective-permute-start(f32[8,1024]{1,0:T(8,128)S(1)} %copy-done.2), channel_id=1, source_target_pairs={{0,1},{1,2},{2,3},{3,4},{4,5},{5,6},{6,7},{7,8},{8,9},{9,10},{10,1... | collective-permute-start | bytes 98312 | tf_op jit(solution)/shard_map/ppermute | solution.py:33
  88.6 3.5 %shard_map.223 = bf16[256,768]{1,0:T(8,128)(2,1)} custom-call(f32[8,1024]{1,0:T(8,128)S(1)} %collective-permute-done.1.refs_0_, f32[256,1024]{1,0:T(8,128)} %get-tuple-element.90.refs_1_, f32[4,1024]{1,0:T(4,128)} %refs_2_.4, bf16[256,128]{1,0:T(8,128)(2,1)} %get-tuple-element.91.refs_3_, bf16[12,768]{1,0:T(8,128)(2,1)} %bitcast.29, bf16[768,1024]{1,0:T(8,128)(2,1)} %refs_5_.3), custom_call_target="tpu_custom_call" | custom-call | tf_op jit(solution)/shard_map/pallas_call | solution.py:176
  92.0 19.9 %all-to-all-done.4.refs_1_ = bf16[8,64,1024]{2,1,0:T(8,128)(2,1)S(1)} async-done(((bf16[8,64,1024]{2,1,0:T(8,128)(2,1)}), bf16[8,64,1024]{2,1,0:T(8,128)(2,1)S(1)}, u32[]{:S(2)}, u32[]{:S(2)}) %all-to-all-start.4) | async-done | bytes 1048608 | tf_op jit(solution)/shard_map/all_to_all | solution.py:676
  111.9 1.3 %shard_map.225 = (f32[48,1024]{1,0:T(8,128)}, f32[4,1024]{1,0:T(4,128)}, f32[12,768]{1,0:T(8,128)}, f32[3,12]{1,0:T(4,128)}, f32[768]{0:T(1024)}, /*index=5*/f32...) custom-call(s32[1]{0:T(128)} %bitcast.refs_0_, bf16[8,64,1024]{2,1,0:T(8,128)(2,1)S(1)} %all-to-all-done.4.refs_1_, ...), custom_call_target="tpu_custom_call" | custom-call | tf_op jit(solution)/shard_map/pallas_call | solution.py:176
  (12 shorter events, 2.6 us)
Async XLA Ops:
  1.4 4.2 %collective-permute-start = (bf16[8,768]{1,0:T(8,128)(2,1)S(1)}, bf16[8,768]{1,0:T(8,128)(2,1)S(1)}, u32[]{:S(2)}, u32[]{:S(2)}) collective-permute-start(bf16[8,768]{1,0:T(8,128)(2,1)S(1)} %slice.3), channel_id=1, source_target_pairs={{1,0},{2,1},{3,2},{4,3},{5,4},{6,5},{7,6},{8,7},{9,8},{10,9},{11,1... | collective-permute-start | bytes 36872 | tf_op jit(solution)/shard_map/ppermute | solution.py:33
  9.7 17.7 %all-to-all-start = ((bf16[16,8,896]{2,1,0:T(8,128)(2,1)}), bf16[16,8,896]{2,1,0:T(8,128)(2,1)S(1)}, u32[]{:S(2)}, u32[]{:S(2)}) async-start(bf16[16,8,896]{2,1,0:T(8,128)(2,1)} %bitcast.25), calls=%async_computation | async-start | bytes 458752 | tf_op jit(solution)/shard_map/all_to_all | solution.py:621
  28.9 12.5 %all-to-all-start.1 = ((bf16[16,8,768]{2,1,0:T(8,128)(2,1)}), bf16[16,8,768]{2,1,0:T(8,128)(2,1)S(1)}, u32[]{:S(2)}, u32[]{:S(2)}) async-start(bf16[16,8,768]{2,1,0:T(8,128)(2,1)} %get-tuple-element.66), calls=%async_computation.1 | async-start | bytes 393216 | tf_op jit(solution)/shard_map/all_to_all | solution.py:621
  45.4 12.5 %all-to-all-start.2 = ((bf16[16,8,768]{2,1,0:T(8,128)(2,1)}), bf16[16,8,768]{2,1,0:T(8,128)(2,1)S(1)}, u32[]{:S(2)}, u32[]{:S(2)}) async-start(bf16[16,8,768]{2,1,0:T(8,128)(2,1)} %bitcast.26), calls=%async_computation.2 | async-start | bytes 393216 | tf_op jit(solution)/shard_map/all_to_all | solution.py:621
  78.2 2.7 %collective-permute-start.2 = (bf16[384,1024]{1,0:T(8,128)(2,1)}, bf16[384,1024]{1,0:T(8,128)(2,1)S(1)}, u32[]{:S(2)}, u32[]{:S(2)}) collective-permute-start(bf16[384,1024]{1,0:T(8,128)(2,1)} %get-tuple-element.93), channel_id=1, source_target_pairs={{0,1},{1,0},{2,3},{3,2},{4,5},{5,4},{6,7},{7,6},{8,9},{9,8},{10,11... | collective-permute-start | bytes 2359304 | tf_op jit(solution)/shard_map/ppermute | solution.py:27
  78.3 2.1 %collective-permute-start.3 = (f32[16,1024]{1,0:T(8,128)S(1)}, f32[16,1024]{1,0:T(8,128)S(1)}, u32[]{:S(2)}, u32[]{:S(2)}) collective-permute-start(f32[16,1024]{1,0:T(8,128)S(1)} %get-tuple-element.94.refs_2_), channel_id=1, source_target_pairs={{0,1},{1,0},{2,3},{3,2},{4,5},{5,4},{6,7},{7,6},{8,9},{9,8},{10,11... | collective-permute-start | bytes 196616 | tf_op jit(solution)/shard_map/ppermute | solution.py:27
  82.1 3.6 %copy-start.2 = (f32[8,1024]{1,0:T(8,128)S(1)}, f32[8,1024]{1,0:T(8,128)}, u32[]{:S(2)}) copy-start(f32[8,1024]{1,0:T(8,128)} %get-tuple-element.89) | copy-start | bytes 98308
  82.1 29.8 %all-to-all-start.4 = ((bf16[8,64,1024]{2,1,0:T(8,128)(2,1)}), bf16[8,64,1024]{2,1,0:T(8,128)(2,1)S(1)}, u32[]{:S(2)}, u32[]{:S(2)}) async-start(bf16[8,64,1024]{2,1,0:T(8,128)(2,1)} %bitcast.24), calls=%async_computation.4 | async-start | bytes 2097152 | tf_op jit(solution)/shard_map/all_to_all | solution.py:676
  85.7 2.9 %collective-permute-start.1 = (f32[8,1024]{1,0:T(8,128)S(1)}, f32[8,1024]{1,0:T(8,128)S(1)}, u32[]{:S(2)}, u32[]{:S(2)}) collective-permute-start(f32[8,1024]{1,0:T(8,128)S(1)} %copy-done.2), channel_id=1, source_target_pairs={{0,1},{1,2},{2,3},{3,4},{4,5},{5,6},{6,7},{7,8},{8,9},{9,10},{10,1... | collective-permute-start | bytes 98312 | tf_op jit(solution)/shard_map/ppermute | solution.py:33
  88.5 23.4 %copy-start = (bf16[768,768]{1,0:T(8,128)(2,1)S(1)}, bf16[768,768]{1,0:T(8,128)(2,1)}, u32[]{:S(2)}) copy-start(bf16[768,768]{1,0:T(8,128)(2,1)} %refs_2_.5) | copy-start | bytes 3538948
  88.5 23.4 %copy-start.1 = (bf16[768,16]{0,1:T(8,128)(2,1)S(1)}, bf16[768,16]{0,1:T(8,128)(2,1)}, u32[]{:S(2)}) copy-start(bf16[768,16]{0,1:T(8,128)(2,1)} %param.24) | copy-start | bytes 73732
